TPU v7x, 32 devices: a whole 2x2x4 slice. The times are simulated.
32 devices in a mesh: seq: 2 (over y), row: 4 (over x, core), rep: 4 (over z).
Axes of the slice: x: 2, y: 2, z: 4, core: 2. Of those that a mesh axis runs over, the one named last changes fastest.
Arguments:
- block_input: bfloat16 [4, 2048, 2048], P('row', 'seq', 'rep'), may hold values from -6 to 6
- cotangent: bfloat16 [4, 2048, 2048], P('row', 'seq', 'rep'), may hold values from -6 to 6
- segment_ids: int32 [4, 2048], P('row', 'seq'), may hold values from 0 to 3, never falling along the last dimension, each value on 1 to 1024 neighbouring positions
- pad_mask: int32 [4, 2048], P('row', 'seq'), may hold values 0 or 1
- state_init: float32 [4, 2816], P('row', 'rep'), may hold values from -6 to 6
- window_init: bfloat16 [4, 3, 2816], P('row', None, 'rep'), may hold values from -6 to 6
- recur_input: bfloat16 [2048, 2816], P(('seq', 'row'), 'rep'), may hold values from -0.125 to 0.125
- recur_gate: bfloat16 [2048, 2816], P(('seq', 'row'), 'rep'), may hold values from -0.125 to 0.125
- recur_output: bfloat16 [2048, 2816], P(('seq', 'row'), 'rep'), may hold values from -0.3125 to 0.3125
- feed_gate: bfloat16 [2048, 6144], P(('seq', 'row'), 'rep'), may hold values from -0.125 to 0.125
- feed_up: bfloat16 [2048, 6144], P(('seq', 'row'), 'rep'), may hold values from -0.125 to 0.125
- feed_down: bfloat16 [2048, 6144], P(('seq', 'row'), 'rep'), may hold values from -0.15625 to 0.15625
- conv_kernel: float32 [4, 2816], P(None, 'rep'), may hold values from -3 to 3
- conv_bias: float32 [2816], P('rep'), may hold values from -3 to 3
- decay_gate: bfloat16 [16, 176, 176], P('rep'), may hold values from -0.4375 to 0.4375
- input_gate: bfloat16 [16, 176, 176], P('rep'), may hold values from -0.4375 to 0.4375
- decay_bias: float32 [2816], P('rep'), may hold values from -4 to 4
- input_bias: float32 [2816], P('rep'), may hold values from -4 to 4
- decay_logit: float32 [2816], P('rep'), may hold values from -10.5 to -4.5
- mixer_gain: float32 [2048], replicated, may hold values from 0.25 to 1.75
- feed_gain: float32 [2048], replicated, may hold values from 0.25 to 1.75
Outputs:
- block_output: bfloat16 [4, 2048, 2048], P('row', 'seq', 'rep')
- block_states: float32 [4, 2, 2816], P('row', 'seq', 'rep')
- block_windows: bfloat16 [4, 2, 3, 2816], P('row', 'seq', None, 'rep')
- input_grad: bfloat16 [4, 2048, 2048], P('row', 'seq', 'rep')
- recur_input_grad: float32 [2048, 2816], P(('seq', 'row'), 'rep')
- recur_gate_grad: float32 [2048, 2816], P(('seq', 'row'), 'rep')
- recur_output_grad: float32 [2048, 2816], P(('seq', 'row'), 'rep')
- feed_gate_grad: float32 [2048, 6144], P(('seq', 'row'), 'rep')
- feed_up_grad: float32 [2048, 6144], P(('seq', 'row'), 'rep')
- feed_down_grad: float32 [2048, 6144], P(('seq', 'row'), 'rep')
- conv_kernel_grad: float32 [4, 2816], P(None, 'rep')
- conv_bias_grad: float32 [2816], P('rep')
- decay_gate_grad: float32 [16, 176, 176], P('rep')
- input_gate_grad: float32 [16, 176, 176], P('rep')
- decay_bias_grad: float32 [2816], P('rep')
- input_bias_grad: float32 [2816], P('rep')
- decay_logit_grad: float32 [2816], P('rep')
- mixer_gain_grad: float32 [2048], replicated
- feed_gain_grad: float32 [2048], replicated
Inputs may be any that keep to these rules, and one draw needn't show every extreme that they name: `segment_ids`: document numbers never fall along a row; each row holds 4 documents of at most 1024 positions.
All inputs are finite; a program needn't handle non-finite values. No bound on the sum of `pad_mask` on one device may be relied on, other than what follows from the above.
Results may differ from a plain program's by a relative error of at most 0.01.
Values may be sent and summed in bfloat16 or wider, within the bound.
A program may use at most 384 MiB of HBM per device.

v0:
```python
from functools import partial

import jax
import jax.numpy as jnp
from jax import lax
from jax.sharding import PartitionSpec as P

eps = 1e-06


def shifted_2(block, axis, distance):
    devices = range(lax.axis_size(axis))
    route = [(i - distance, i) for i in devices if i - distance in devices]
    return lax.ppermute(block, axis, route)


def entering(value, axis, join, neutral, backward):
    count, mine = (lax.axis_size(axis), lax.axis_index(axis))
    pieces = jax.tree.map(lambda part: lax.all_gather(part, axis), value)
    if backward:
        pieces = jax.tree.map(lambda part: part[::-1], pieces)
        mine = count - 1 - mine
    subtotal = jax.tree.map(
        lambda part, zero: jnp.full_like(part, 0) + jnp.asarray(zero, part.dtype), value, neutral
    )

    def hop(position, subtotal):
        longer = join(subtotal, jax.tree.map(lambda part: part[position], pieces))
        return jax.tree.map(lambda new, old: jnp.where(position < mine, new, old), longer, subtotal)

    return lax.fori_loop(0, count - 1, hop, subtotal)


def rms_norm(values, scales):
    return values * lax.rsqrt(jnp.mean(values * values, axis=-1, keepdims=True) + eps) * scales


def affine(former, latter):
    return (former[0] * latter[0], latter[0] * former[1] + latter[1])


def conv_math(padded, kernel, offset_bias, same_masks):
    tap_count = kernel.shape[0]
    length = padded.shape[1] - tap_count + 1
    total = offset_bias
    for offset in range(tap_count):
        start = tap_count - 1 - offset
        total = (
            total
            + kernel[offset] * padded[:, start : start + length] * same_masks[offset][..., None]
        )
    return total


def gate_math(conv_out, decay_pre, input_pre, decay_logit, retain_mask):
    rate_scale = 8.0 * jax.nn.softplus(decay_logit)
    exponent = rate_scale * jax.nn.sigmoid(decay_pre)
    retain = retain_mask[..., None] * jnp.exp(-exponent)
    inflow = jnp.sqrt(-jnp.expm1(-2.0 * exponent)) * jax.nn.sigmoid(input_pre) * conv_out
    return (retain, inflow)


def output_gate(hidden, gate_branch):
    return hidden * jax.nn.gelu(gate_branch, approximate=True)


def feed_math(gate_pre, up_pre):
    return jax.nn.gelu(gate_pre, approximate=True) * up_pre


def contract_last(left, right):
    return lax.dot_general(
        left, right, (((2,), (1,)), ((), ())), preferred_element_type=jnp.float32
    )


def outer_sum(left, right):
    return jnp.einsum("rtd,rtm->dm", left, right, preferred_element_type=jnp.float32)


def split_heads(values, head_count):
    return values.reshape(
        values.shape[0], values.shape[1], head_count, values.shape[2] // head_count
    )


def block_apply(values, blocks):
    row_count, length, channels = values.shape
    heads_in = split_heads(values, blocks.shape[0])
    mixed = jnp.einsum("rthi,hij->rthj", heads_in, blocks, preferred_element_type=jnp.float32)
    return mixed.reshape(row_count, length, channels)


def block_apply_back(grads, blocks):
    row_count, length, channels = grads.shape
    heads_in = split_heads(grads, blocks.shape[0])
    mixed = jnp.einsum("rthj,hij->rthi", heads_in, blocks, preferred_element_type=jnp.float32)
    return mixed.reshape(row_count, length, channels)


def block_outer(values, grads, head_count):
    return jnp.einsum(
        "rthi,rthj->hij",
        split_heads(values, head_count),
        split_heads(grads, head_count),
        preferred_element_type=jnp.float32,
    )


def shards(
    block_input,
    cotangent,
    segment_ids,
    pad_mask,
    state_init,
    window_init,
    recur_input,
    recur_gate,
    recur_output,
    feed_gate,
    feed_up,
    feed_down,
    conv_kernel,
    conv_bias,
    decay_gate,
    input_gate,
    decay_bias,
    input_bias,
    decay_logit,
    mixer_gain,
    feed_gain,
):
    own_width = block_input.shape[2]
    rep_index = lax.axis_index("rep")
    at_start = lax.axis_index("seq") == 0
    head_count = decay_gate.shape[0]
    tap_count = conv_kernel.shape[0]
    edge_width = tap_count - 1
    length = segment_ids.shape[1]
    masked_low = cotangent * pad_mask[..., None].astype(jnp.bfloat16)
    whole_input, whole_masked = (
        lax.all_gather(block_input, "rep", axis=2, tiled=True),
        lax.all_gather(masked_low, "rep", axis=2, tiled=True),
    )
    fetched = (
        lax.all_gather(recur_input, ("seq", "row"), axis=0, tiled=True),
        lax.all_gather(recur_gate, ("seq", "row"), axis=0, tiled=True),
        lax.all_gather(recur_output, ("seq", "row"), axis=0, tiled=True),
        lax.all_gather(feed_gate, ("seq", "row"), axis=0, tiled=True),
        lax.all_gather(feed_up, ("seq", "row"), axis=0, tiled=True),
        lax.all_gather(feed_down, ("seq", "row"), axis=0, tiled=True),
    )
    input_float = whole_input.astype(jnp.float32)
    normed_f, norm_one_back = jax.vjp(rms_norm, input_float, mixer_gain)
    normed = normed_f.astype(jnp.bfloat16)
    conv_input = jnp.dot(normed, fetched[0], preferred_element_type=jnp.float32).astype(
        jnp.bfloat16
    )
    gate_branch = jnp.dot(normed, fetched[1], preferred_element_type=jnp.float32)
    left_input, left_marks = shifted_2(
        (conv_input[:, -edge_width:], segment_ids[:, -edge_width:].astype(jnp.bfloat16)), "seq", 1
    )
    left_ids = left_marks.astype(jnp.int32)
    left_ids = jnp.where(at_start, jnp.broadcast_to(segment_ids[:, :1], left_ids.shape), left_ids)
    left_input = jnp.where(at_start, window_init, left_input)
    ids_ext = jnp.concatenate([left_ids, segment_ids], axis=1)
    same_masks = [
        (ids_ext[:, edge_width - offset : edge_width - offset + length] == segment_ids).astype(
            jnp.float32
        )
        for offset in range(tap_count)
    ]
    retain_mask = (ids_ext[:, edge_width - 1 : edge_width - 1 + length] == segment_ids).astype(
        jnp.float32
    )
    padded = jnp.concatenate([left_input, conv_input], axis=1).astype(jnp.float32)
    conv_out, conv_back = jax.vjp(
        partial(conv_math, same_masks=same_masks), padded, conv_kernel, conv_bias
    )
    conv_low = conv_out.astype(jnp.bfloat16)
    decay_pre = block_apply(conv_low, decay_gate) + decay_bias
    input_pre = block_apply(conv_low, input_gate) + input_bias
    (retain, inflow), gate_back = jax.vjp(
        partial(gate_math, retain_mask=retain_mask), conv_out, decay_pre, input_pre, decay_logit
    )
    products, partial_states = lax.associative_scan(affine, (retain, inflow), axis=1)
    carry_decay, carry_state = entering(
        (products[:, -1], partial_states[:, -1]),
        "seq",
        affine,
        (jnp.ones_like(state_init), jnp.zeros_like(state_init)),
        False,
    )
    state_in = carry_decay * state_init + carry_state
    hidden = partial_states + products * state_in[:, None]
    block_states = hidden[:, -1:]
    block_windows = conv_input[:, None, -edge_width:]
    gated_f, gated_back = jax.vjp(output_gate, hidden, gate_branch)
    gated = gated_f.astype(jnp.bfloat16)
    branch = lax.psum(contract_last(gated, fetched[2]), "rep")
    middle = input_float + branch
    normed_mid_f, norm_two_back = jax.vjp(rms_norm, middle, feed_gain)
    normed_mid = normed_mid_f.astype(jnp.bfloat16)
    gate_pre = jnp.dot(normed_mid, fetched[3], preferred_element_type=jnp.float32)
    up_pre = jnp.dot(normed_mid, fetched[4], preferred_element_type=jnp.float32)
    feed_f, feed_back = jax.vjp(feed_math, gate_pre, up_pre)
    feed_low = feed_f.astype(jnp.bfloat16)
    feed_out = lax.psum_scatter(
        contract_last(feed_low, fetched[5]), "rep", scatter_dimension=2, tiled=True
    )
    middle_own = lax.dynamic_slice_in_dim(middle, rep_index * own_width, own_width, 2)
    block_output = (middle_own + feed_out).astype(jnp.bfloat16)
    back_weights = (
        lax.all_gather(recur_input, ("seq", "row"), axis=0, tiled=True),
        lax.all_gather(recur_gate, ("seq", "row"), axis=0, tiled=True),
        lax.all_gather(recur_output, ("seq", "row"), axis=0, tiled=True),
        lax.all_gather(feed_gate, ("seq", "row"), axis=0, tiled=True),
        lax.all_gather(feed_up, ("seq", "row"), axis=0, tiled=True),
        lax.all_gather(feed_down, ("seq", "row"), axis=0, tiled=True),
    )
    grad_feed = jnp.dot(whole_masked, back_weights[5], preferred_element_type=jnp.float32)
    feed_down_grad = outer_sum(whole_masked, feed_low)
    gate_grad_f, up_grad_f = feed_back(grad_feed)
    gate_grad = gate_grad_f.astype(jnp.bfloat16)
    up_grad = up_grad_f.astype(jnp.bfloat16)
    feed_gate_grad = outer_sum(normed_mid, gate_grad)
    feed_up_grad = outer_sum(normed_mid, up_grad)
    mid_normed_grad = lax.psum(
        contract_last(gate_grad, back_weights[3]) + contract_last(up_grad, back_weights[4]), "rep"
    )
    middle_norm_grad, feed_gain_grad = norm_two_back(mid_normed_grad)
    middle_grad = whole_masked.astype(jnp.float32) + middle_norm_grad
    middle_low = middle_grad.astype(jnp.bfloat16)
    gated_grad = jnp.dot(middle_low, back_weights[2], preferred_element_type=jnp.float32)
    recur_output_grad = outer_sum(middle_low, gated)
    hidden_grad, branch_grad_f = gated_back(gated_grad)
    branch_grad = branch_grad_f.astype(jnp.bfloat16)
    shifted = jnp.concatenate([retain[:, 1:], jnp.ones_like(retain[:, :1])], axis=1)
    after_decay, local_adjoint = lax.associative_scan(
        affine, (shifted, hidden_grad), axis=1, reverse=True
    )
    carry_back = entering(
        (products[:, -1], retain[:, 0] * local_adjoint[:, 0]),
        "seq",
        affine,
        (jnp.ones_like(state_init), jnp.zeros_like(state_init)),
        True,
    )
    adjoint = local_adjoint + after_decay * carry_back[1][:, None]
    hidden_prev = jnp.concatenate([state_in[:, None], hidden[:, :-1]], axis=1)
    conv_direct, decay_pre_f, input_pre_f, decay_logit_grad = gate_back(
        (adjoint * hidden_prev, adjoint)
    )
    decay_pre_grad = decay_pre_f.astype(jnp.bfloat16)
    input_pre_grad = input_pre_f.astype(jnp.bfloat16)
    decay_gate_grad = block_outer(conv_low, decay_pre_grad, head_count)
    input_gate_grad = block_outer(conv_low, input_pre_grad, head_count)
    decay_bias_grad = jnp.sum(decay_pre_grad.astype(jnp.float32), axis=(0, 1))
    input_bias_grad = jnp.sum(input_pre_grad.astype(jnp.float32), axis=(0, 1))
    conv_grad = (
        conv_direct
        + block_apply_back(decay_pre_grad, decay_gate)
        + block_apply_back(input_pre_grad, input_gate)
    )
    padded_grad, conv_kernel_grad, conv_bias_grad = conv_back(conv_grad)
    from_right = shifted_2(padded_grad[:, :edge_width], "seq", -1)
    own_grad = padded_grad[:, edge_width:]
    own_grad = jnp.concatenate(
        [own_grad[:, :-edge_width], own_grad[:, -edge_width:] + from_right], axis=1
    )
    input_low_grad = own_grad.astype(jnp.bfloat16)
    recur_input_grad = outer_sum(normed, input_low_grad)
    recur_gate_grad = outer_sum(normed, branch_grad)
    normed_terms = contract_last(input_low_grad, back_weights[0]) + contract_last(
        branch_grad, back_weights[1]
    )
    middle_grad_own = lax.dynamic_slice_in_dim(middle_grad, rep_index * own_width, own_width, 2)
    normed_grad = lax.psum(normed_terms, "rep")
    input_norm_grad, mixer_gain_grad = norm_one_back(normed_grad)
    input_norm_own = lax.dynamic_slice_in_dim(input_norm_grad, rep_index * own_width, own_width, 2)
    input_grad = (middle_grad_own + input_norm_own).astype(jnp.bfloat16)
    matrix_grads = (
        lax.psum_scatter(recur_input_grad, ("seq", "row"), scatter_dimension=0, tiled=True),
        lax.psum_scatter(recur_gate_grad, ("seq", "row"), scatter_dimension=0, tiled=True),
        lax.psum_scatter(recur_output_grad, ("seq", "row"), scatter_dimension=0, tiled=True),
        lax.psum_scatter(feed_gate_grad, ("seq", "row"), scatter_dimension=0, tiled=True),
        lax.psum_scatter(feed_up_grad, ("seq", "row"), scatter_dimension=0, tiled=True),
        lax.psum_scatter(feed_down_grad, ("seq", "row"), scatter_dimension=0, tiled=True),
    )
    small_grads = lax.psum(
        (
            conv_kernel_grad,
            conv_bias_grad,
            decay_gate_grad,
            input_gate_grad,
            decay_bias_grad,
            input_bias_grad,
            decay_logit_grad,
            mixer_gain_grad,
            feed_gain_grad,
        ),
        ("seq", "row"),
    )
    return (
        block_output,
        block_states,
        block_windows,
        input_grad,
        matrix_grads[0],
        matrix_grads[1],
        matrix_grads[2],
        matrix_grads[3],
        matrix_grads[4],
        matrix_grads[5],
        small_grads[0],
        small_grads[1],
        small_grads[2],
        small_grads[3],
        small_grads[4],
        small_grads[5],
        small_grads[6],
        small_grads[7],
        small_grads[8],
    )


def solution(mesh):
    in_specs = (
        P("row", "seq", "rep"),
        P("row", "seq", "rep"),
        P("row", "seq"),
        P("row", "seq"),
        P("row", "rep"),
        P("row", None, "rep"),
        P(("seq", "row"), "rep"),
        P(("seq", "row"), "rep"),
        P(("seq", "row"), "rep"),
        P(("seq", "row"), "rep"),
        P(("seq", "row"), "rep"),
        P(("seq", "row"), "rep"),
        P(None, "rep"),
        P("rep"),
        P("rep", None, None),
        P("rep", None, None),
        P("rep"),
        P("rep"),
        P("rep"),
        P(),
        P(),
    )
    out_specs = (
        P("row", "seq", "rep"),
        P("row", "seq", "rep"),
        P("row", "seq", None, "rep"),
        P("row", "seq", "rep"),
        P(("seq", "row"), "rep"),
        P(("seq", "row"), "rep"),
        P(("seq", "row"), "rep"),
        P(("seq", "row"), "rep"),
        P(("seq", "row"), "rep"),
        P(("seq", "row"), "rep"),
        P(None, "rep"),
        P("rep"),
        P("rep", None, None),
        P("rep", None, None),
        P("rep"),
        P("rep"),
        P("rep"),
        P(),
        P(),
    )
    return jax.shard_map(shards, mesh=mesh, in_specs=in_specs, out_specs=out_specs, check_vma=False)
```

profile of v0, /device:TPU:0, one launch (start us, length us, event | category | flops | bytes accessed | tf_op | source)
XLA Modules:
  0.0 4679.4 jit_solution(15603391600166171410)
XLA Ops:
  20.5 72.6 %all-gather.9.cloned.1.call-done = bf16[1,1024,2048]{2,1,0:T(8,128)(2,1)} async-done(((bf16[1,1024,512]{2,1,0:T(8,128)(2,1)}), bf16[1,1024,2048]{2,1,0:T(8,128)(2,1)}) %all-gather.9.cloned.1.call-update) | async-done | bytes 4194320 | tf_op jit(solution)/shard_map/all_gather | solution.py:142
  181.9 50.8 %slice.699 = f32[1,512,704]{1,2,0:T(8,128)} slice(f32[1,1024,704]{1,2,0:T(8,128)S(1)} %get-tuple-element.180), slice={[0:1:1], [1:1024:2], [0:704:1]} | slice | bytes 2883584 | tf_op jit(solution)/shard_map/slice | solution.py:186
  232.7 50.7 %slice.703 = f32[1,512,704]{1,2,0:T(8,128)} slice(f32[1,1024,704]{1,2,0:T(8,128)S(1)} %get-tuple-element.180), slice={[0:1:1], [0:1023:2], [0:704:1]} | slice | bytes 2883584 | tf_op jit(solution)/shard_map/slice | solution.py:186
  283.5 51.4 %slice.700 = f32[1,512,704]{1,2,0:T(8,128)} slice(f32[1,1024,704]{1,2,0:T(8,128)} %get-tuple-element.181), slice={[0:1:1], [0:1023:2], [0:704:1]} | slice | bytes 2883584 | tf_op jit(solution)/shard_map/slice | solution.py:186
  334.9 51.3 %slice.701 = f32[1,512,704]{1,2,0:T(8,128)} slice(f32[1,1024,704]{1,2,0:T(8,128)} %get-tuple-element.181), slice={[0:1:1], [1:1024:2], [0:704:1]} | slice | bytes 2883584 | tf_op jit(solution)/shard_map/slice | solution.py:186
  856.0 50.7 %slice.698 = f32[1,511,704]{1,2,0:T(8,128)} slice(f32[1,1024,704]{1,2,0:T(8,128)S(1)} %get-tuple-element.180), slice={[0:1:1], [2:1024:2], [0:704:1]} | slice | bytes 2877952 | tf_op jit(solution)/shard_map/slice | solution.py:186
  906.7 51.2 %slice.771 = f32[1,511,704]{1,2,0:T(8,128)} slice(f32[1,1024,704]{1,2,0:T(8,128)} %get-tuple-element.181), slice={[0:1:1], [2:1024:2], [0:704:1]} | slice | bytes 2877952 | tf_op jit(solution)/shard_map/slice | solution.py:186
  1326.9 57.3 %pad.308 = f32[1,1024,704]{1,2,0:T(8,128)} pad(f32[1,512,704]{1,2,0:T(8,128)} %pad_maximum_fusion.1, f32[]{:T(128)} %constant.20.clone.1), padding=0_0_0x0_1_1x0_0_0 | pad | bytes 4325380 | tf_op jit(solution)/shard_map/pad | solution.py:186
  1384.2 57.2 %pad.309 = f32[1,1024,704]{1,2,0:T(8,128)} pad(f32[1,512,704]{1,2,0:T(8,128)} %add.770, f32[]{:T(128)} %constant.20.clone.1), padding=0_0_0x1_0_1x0_0_0 | pad | bytes 4325380 | tf_op jit(solution)/shard_map/pad | solution.py:186
  1447.5 57.1 %pad.288 = f32[1,1024,704]{1,2,0:T(8,128)} pad(f32[1,512,704]{1,2,0:T(8,128)} %pad_maximum_fusion, f32[]{:T(128)} %constant.20.clone.1), padding=0_0_0x0_1_1x0_0_0 | pad | bytes 4325380 | tf_op jit(solution)/shard_map/pad | solution.py:186
  1504.6 57.3 %pad.289 = f32[1,1024,704]{1,2,0:T(8,128)} pad(f32[1,512,704]{1,2,0:T(8,128)} %add.759, f32[]{:T(128)} %constant.20.clone.1), padding=0_0_0x1_0_1x0_0_0 | pad | bytes 4325380 | tf_op jit(solution)/shard_map/pad | solution.py:186
  1595.3 286.3 %all-reduce.97.cloned.1.call-done = f32[1,1024,2048]{2,1,0:T(8,128)} async-done(((f32[1,1024,2048]{2,1,0:T(8,128)}), f32[1,1024,2048]{2,1,0:T(8,128)}) %all-reduce.97.cloned.1.call-update) | async-done | bytes 8388624 | tf_op jit(solution)/shard_map/psum | solution.py:200
  1987.1 71.2 %all-gather.23.cloned.1.call-done = bf16[1,1024,2048]{2,1,0:T(8,128)(2,1)} async-done(((bf16[1,1024,512]{2,1,0:T(8,128)(2,1)}), bf16[1,1024,2048]{2,1,0:T(8,128)(2,1)}) %all-gather.23.cloned.1.call-update) | async-done | bytes 4194320 | tf_op jit(solution)/shard_map/all_gather | solution.py:143
  2058.3 46.0 all-gather.21.cloned.1.call-done
  2146.4 51.2 %slice.798 = f32[1,512,704]{1,2,0:T(8,128)} slice(f32[1,1024,704]{1,2,0:T(8,128)} %concatenate.160), slice={[0:1:1], [0:1023:2], [0:704:1]} | slice | bytes 2883584 | tf_op jit(solution)/shard_map/slice | solution.py:239
  2197.7 51.3 %slice.805 = f32[1,512,704]{1,2,0:T(8,128)} slice(f32[1,1024,704]{1,2,0:T(8,128)} %concatenate.160), slice={[0:1:1], [1:1024:2], [0:704:1]} | slice | bytes 2883584 | tf_op jit(solution)/shard_map/slice | solution.py:239
  2249.0 51.3 %slice.796 = f32[1,511,704]{1,2,0:T(8,128)} slice(f32[1,1024,704]{1,2,0:T(8,128)} %concatenate.160), slice={[0:1:1], [1:1022:2], [0:704:1]} | slice | bytes 2877952 | tf_op jit(solution)/shard_map/slice | solution.py:239
  2352.8 81.8 %all-reduce.99.cloned.1.call-done = f32[1,1024,2048]{2,1,0:T(8,128)} async-done(((f32[1,1024,2048]{2,1,0:T(8,128)}), f32[1,1024,2048]{2,1,0:T(8,128)}) %all-reduce.99.cloned.1.call-update) | async-done | bytes 8388624 | tf_op jit(solution)/shard_map/psum | solution.py:228
  2462.4 51.3 %slice.800 = f32[1,512,704]{1,2,0:T(8,128)} slice(f32[1,1024,704]{1,2,0:T(8,128)} %multiply_bitcast_fusion), slice={[0:1:1], [1:1024:2], [0:704:1]} | slice | bytes 2883584 | tf_op jit(solution)/shard_map/slice | solution.py:239
  2513.7 51.4 %slice.802 = f32[1,512,704]{1,2,0:T(8,128)} slice(f32[1,1024,704]{1,2,0:T(8,128)} %multiply_bitcast_fusion), slice={[0:1:1], [0:1023:2], [0:704:1]} | slice | bytes 2883584 | tf_op jit(solution)/shard_map/slice | solution.py:239
  3057.2 51.3 %slice.874 = f32[1,511,704]{1,2,0:T(8,128)} slice(f32[1,1024,704]{1,2,0:T(8,128)} %multiply_bitcast_fusion), slice={[0:1:1], [1:1022:2], [0:704:1]} | slice | bytes 2877952 | tf_op jit(solution)/shard_map/slice | solution.py:239
  3415.7 57.2 %pad.329 = f32[1,1024,704]{1,2,0:T(8,128)} pad(f32[1,512,704]{1,2,0:T(8,128)} %add.812, f32[]{:T(128)} %constant.20.clone.1), padding=0_0_0x1_0_1x0_0_0 | pad | bytes 4325380 | tf_op jit(solution)/shard_map/pad | solution.py:239
  3554.7 57.2 %pad.328 = f32[1,1024,704]{1,2,0:T(8,128)} pad(f32[1,512,704]{1,2,0:T(8,128)} %pad_maximum_fusion.2, f32[]{:T(128)} %constant.20.clone.1), padding=0_0_0x0_1_1x0_0_0 | pad | bytes 4325380 | tf_op jit(solution)/shard_map/pad | solution.py:239
  3620.2 52.7 %pad.349 = f32[1,1024,704]{1,2,0:T(8,128)S(1)} pad(f32[1,512,704]{1,2,0:T(8,128)} %add.823, f32[]{:T(128)} %constant.20.clone.1), padding=0_0_0x1_0_1x0_0_0 | pad | bytes 4325380 | tf_op jit(solution)/shard_map/pad | solution.py:239
  3676.0 57.2 %pad.348 = f32[1,1024,704]{1,2,0:T(8,128)} pad(f32[1,512,704]{1,2,0:T(8,128)} %concatenate.178, f32[]{:T(128)} %constant.20.clone.1), padding=0_0_0x0_1_1x0_0_0 | pad | bytes 4325380 | tf_op jit(solution)/shard_map/pad | solution.py:239
  3924.4 204.8 %all-reduce.101.cloned.1.call-done = f32[1,1024,2048]{2,1,0:T(8,128)} async-done(((f32[1,1024,2048]{2,1,0:T(8,128)}), f32[1,1024,2048]{2,1,0:T(8,128)}) %all-reduce.101.cloned.1.call-update) | async-done | bytes 8388624 | tf_op jit(solution)/shard_map/psum | solution.py:278
  4190.7 62.5 %reduce-scatter.14.cloned.1.call-done = f32[256,704]{0,1:T(8,128)} async-done(((f32[2048,704]{0,1:T(8,128)}), f32[256,704]{0,1:T(8,128)}) %reduce-scatter.14.cloned.1.call-update) | async-done | bytes 720912 | tf_op jit(solution)/shard_map/reduce_scatter | solution.py:285
  4253.2 62.9 %reduce-scatter.12.cloned.1.call-done = f32[256,704]{0,1:T(8,128)} async-done(((f32[2048,704]{0,1:T(8,128)}), f32[256,704]{0,1:T(8,128)}) %reduce-scatter.12.cloned.1.call-update) | async-done | bytes 720912 | tf_op jit(solution)/shard_map/reduce_scatter | solution.py:284
  4316.2 63.3 %reduce-scatter.10.cloned.1.call-done = f32[256,704]{0,1:T(8,128)} async-done(((f32[2048,704]{0,1:T(8,128)}), f32[256,704]{0,1:T(8,128)}) %reduce-scatter.10.cloned.1.call-update) | async-done | bytes 720912 | tf_op jit(solution)/shard_map/reduce_scatter | solution.py:283
  4379.5 96.3 %reduce-scatter.16.cloned.1.call-done = f32[256,1536]{1,0:T(8,128)} async-done(((f32[2048,1536]{1,0:T(8,128)}), f32[256,1536]{1,0:T(8,128)}) %reduce-scatter.16.cloned.1.call-update) | async-done | bytes 1572880 | tf_op jit(solution)/shard_map/reduce_scatter | solution.py:286
  4475.8 96.4 %reduce-scatter.18.cloned.1.call-done = f32[256,1536]{1,0:T(8,128)} async-done(((f32[2048,1536]{1,0:T(8,128)}), f32[256,1536]{1,0:T(8,128)}) %reduce-scatter.18.cloned.1.call-update) | async-done | bytes 1572880 | tf_op jit(solution)/shard_map/reduce_scatter | solution.py:287
  4572.2 96.5 %reduce-scatter.20.cloned.1.call-done = f32[256,1536]{1,0:T(8,128)} async-done(((f32[2048,1536]{1,0:T(8,128)}), f32[256,1536]{1,0:T(8,128)}) %reduce-scatter.20.cloned.1.call-update) | async-done | bytes 1572880 | tf_op jit(solution)/shard_map/reduce_scatter | solution.py:288
  (674 shorter events, 2355.8 us)
Async XLA Ops:
  7.2 167.8 %copy-start = (bf16[4,176,176]{2,1,0:T(8,128)(2,1)S(1)}, bf16[4,176,176]{2,1,0:T(8,128)(2,1)}, u32[]{:S(2)}) copy-start(bf16[4,176,176]{2,1,0:T(8,128)(2,1)} %param.36) | copy-start | bytes 743428
  7.2 85.9 %all-gather.9.cloned.1.call-start = ((), (), s32[]{:S(2)}) async-start(), calls=%async_computation.7 | async-start | bytes 5242880 | tf_op jit(solution)/shard_map/all_gather | solution.py:142
  8.0 117.3 %all-gather.11.cloned.1.call-start = ((), (), s32[]{:S(2)}) async-start(), calls=%async_computation.8 | async-start | bytes 3244032 | tf_op jit(solution)/shard_map/all_gather | solution.py:146
  8.7 153.6 %all-gather.13.cloned.1.call-start = ((), (), s32[]{:S(2)}) async-start(), calls=%async_computation.9 | async-start | bytes 3244032 | tf_op jit(solution)/shard_map/all_gather | solution.py:147
  9.4 1572.1 %all-gather.15.cloned.1.call-start = ((), (), s32[]{:S(2)}) async-start(), calls=%async_computation.10 | async-start | bytes 3244032 | tf_op jit(solution)/shard_map/all_gather | solution.py:148
  10.2 8.6 collective-permute-start.1
  15.1 1866.5 %all-reduce.97.cloned.1.call-start = ((), (), s32[]{:S(2)}) async-start(), calls=%async_computation.11 | async-start | bytes 16777216 | tf_op jit(solution)/shard_map/psum | solution.py:200
  18.1 153.1 %copy-start.84 = (f32[704]{0:T(1024)}, f32[704]{0:T(1024)S(1)}, u32[]{:S(2)}) copy-start(f32[704]{0:T(1024)S(1)} %get-tuple-element.143) | copy-start | bytes 8452
  18.1 153.1 %copy-start.86 = (f32[704]{0:T(1024)}, f32[704]{0:T(1024)S(1)}, u32[]{:S(2)}) copy-start(f32[704]{0:T(1024)S(1)} %get-tuple-element.144) | copy-start | bytes 8452
  18.1 153.1 %copy-start.88 = (f32[704]{0:T(1024)}, f32[704]{0:T(1024)S(1)}, u32[]{:S(2)}) copy-start(f32[704]{0:T(1024)S(1)} %get-tuple-element.145) | copy-start | bytes 8452
  18.1 153.0 %copy-start.90 = (f32[704]{0:T(1024)}, f32[704]{0:T(1024)S(1)}, u32[]{:S(2)}) copy-start(f32[704]{0:T(1024)S(1)} %get-tuple-element.146) | copy-start | bytes 8452
  18.8 158.0 %copy-start.71 = (f32[704]{0:T(1024)}, f32[704]{0:T(1024)S(1)}, u32[]{:S(2)}) copy-start(f32[704]{0:T(1024)S(1)} %fusion.79) | copy-start | bytes 8452
  20.5 156.4 %copy-start.69 = (f32[1,1024]{1,0:T(1,128)}, f32[1,1024]{1,0:T(1,128)S(1)}, u32[]{:S(2)}) copy-start(f32[1,1024]{1,0:T(1,128)S(1)} %get-tuple-element.272) | copy-start | bytes 12292
  132.4 38.0 collective-permute-start
  1590.6 337.3 %all-gather.17.cloned.1.call-start = ((), (), s32[]{:S(2)}) async-start(), calls=%async_computation.12 | async-start | bytes 7077888 | tf_op jit(solution)/shard_map/all_gather | solution.py:149
  1591.2 384.1 %all-gather.19.cloned.1.call-start = ((), (), s32[]{:S(2)}) async-start(), calls=%async_computation.13 | async-start | bytes 7077888 | tf_op jit(solution)/shard_map/all_gather | solution.py:150
  1592.0 466.3 %all-gather.23.cloned.1.call-start = ((), (), s32[]{:S(2)}) async-start(), calls=%async_computation.16 | async-start | bytes 5242880 | tf_op jit(solution)/shard_map/all_gather | solution.py:143
  1594.5 509.8 %all-gather.21.cloned.1.call-start = ((), (), s32[]{:S(2)}) async-start(), calls=%async_computation.14 | async-start | bytes 7077888 | tf_op jit(solution)/shard_map/all_gather | solution.py:151
  1595.2 295.8 %copy-start.73 = (f32[2048]{0:T(1024)S(1)}, f32[2048]{0:T(1024)}, u32[]{:S(2)}) copy-start(f32[2048]{0:T(1024)} %param.41) | copy-start | bytes 24580
  1595.2 839.5 %all-reduce.99.cloned.1.call-start = ((), (), s32[]{:S(2)}) async-start(), calls=%async_computation.17 | async-start | bytes 16777216 | tf_op jit(solution)/shard_map/psum | solution.py:228
  2143.7 1777.1 %reduce-scatter.8.cloned.1.call-start = ((), (), s32[]{:S(2)}) async-start(), calls=%async_computation.15 | async-start | bytes 10485760 | tf_op jit(solution)/shard_map/reduce_scatter | solution.py:208
  2352.8 1776.5 %all-reduce.101.cloned.1.call-start = ((), (), s32[]{:S(2)}) async-start(), calls=%async_computation.18 | async-start | bytes 16777216 | tf_op jit(solution)/shard_map/psum | solution.py:278
  3819.2 10.5 collective-permute-start.2
  3839.6 351.1 %all-reduce.103.cloned.1.call-start = ((), (), s32[]{:S(2)}) async-start(), calls=%async_computation.25 | async-start | bytes 2883584 | tf_op jit(solution)/shard_map/psum | solution.py:290
  3845.1 408.1 %reduce-scatter.14.cloned.1.call-start = ((), (), s32[]{:S(2)}) async-start(), calls=%async_computation.21 | async-start | bytes 6488064 | tf_op jit(solution)/shard_map/reduce_scatter | solution.py:285
  3854.6 461.5 %reduce-scatter.12.cloned.1.call-start = ((), (), s32[]{:S(2)}) async-start(), calls=%async_computation.20 | async-start | bytes 6488064 | tf_op jit(solution)/shard_map/reduce_scatter | solution.py:284
  3863.3 516.2 %reduce-scatter.10.cloned.1.call-start = ((), (), s32[]{:S(2)}) async-start(), calls=%async_computation.19 | async-start | bytes 6488064 | tf_op jit(solution)/shard_map/reduce_scatter | solution.py:283
  3872.4 603.4 %reduce-scatter.16.cloned.1.call-start = ((), (), s32[]{:S(2)}) async-start(), calls=%async_computation.22 | async-start | bytes 14155776 | tf_op jit(solution)/shard_map/reduce_scatter | solution.py:286
  3885.0 687.2 %reduce-scatter.18.cloned.1.call-start = ((), (), s32[]{:S(2)}) async-start(), calls=%async_computation.23 | async-start | bytes 14155776 | tf_op jit(solution)/shard_map/reduce_scatter | solution.py:287
  3897.6 771.1 %reduce-scatter.20.cloned.1.call-start = ((), (), s32[]{:S(2)}) async-start(), calls=%async_computation.24 | async-start | bytes 14155776 | tf_op jit(solution)/shard_map/reduce_scatter | solution.py:288
  3924.4 213.0 %copy-start.94 = (f32[2048]{0:T(1024)S(1)}, f32[2048]{0:T(1024)}, u32[]{:S(2)}) copy-start(f32[2048]{0:T(1024)} %get-tuple-element.134) | copy-start | bytes 24580
  3924.4 238.4 %copy-start.83 = (f32[1024]{0:T(1024)S(1)}, f32[1024]{0:T(1024)}, u32[]{:S(2)}) copy-start(f32[1024]{0:T(1024)} %copy-done.82) | copy-start | bytes 12292
  (99 other events, 1120.1 us)
Sparse Core Ops, SparseCore 0:
  9.6 83.4 all-gather.8
  95.0 30.1 all-gather.10
  127.1 35.1 all-gather.12
  164.0 31.6 all-gather.14
  1590.8 290.8 all-reduce.96
  1883.4 44.5 all-gather.16
  1929.8 45.5 all-gather.18
  1977.5 80.7 all-gather.22
  2060.2 44.0 all-gather.20
  2143.8 290.8 all-reduce.98
  2437.0 143.4 reduce-scatter.7
  3839.7 289.5 all-reduce.100
  4133.1 57.5 all-reduce.102
  4195.0 58.2 reduce-scatter.13
  4257.1 59.0 reduce-scatter.11
  4320.4 59.0 reduce-scatter.9
  4383.4 92.3 reduce-scatter.15
  4479.7 92.3 reduce-scatter.17
  4576.2 92.3 reduce-scatter.19
where the time goes:
time: 4710 us; the launch traced here: 4680 us
  local copies, waits for them, and re-layouts  2710 us (58%)
  waiting for transfers between devices  1400 us (30%)
  other arithmetic  315 us (7%)
  matrix products  186 us (4%)
    slice x62, local copies, waits for them, and re-layouts, shards(): lax.associative_scan(affine, (shifted, hidden_grad), axis=1, reverse=True)  809 us
    slice x58, local copies, waits for them, and re-layouts, shards(): lax.associative_scan(affine, (retain, inflow), axis=1)  752 us
    pad x36, local copies, waits for them, and re-layouts, shards(): lax.associative_scan(affine, (retain, inflow), axis=1)  508 us
    pad x36, local copies, waits for them, and re-layouts, shards(): lax.associative_scan(affine, (shifted, hidden_grad), axis=1, reverse=True)  504 us
    psum x1, waiting for transfers between devices, shards(): branch = lax.psum(contract_last(gated, fetched[2]), 'rep')  286 us
    psum x1, waiting for transfers between devices, shards(): normed_grad = lax.psum(normed_terms, 'rep')  205 us
    reduce_scatter x1, waiting for transfers between devices, shards(): lax.psum_scatter(feed_down_grad, ('seq', 'row'), scatter_dimension=0, til...  96.5 us
    reduce_scatter x1, waiting for transfers between devices, shards(): lax.psum_scatter(feed_up_grad, ('seq', 'row'), scatter_dimension=0, tiled...  96.4 us
  transfers between devices with their start and end apart: 22, of which 18 were waited for; matrix products, arithmetic and copies ran while one was open for 67% of the time, Pallas kernels for 0%

commit v1 on v0

v1 whole, which is shorter than its diff:
```python
import jax
import jax.numpy as jnp
from jax import lax
from jax.experimental import pallas as pl
from jax.experimental.pallas import tpu as pltpu
from jax.sharding import PartitionSpec as P

eps = 1e-06
SEGS = 8
BF = jnp.bfloat16
F32 = jnp.float32
LIMIT = 48 * 1024 * 1024


def gelu(v):
    return 0.5 * v * (1.0 + jnp.tanh(0.7978845608 * (v + 0.044715 * v * v * v)))


def gelu_both(v):
    square = v * v
    t = jnp.tanh(0.7978845608 * v * (1.0 + 0.044715 * square))
    value = 0.5 * v * (1.0 + t)
    slope = 0.5 * (1.0 + t) + 0.5 * v * (1.0 - t * t) * 0.7978845608 * (1.0 + 3 * 0.044715 * square)
    return value, slope


def one_minus_exp(y):
    series = y * (1 - y / 2 * (1 - y / 3 * (1 - y / 4 * (1 - y / 5 * (1 - y / 6 * (1 - y / 7))))))
    return jnp.where(y < 0.4, series, 1.0 - jnp.exp(-y))


def gather_line(own, axis):
    count, me = lax.axis_size(axis), lax.axis_index(axis)
    width = own.shape[1]
    total = jnp.zeros((own.shape[0], count * width), own.dtype)
    total = lax.dynamic_update_slice(total, own, (0, me * width))
    right, left = own, own
    held = {}
    for k in range(1, count):
        right = lax.ppermute(right, axis, [(i, i + 1) for i in range(k - 1, count - 1)])
        left = lax.ppermute(left, axis, [(i, i - 1) for i in range(1, count - k + 1)])
        held[-k], held[k] = right, left
    for k in range(1, count):
        there = me + k
        piece = jnp.where(there < count, held[k], held[k - count])
        total = lax.dynamic_update_slice(total, piece, (0, lax.rem(there, count) * width))
    return total


def reduce_line(whole, axis):
    count, me = lax.axis_size(axis), lax.axis_index(axis)
    width = whole.shape[1] // count

    def part(target):
        target = jnp.clip(target, 0, count - 1)
        return lax.dynamic_slice_in_dim(whole, target * width, width, 1).astype(F32)

    right = left = None
    for k in range(1, count):
        far = count - k
        to_right, to_left = part(me + far), part(me - far)
        if k > 1:
            to_right, to_left = to_right + right, to_left + left
        right = lax.ppermute(to_right.astype(BF), axis, [(i, i + 1) for i in range(k)]).astype(F32)
        left = lax.ppermute(to_left.astype(BF), axis, [(i, i - 1) for i in range(far, count)]).astype(F32)
    return part(me) + right + left


def small_sum(own, axis):
    count = lax.axis_size(axis)
    total = own
    for k in range(1, count):
        total = total + lax.ppermute(own, axis, [(i, (i + k) % count) for i in range(count)])
    return total


def row_sum(values, axis):
    sums = jnp.sum(values, axis=1)
    return small_sum(sums.reshape(8, -1), axis).reshape(-1, 1)


def by_step(values):
    length, width = values.shape
    return values.reshape(SEGS, length // SEGS, width).transpose(1, 0, 2).reshape(length, width)


def by_segment(values):
    length, width = values.shape
    return values.reshape(length // SEGS, SEGS, width).transpose(1, 0, 2).reshape(length, width)


def block_diagonal(blocks):
    heads, wide = blocks.shape[0], blocks.shape[1]
    rows = [jnp.pad(blocks[h], ((0, 0), (h * wide, (heads - 1 - h) * wide))) for h in range(heads)]
    return jnp.concatenate(rows, axis=0)


def diagonal_blocks(dense, heads):
    wide = dense.shape[0] // heads
    return jnp.stack([dense[h * wide : (h + 1) * wide, h * wide : (h + 1) * wide] for h in range(heads)])


def forward_kernel(
    conv_in, same, prefix, params, decay_w, input_w,
    out_conv, out_decay, out_gate, out_retain, out_prod, out_state, out_pre_a, out_pre_b, out_total,
    last_rows, prod_now, state_now, inflow_s,
):
    step = pl.program_id(0)
    rows = conv_in.shape[0]

    @pl.when(step == 0)
    def _():
        last_rows[...] = prefix[...].astype(F32)
        prod_now[...] = jnp.ones_like(prod_now)
        state_now[...] = jnp.zeros_like(state_now)

    now = conv_in[...].astype(F32)
    ext = jnp.concatenate([last_rows[...], now], axis=0)
    same_all = same[...]
    total = params[4:5, :] + params[0:1, :] * now
    for k in (1, 2, 3):
        start = 24 - 8 * k
        total = total + params[k : k + 1, :] * ext[start : start + rows] * same_all[:, k : k + 1]
    last_rows[...] = now[rows - 24 :]
    out_conv[...] = total
    low = total.astype(BF)
    decay_sig = jax.nn.sigmoid(jnp.dot(low, decay_w[...], preferred_element_type=F32) + params[5:6, :])
    gate_sig = jax.nn.sigmoid(jnp.dot(low, input_w[...], preferred_element_type=F32) + params[6:7, :])
    out_decay[...] = decay_sig
    out_gate[...] = gate_sig
    expo = params[7:8, :] * decay_sig
    out_retain[...] = same_all[:, 1:2] * jnp.exp(-expo)
    inflow_s[...] = jnp.sqrt(one_minus_exp(2.0 * expo)) * gate_sig * total
    prod, state = prod_now[...], state_now[...]
    for t in range(rows // SEGS):
        at = slice(t * SEGS, (t + 1) * SEGS)
        keep = out_retain[at, :]
        prod = prod * keep
        state = state * keep + inflow_s[at, :]
        out_prod[at, :] = prod
        out_state[at, :] = state
    prod_now[...] = prod
    state_now[...] = state

    @pl.when(step == pl.num_programs(0) - 1)
    def _():
        carry_a = jnp.ones_like(prod[0:1])
        carry_b = jnp.zeros_like(carry_a)
        for s in range(SEGS):
            out_pre_a[s : s + 1, :] = carry_a
            out_pre_b[s : s + 1, :] = carry_b
            carry_b = prod[s : s + 1] * carry_b + state[s : s + 1]
            carry_a = prod[s : s + 1] * carry_a
        out_total[0:1, :] = carry_a
        out_total[1:2, :] = carry_b
        out_total[2:8, :] = jnp.zeros((6, carry_a.shape[1]), F32)


def recur_forward(conv_in, same, prefix, params, decay_w, input_w, rows=128):
    length, width = conv_in.shape
    block = pl.BlockSpec((rows, width), lambda i: (i, 0))
    fixed = lambda shape: pl.BlockSpec(shape, lambda i: (0, 0))
    big = jax.ShapeDtypeStruct((length, width), F32)
    small = jax.ShapeDtypeStruct((SEGS, width), F32)
    return pl.pallas_call(
        forward_kernel,
        grid=(length // rows,),
        in_specs=[
            block,
            pl.BlockSpec((rows, 8), lambda i: (i, 0)),
            fixed((24, width)),
            fixed((8, width)),
            fixed((width, width)),
            fixed((width, width)),
        ],
        out_specs=[block] * 6 + [fixed((SEGS, width))] * 3,
        out_shape=[big] * 6 + [small] * 3,
        scratch_shapes=[
            pltpu.VMEM((24, width), F32),
            pltpu.VMEM((SEGS, width), F32),
            pltpu.VMEM((SEGS, width), F32),
            pltpu.VMEM((rows, width), F32),
        ],
        compiler_params=pltpu.CompilerParams(vmem_limit_bytes=LIMIT),
        cost_estimate=pl.CostEstimate(
            flops=4 * length * width * width, bytes_accessed=26 * length * width, transcendentals=5 * length * width
        ),
    )(conv_in, same, prefix, params, decay_w, input_w)


def adjoint_kernel(
    gated_grad, gate_branch, hidden, retain,
    out_local, out_after, out_branch, out_pre_a, out_pre_b, out_total, out_dot,
    local_now, after_now, next_retain, grad_s,
):
    step = pl.program_id(0)
    rows = gated_grad.shape[0]

    @pl.when(step == 0)
    def _():
        local_now[...] = jnp.zeros_like(local_now)
        after_now[...] = jnp.ones_like(after_now)
        next_retain[...] = jnp.ones_like(next_retain)

    value, slope = gelu_both(gate_branch[...])
    upstream = gated_grad[...]
    grad_s[...] = upstream * value
    branch = upstream * hidden[...] * slope
    out_branch[...] = branch.astype(BF)
    out_dot[...] = jnp.broadcast_to(jnp.sum(branch * gate_branch[...], axis=1, keepdims=True), out_dot.shape)
    local, after, keep = local_now[...], after_now[...], next_retain[...]
    for t in reversed(range(rows // SEGS)):
        at = slice(t * SEGS, (t + 1) * SEGS)
        local = grad_s[at, :] + keep * local
        after = keep * after
        out_local[at, :] = local
        out_after[at, :] = after
        keep = retain[at, :]
    local_now[...] = local
    after_now[...] = after
    next_retain[...] = keep

    @pl.when(step == pl.num_programs(0) - 1)
    def _():
        carry_a = jnp.ones_like(local[0:1])
        carry_b = jnp.zeros_like(carry_a)
        for s in reversed(range(SEGS)):
            out_pre_a[s : s + 1, :] = carry_a
            out_pre_b[s : s + 1, :] = carry_b
            carry_b = keep[s : s + 1] * (local[s : s + 1] + after[s : s + 1] * carry_b)
            carry_a = keep[s : s + 1] * after[s : s + 1] * carry_a
        out_total[0:1, :] = carry_a
        out_total[1:2, :] = carry_b
        out_total[2:8, :] = jnp.zeros((6, carry_a.shape[1]), F32)


def recur_adjoint(gated_grad, gate_branch, hidden, retain, rows=128):
    length, width = gated_grad.shape
    last = length // rows - 1
    block = pl.BlockSpec((rows, width), lambda i: (last - i, 0))
    fixed = lambda shape: pl.BlockSpec(shape, lambda i: (0, 0))
    big = jax.ShapeDtypeStruct((length, width), F32)
    small = jax.ShapeDtypeStruct((SEGS, width), F32)
    return pl.pallas_call(
        adjoint_kernel,
        grid=(length // rows,),
        in_specs=[block] * 4,
        out_specs=[block] * 3 + [fixed((SEGS, width))] * 3 + [pl.BlockSpec((rows, 128), lambda i: (last - i, 0))],
        out_shape=[big, big, jax.ShapeDtypeStruct((length, width), BF)]
        + [small] * 3
        + [jax.ShapeDtypeStruct((length, 128), F32)],
        scratch_shapes=[pltpu.VMEM((SEGS, width), F32)] * 3 + [pltpu.VMEM((rows, width), F32)],
        compiler_params=pltpu.CompilerParams(vmem_limit_bytes=LIMIT),
        cost_estimate=pl.CostEstimate(
            flops=20 * length * width, bytes_accessed=26 * length * width, transcendentals=length * width
        ),
    )(gated_grad, gate_branch, hidden, retain)


def backward_kernel(
    local, after, enter, hidden, hidden_before, carry, conv_out, decay_sig, gate_sig, retain, same, params, conv_in,
    decay_w, input_w,
    out_decay, out_input, out_low, out_first, out_sums,
    next_one, next_two, next_three,
):
    step = pl.program_id(0)
    blocks = pl.num_programs(0)
    rows = local.shape[0]
    width = local.shape[1]

    @pl.when(step == 0)
    def _():
        for held in (next_one, next_two, next_three):
            held[...] = jnp.zeros_like(held)
        out_sums[...] = jnp.zeros_like(out_sums)

    def per_step(small):
        return jnp.broadcast_to(small[None], (rows // SEGS, SEGS, width)).reshape(rows, width)

    def sums(values):
        return jnp.sum(values.reshape(rows // SEGS, SEGS, width), axis=0)

    adjoint = local[...] + after[...] * per_step(enter[...])
    ahead = jnp.where(step == blocks - 1, carry[...], hidden_before[...])
    hidden_prev = jnp.concatenate([ahead, hidden[...][: rows - SEGS]], axis=0)
    conv, decay, gate = conv_out[...], decay_sig[...], gate_sig[...]
    rate = params[7:8, :]
    expo = rate * decay
    inner = one_minus_exp(2.0 * expo)
    root = jnp.sqrt(inner)
    expo_grad = adjoint * (gate * conv * (1.0 - inner) / root - retain[...] * hidden_prev)
    decay_grad = (expo_grad * rate * decay * (1.0 - decay)).astype(BF)
    input_grad = (adjoint * root * conv * gate * (1.0 - gate)).astype(BF)
    out_decay[...] = decay_grad
    out_input[...] = input_grad
    dims = (((1,), (1,)), ((), ()))
    conv_grad = (
        adjoint * root * gate
        + lax.dot_general(decay_grad, decay_w[...], dims, preferred_element_type=F32)
        + lax.dot_general(input_grad, input_w[...], dims, preferred_element_type=F32)
    )
    same_all = same[...]
    now = conv_in[...].astype(F32)
    low = params[0:1, :] * conv_grad
    out_sums[0:8, :] += sums(conv_grad * now)
    for k, held in ((1, next_one), (2, next_two), (3, next_three)):
        masked = conv_grad * same_all[:, k : k + 1]
        moved = jnp.concatenate([masked[8 * k :], held[...]], axis=0)
        held[...] = masked[: 8 * k]
        low = low + params[k : k + 1, :] * moved
        out_sums[8 * k : 8 * k + 8, :] += sums(moved * now)
    out_low[...] = low
    out_sums[32:40, :] += sums(conv_grad)
    out_sums[40:48, :] += sums(decay_grad.astype(F32))
    out_sums[48:56, :] += sums(input_grad.astype(F32))
    out_sums[56:64, :] += sums(expo_grad * decay)

    @pl.when(step == blocks - 1)
    def _():
        out_first[0:8, :] = next_one[...]
        out_first[8:24, :] = next_two[...]
        out_first[24:48, :] = next_three[...]


def recur_backward(
    local, after, enter, hidden, carry, conv_out, decay_sig, gate_sig, retain, same, params, conv_in, decay_w, input_w,
    rows=128,
):
    length, width = local.shape
    last = length // rows - 1
    block = pl.BlockSpec((rows, width), lambda i: (last - i, 0))
    fixed = lambda shape: pl.BlockSpec(shape, lambda i: (0, 0))
    steps = rows // SEGS
    before = pl.BlockSpec((SEGS, width), lambda i: (jnp.maximum((last - i) * steps - 1, 0), 0))
    return pl.pallas_call(
        backward_kernel,
        grid=(length // rows,),
        in_specs=[
            block, block, fixed((SEGS, width)), block, before, fixed((SEGS, width)), block, block, block, block,
            pl.BlockSpec((rows, 8), lambda i: (last - i, 0)),
            fixed((8, width)), block, fixed((width, width)), fixed((width, width)),
        ],
        out_specs=[block, block, block, fixed((48, width)), fixed((64, width))],
        out_shape=[
            jax.ShapeDtypeStruct((length, width), BF),
            jax.ShapeDtypeStruct((length, width), BF),
            jax.ShapeDtypeStruct((length, width), F32),
            jax.ShapeDtypeStruct((48, width), F32),
            jax.ShapeDtypeStruct((64, width), F32),
        ],
        scratch_shapes=[
            pltpu.VMEM((8, width), F32),
            pltpu.VMEM((16, width), F32),
            pltpu.VMEM((24, width), F32),
        ],
        compiler_params=pltpu.CompilerParams(vmem_limit_bytes=LIMIT),
        cost_estimate=pl.CostEstimate(
            flops=4 * length * width * width, bytes_accessed=40 * length * width, transcendentals=5 * length * width
        ),
    )(
        local, after, enter, hidden, hidden, carry, conv_out, decay_sig, gate_sig, retain, same, params, conv_in,
        decay_w, input_w,
    )


def per_segment(small, length):
    return jnp.broadcast_to(small[None], (length // SEGS,) + small.shape).reshape(length, small.shape[1])


def rows_dot(left, right):
    return lax.dot_general(left, right, (((0,), (0,)), ((), ())), preferred_element_type=F32)


def back_dot(left, right):
    return lax.dot_general(left, right, (((1,), (1,)), ((), ())), preferred_element_type=F32)


def dot(left, right):
    return jnp.dot(left, right, preferred_element_type=F32)


def shards(
    block_input, cotangent, segment_ids, pad_mask, state_init, window_init,
    recur_input, recur_gate, recur_output, feed_gate, feed_up, feed_down,
    conv_kernel, conv_bias, decay_gate, input_gate, decay_bias, input_bias, decay_logit, mixer_gain, feed_gain,
):
    own_width = block_input.shape[2]
    features = mixer_gain.shape[0]
    length = segment_ids.shape[1]
    taps = conv_kernel.shape[0]
    edge = taps - 1
    heads = decay_gate.shape[0]
    rep = lax.axis_index("rep")
    seq, seqs = lax.axis_index("seq"), lax.axis_size("seq")
    at_start = seq == 0
    to_next = [(i, i + 1) for i in range(seqs - 1)]
    to_last = [(i + 1, i) for i in range(seqs - 1)]

    def weights(shard):
        return lax.all_gather(shard, ("seq", "row"), axis=0, tiled=True)

    def spread(partial_grad):
        low = partial_grad.astype(BF)
        return lax.psum_scatter(low, ("seq", "row"), scatter_dimension=0, tiled=True).astype(F32)

    def own_part(vector):
        return lax.dynamic_slice_in_dim(vector, rep * own_width, own_width, 0)[None]

    x_own = by_step(block_input[0]).astype(F32)
    cot_own = by_step(cotangent[0] * pad_mask[0][:, None].astype(BF))
    mixer_own, feed_own = own_part(mixer_gain), own_part(feed_gain)
    s1 = lax.rsqrt(row_sum(x_own * x_own, "rep") / features + eps)
    normed = gather_line((x_own * s1 * mixer_own).astype(BF), "rep")
    w_input, w_gate, w_output = weights(recur_input), weights(recur_gate), weights(recur_output)
    w_feed_gate, w_feed_up, w_down = weights(feed_gate), weights(feed_up), weights(feed_down)

    left_ids = lax.ppermute(segment_ids[:, -edge:].astype(F32), "seq", to_next).astype(jnp.int32)
    left_ids = jnp.where(at_start, jnp.broadcast_to(segment_ids[:, :1], left_ids.shape), left_ids)
    ids_ext = jnp.concatenate([left_ids, segment_ids], axis=1)[0]
    same = [(ids_ext[edge - k : edge - k + length] == segment_ids[0]).astype(F32) for k in range(taps)]
    same = by_step(jnp.stack(same + [same[0]] * (8 - taps), axis=1))

    rate = 8.0 * jax.nn.softplus(decay_logit)
    params = jnp.concatenate([conv_kernel, jnp.stack([conv_bias, decay_bias, input_bias, rate])], axis=0)
    decay_w, input_w = block_diagonal(decay_gate), block_diagonal(input_gate)

    conv_in = dot(normed, w_input).astype(BF)
    gate_branch = dot(normed, w_gate)
    ends = conv_in.reshape(length // SEGS, SEGS, -1)[-edge:]
    left = lax.ppermute(ends[:, -1], "seq", to_next)
    left = jnp.where(at_start, window_init[0], left)
    prefix = jnp.concatenate([left[:, None], ends[:, :-1]], axis=1).reshape(edge * SEGS, -1)
    block_windows = ends[:, -1]

    conv_out, decay_sig, gate_sig, retain, products, states, pre_a, pre_b, total = recur_forward(
        conv_in, same, prefix, params, decay_w, input_w
    )
    state_in = state_init
    for k in range(1, seqs):
        arriving = lax.ppermute(total[0:1] * state_in + total[1:2], "seq", to_next)
        state_in = jnp.where(seq == k, arriving, state_in)
    block_states = total[0:1] * state_in + total[1:2]
    carry = pre_a * state_in + pre_b
    hidden = states + products * per_segment(carry, length)
    gated = (hidden * gelu(gate_branch)).astype(BF)

    middle = x_own + reduce_line(back_dot(gated, w_output).astype(BF), "rep")
    s2 = lax.rsqrt(row_sum(middle * middle, "rep") / features + eps)
    normed_mid = gather_line((middle * s2 * feed_own).astype(BF), "rep")
    cot = gather_line(cot_own, "rep")
    gate_pre, up_pre = dot(normed_mid, w_feed_gate), dot(normed_mid, w_feed_up)
    grad_feed = dot(cot, w_down)
    value, slope = gelu_both(gate_pre)
    feed_low = (value * up_pre).astype(BF)
    gate_grad_f, up_grad_f = grad_feed * up_pre * slope, grad_feed * value
    gate_grad, up_grad = gate_grad_f.astype(BF), up_grad_f.astype(BF)
    mid_mean = row_sum(gate_grad_f * gate_pre + up_grad_f * up_pre, "rep") / features

    mid_grad = reduce_line((back_dot(gate_grad, w_feed_gate) + back_dot(up_grad, w_feed_up)).astype(BF), "rep")
    xh2 = middle * s2
    feed_gain_own = jnp.sum(mid_grad * xh2, axis=0)
    middle_grad = cot_own.astype(F32) + s2 * (mid_grad * feed_own - xh2 * mid_mean)
    middle_low = gather_line(middle_grad.astype(BF), "rep")
    feed_down_grad = spread(rows_dot(cot, feed_low))
    feed_gate_grad = spread(rows_dot(normed_mid, gate_grad))
    feed_up_grad = spread(rows_dot(normed_mid, up_grad))
    feed_out = reduce_line(back_dot(feed_low, w_down).astype(BF), "rep")
    block_output = by_segment((middle + feed_out).astype(BF))[None]

    gated_grad = dot(middle_low, w_output)
    recur_output_grad = spread(rows_dot(middle_low, gated))
    local, after, branch_grad, enter_a, enter_b, back_total, branch_dot = recur_adjoint(
        gated_grad, gate_branch, hidden, retain
    )
    entering = jnp.zeros_like(state_init)
    for k in range(1, seqs):
        arriving = lax.ppermute(back_total[0:1] * entering + back_total[1:2], "seq", to_last)
        entering = jnp.where(seq == seqs - 1 - k, arriving, entering)
    enter = enter_a * entering + enter_b
    decay_grad, input_grad_low, low_grad, first, sums = recur_backward(
        local, after, enter, hidden, carry, conv_out, decay_sig, gate_sig, retain, same, params, conv_in, decay_w, input_w
    )
    owed = [first[0:8], first[8:24], first[24:48]]
    owed = [o.reshape(k + 1, SEGS, -1) for k, o in enumerate(owed)]
    ahead = prefix.reshape(edge, SEGS, -1).astype(F32)
    back_share = jnp.zeros_like(ahead)
    tap_extra = [jnp.zeros_like(conv_bias)]
    for k in range(1, taps):
        term = jnp.pad(owed[k - 1], ((edge - k, 0), (0, 0), (0, 0)))
        tap_extra.append(jnp.sum(term * ahead, axis=(0, 1)))
        back_share = back_share + conv_kernel[k] * term
    from_right = lax.ppermute(back_share[:, 0], "seq", to_last)
    share = jnp.concatenate([back_share[:, 1:], from_right[:, None]], axis=1)
    low_grad = low_grad.reshape(length // SEGS, SEGS, -1)
    low_grad = jnp.concatenate([low_grad[:-edge], low_grad[-edge:] + share], axis=0).reshape(length, -1)
    input_low = low_grad.astype(BF)
    in_mean = jnp.sum(low_grad * conv_in.astype(F32), axis=1) + branch_dot[:, 0]
    in_mean = small_sum(in_mean.reshape(8, -1), "rep").reshape(-1, 1) / features

    normed_grad = reduce_line((back_dot(input_low, w_input) + back_dot(branch_grad, w_gate)).astype(BF), "rep")
    recur_gate_grad = spread(rows_dot(normed, branch_grad))
    recur_input_grad = spread(rows_dot(normed, input_low))
    xh1 = x_own * s1
    mixer_gain_own = jnp.sum(normed_grad * xh1, axis=0)
    input_grad = middle_grad + s1 * (normed_grad * mixer_own - xh1 * in_mean)
    input_grad = by_segment(input_grad.astype(BF))[None]

    conv_low = conv_out.astype(BF)
    decay_gate_grad = diagonal_blocks(rows_dot(conv_low, decay_grad), heads)
    input_gate_grad = diagonal_blocks(rows_dot(conv_low, input_grad_low), heads)
    sums = jnp.sum(sums.reshape(8, 8, -1), axis=1)
    conv_kernel_grad = sums[:taps] + jnp.stack(tap_extra)
    small = (
        conv_kernel_grad, sums[4], decay_gate_grad, input_gate_grad, sums[5], sums[6],
        sums[7] * 8.0 * jax.nn.sigmoid(decay_logit),
    )
    small = lax.psum(small, ("seq", "row"))
    gains = jnp.stack([mixer_gain_own, feed_gain_own])
    gains = lax.dynamic_update_slice(jnp.zeros((2, features), F32), gains, (0, rep * own_width))
    gains = lax.psum(gains, ("seq", "row", "rep"))
    return (
        block_output, block_states[:, None], block_windows[None, None], input_grad,
        recur_input_grad, recur_gate_grad, recur_output_grad, feed_gate_grad, feed_up_grad, feed_down_grad,
        *small, gains[0], gains[1],
    )


def solution(mesh):
    tokens = P("row", "seq", "rep")
    matrix = P(("seq", "row"), "rep")
    in_specs = (
        tokens, tokens, P("row", "seq"), P("row", "seq"), P("row", "rep"), P("row", None, "rep"),
        matrix, matrix, matrix, matrix, matrix, matrix,
        P(None, "rep"), P("rep"), P("rep", None, None), P("rep", None, None), P("rep"), P("rep"), P("rep"), P(), P(),
    )
    out_specs = (
        tokens, tokens, P("row", "seq", None, "rep"), tokens,
        matrix, matrix, matrix, matrix, matrix, matrix,
        P(None, "rep"), P("rep"), P("rep", None, None), P("rep", None, None), P("rep"), P("rep"), P("rep"), P(), P(),
    )
    return jax.shard_map(shards, mesh=mesh, in_specs=in_specs, out_specs=out_specs, check_vma=False)
```

time: 4710 us -> 932 us (0.20)
  local copies, waits for them, and re-layouts: 2710 us -> 42.5 us
  waiting for transfers between devices: 1400 us -> 295 us
  other arithmetic: 315 us -> 92.3 us
  starting transfers between devices: 10.6 us -> 210 us
    slice x125 -> x8, local copies, waits for them, and re-layouts: 1570 us -> 3.32 us  [the longest x1 2.43 us: shards(): low_grad[:-edge]]
    pad x72 -> x0, local copies, waits for them, and re-layouts: 1010 us -> none  [the longest x36 508 us: shards(): lax.associative_scan(affine, (retain, inflow), axis=1)]
    psum x4 -> x1, waiting for transfers between devices: 597 us -> 0.01 us  [shards(): small = lax.psum(small, ('seq', 'row'))]
    reduce_scatter x7 -> x6, waiting for transfers between devices: 478 us -> 0.03 us  [spread(): lax.psum_scatter(low, ('seq', 'row'), scatter_dimension=0, tiled=True)]
    all_gather x8 -> x6, waiting for transfers between devices: 315 us -> 0.03 us  [weights(): return lax.all_gather(shard, ('seq', 'row'), axis=0, tiled=True)]
    ppermute x3 -> x65, waiting for transfers between devices: 5.74 us -> 292 us  [the longest x12 152 us: gather_line(): lax.ppermute(left, axis, [(i, i - 1) for i in range(1, count - k + 1)])]
    ppermute x3 -> x65, starting transfers between devices: 9.29 us -> 210 us  [the longest x12 71.5 us: reduce_line(): lax.ppermute(to_right.astype(BF), axis, [(i, i + 1) for i in range(k)])]
    add x65 -> x7, other arithmetic: 130 us -> 0.97 us  [the longest x1 0.92 us: shards(): low_grad[-edge:] + share]
  transfers between devices with their start and end apart: 22 -> 78, of which waited for: 18 -> 28; matrix products, arithmetic and copies ran while one was open for 67% -> 27% of each run, Pallas kernels for 0% -> 4%
where the time goes in v1:
time: 932 us; the launch traced here: 921 us
  waiting for transfers between devices  295 us (32%)
  starting transfers between devices  210 us (23%)
  matrix products  165 us (18%)
  other arithmetic  92.3 us (10%)
  blocking collectives  61.5 us (7%)
  local copies, waits for them, and re-layouts  42.5 us (5%)
  Pallas kernels  38.7 us (4%)
  between operations  16.2 us (2%)
    ppermute x12, waiting for transfers between devices, gather_line(): lax.ppermute(left, axis, [(i, i - 1) for i in range(1, count - k + 1)])  152 us
    ppermute x12, waiting for transfers between devices, reduce_line(): lax.ppermute(to_right.astype(BF), axis, [(i, i + 1) for i in range(k)])  75.7 us
    ppermute x12, starting transfers between devices, reduce_line(): lax.ppermute(to_right.astype(BF), axis, [(i, i + 1) for i in range(k)])  71.5 us
    dot_general x6, matrix products, dot(): return jnp.dot(left, right, preferred_element_type=F32)  61.2 us
    ppermute x12, starting transfers between devices, small_sum(): lax.ppermute(own, axis, [(i, (i + k) % count) for i in range(count)])  57.9 us
    dot_general x8, matrix products, rows_dot(): lax.dot_general(left, right, (((0,), (0,)), ((), ())), preferred_element_...  53 us
    dot_general x6, matrix products, back_dot(): lax.dot_general(left, right, (((1,), (1,)), ((), ())), preferred_element_...  50.4 us
    ppermute x12, waiting for transfers between devices, gather_line(): lax.ppermute(right, axis, [(i, i + 1) for i in range(k - 1, count - 1)])  39.4 us
  transfers between devices with their start and end apart: 78, of which 28 were waited for; matrix products, arithmetic and copies ran while one was open for 27% of the time, Pallas kernels for 4%

profile of v1, /device:TPU:0, one launch (start us, length us, event | category | flops | bytes accessed | tf_op | source)
XLA Modules:
  0.0 921.2 jit_solution(7954645899302723578)
XLA Ops:
  28.2 19.7 %collective-permute-done.4 = bf16[1024,512]{1,0:T(8,128)(2,1)S(1)} collective-permute-done((bf16[1024,512]{1,0:T(8,128)(2,1)S(1)}, bf16[1024,512]{1,0:T(8,128)(2,1)S(1)}, u32[]{:S(2)}, u32[]{:S(2)}) %collective-permute-start.4) | collective-permute-done | bytes 1048608 | tf_op jit(solution)/shard_map/ppermute | solution.py:40
  68.0 9.4 %collective-permute-done.7 = bf16[1024,512]{1,0:T(8,128)(2,1)S(1)} collective-permute-done((bf16[1024,512]{1,0:T(8,128)(2,1)}, bf16[1024,512]{1,0:T(8,128)(2,1)S(1)}, u32[]{:S(2)}, u32[]{:S(2)}) %collective-permute-start.7) | collective-permute-done | bytes 1048608 | tf_op jit(solution)/shard_map/ppermute | solution.py:41
  83.6 20.9 %collective-permute-done.8 = bf16[1024,512]{1,0:T(8,128)(2,1)} collective-permute-done((bf16[1024,512]{1,0:T(8,128)(2,1)S(1)}, bf16[1024,512]{1,0:T(8,128)(2,1)}, u32[]{:S(2)}, u32[]{:S(2)}) %collective-permute-start.8) | collective-permute-done | bytes 1048608 | tf_op jit(solution)/shard_map/ppermute | solution.py:41
  120.5 12.0 %shard_map.348 = (f32[1024,704]{1,0:T(8,128)}, f32[1024,704]{1,0:T(8,128)}, f32[1024,704]{1,0:T(8,128)}, f32[1024,704]{1,0:T(8,128)}, f32[1024,704]{1,0:T(8,128)...) custom-call(bf16[1024,704]{1,0:T(8,128)(2,1)S(1)} %convolution_convert_fusion.8.conv, ...), custom_call_target="tpu_custom_call" | custom-call | flops 2030043136 | bytes 18743296 | tf_op jit(solution)/shard_map/pallas_call | solution.py:165
  163.2 14.6 %collective-permute-done.12 = bf16[1024,512]{1,0:T(8,128)(2,1)} collective-permute-done((bf16[1024,512]{1,0:T(8,128)(2,1)}, bf16[1024,512]{1,0:T(8,128)(2,1)}, u32[]{:S(2)}, u32[]{:S(2)}) %collective-permute-start.12) | collective-permute-done | bytes 1048608 | tf_op jit(solution)/shard_map/ppermute | solution.py:64
  185.0 14.6 %collective-permute-done.13 = bf16[1024,512]{1,0:T(8,128)(2,1)} collective-permute-done((bf16[1024,512]{1,0:T(8,128)(2,1)S(1)}, bf16[1024,512]{1,0:T(8,128)(2,1)}, u32[]{:S(2)}, u32[]{:S(2)}) %collective-permute-start.13) | collective-permute-done | bytes 1048608 | tf_op jit(solution)/shard_map/ppermute | solution.py:64
  220.2 20.1 %collective-permute-start.34 = (bf16[1024,512]{1,0:T(8,128)(2,1)S(1)}, bf16[1024,512]{1,0:T(8,128)(2,1)}, u32[]{:S(2)}, u32[]{:S(2)}) collective-permute-start(bf16[1024,512]{1,0:T(8,128)(2,1)S(1)} %get-tuple-element.81), channel_id=1, source_target_pairs={{0,1},{1,2},{2,3},{4,5},{5,6},{6,7},{8,9},{9,10},{10,11},{12,13},{... | collective-permute-start | bytes 3145736 | tf_op jit(solution)/shard_map/ppermute | solution.py:40
  267.6 15.4 %collective-permute-done.33 = bf16[1024,512]{1,0:T(8,128)(2,1)S(1)} collective-permute-done((bf16[1024,512]{1,0:T(8,128)(2,1)S(1)}, bf16[1024,512]{1,0:T(8,128)(2,1)S(1)}, u32[]{:S(2)}, u32[]{:S(2)}) %collective-permute-start.33) | collective-permute-done | bytes 1048608 | tf_op jit(solution)/shard_map/ppermute | solution.py:41
  285.7 19.7 %collective-permute-done.21 = bf16[1024,512]{1,0:T(8,128)(2,1)S(1)} collective-permute-done((bf16[1024,512]{1,0:T(8,128)(2,1)S(1)}, bf16[1024,512]{1,0:T(8,128)(2,1)S(1)}, u32[]{:S(2)}, u32[]{:S(2)}) %collective-permute-start.21) | collective-permute-done | bytes 1048608 | tf_op jit(solution)/shard_map/ppermute | solution.py:41
  306.7 21.2 %collective-permute-done.37 = bf16[1024,512]{1,0:T(8,128)(2,1)S(1)} collective-permute-done((bf16[1024,512]{1,0:T(8,128)(2,1)S(1)}, bf16[1024,512]{1,0:T(8,128)(2,1)S(1)}, u32[]{:S(2)}, u32[]{:S(2)}) %collective-permute-start.37) | collective-permute-done | bytes 1048608 | tf_op jit(solution)/shard_map/ppermute | solution.py:41
  331.3 19.1 %collective-permute-done.25 = bf16[1024,512]{1,0:T(8,128)(2,1)S(1)} collective-permute-done((bf16[1024,512]{1,0:T(8,128)(2,1)S(1)}, bf16[1024,512]{1,0:T(8,128)(2,1)S(1)}, u32[]{:S(2)}, u32[]{:S(2)}) %collective-permute-start.25) | collective-permute-done | bytes 1048608 | tf_op jit(solution)/shard_map/ppermute | solution.py:41
  353.4 19.4 %collective-permute-done.38 = bf16[1024,512]{1,0:T(8,128)(2,1)S(1)} collective-permute-done((bf16[1024,512]{1,0:T(8,128)(2,1)S(1)}, bf16[1024,512]{1,0:T(8,128)(2,1)S(1)}, u32[]{:S(2)}, u32[]{:S(2)}) %collective-permute-start.38) | collective-permute-done | bytes 1048608 | tf_op jit(solution)/shard_map/ppermute | solution.py:41
  385.5 11.7 %fusion.61 = f32[1024,1536]{1,0:T(8,128)} fusion(bf16[1024,2048]{1,0:T(8,128)(2,1)} %select_dynamic-update-slice_fusion.6, bf16[2048,1536]{1,0:T(8,128)(2,1)} %all-gather.15.cloned.1.call-done), kind=kOutput, calls=%fused_computation.205 | convolution fusion | flops 6442450944 | bytes 16777216 | tf_op jit(solution)/shard_map/dot_general | solution.py:379
  397.2 11.7 %fusion.60 = f32[1024,1536]{1,0:T(8,128)} fusion(bf16[1024,2048]{1,0:T(8,128)(2,1)} %select_dynamic-update-slice_fusion.6, bf16[2048,1536]{1,0:T(8,128)(2,1)} %all-gather.13.cloned.1.call-done), kind=kOutput, calls=%fused_computation.204 | convolution fusion | flops 6442450944 | bytes 16777216 | tf_op jit(solution)/shard_map/dot_general | solution.py:379
  408.8 18.9 %fusion.9 = (bf16[1024,1536]{1,0:T(8,128)(2,1)}, f32[1024]{0:T(1024)S(1)}, bf16[1024,1536]{1,0:T(8,128)(2,1)}, f32[1024,1536]{1,0:T(8,128)}) fusion(f32[1024,1536]{1,0:T(8,128)} %fusion.60, f32[1024,1536]{1,0:T(8,128)} %fusion.61, bf16[1024,2048]{1,0:T(8,128)(2,1)} %select_dynamic-update-slice_fusion.3, bf16[2048,1536]{1,0:T(8,128)(2,1)} %all-gather.17.cloned.1.call-done), kind=kOutput, calls=%fused_computation.33 | convolution fusion | flops 6484917248 | bytes 35655680 | tf_op jit(solution)/shard_map/dot_general | solution.py:379
  427.8 13.7 %convolution_convert_fusion.2 = bf16[2048,1536]{1,0:T(8,128)(2,1)} fusion(bf16[1024,2048]{1,0:T(8,128)(2,1)} %select_dynamic-update-slice_fusion.6, f32[1024,1536]{1,0:T(8,128)} %get-tuple-element.139, f32[1024,1536]{1,0:T(8,128)S(1)} %copy-done.67, f32[1024,1536]{1,0:T(8,128)S(1)} %copy-done.68), kind=kOutput, calls=%fused_computation.4 | convolution fusion | flops 6475481088 | bytes 29360128 | tf_op jit(solution)/shard_map/dot_general | solution.py:371
  441.5 11.5 %convolution_convert_fusion.1 = bf16[2048,1536]{1,0:T(8,128)(2,1)} fusion(bf16[1024,2048]{1,0:T(8,128)(2,1)} %select_dynamic-update-slice_fusion.6, bf16[1024,1536]{1,0:T(8,128)(2,1)} %get-tuple-element.90), kind=kOutput, calls=%fused_computation.3 | convolution fusion | flops 6445596672 | bytes 13631488 | tf_op jit(solution)/shard_map/dot_general | solution.py:371
  453.1 19.6 %fusion.21 = f32[1024,2048]{1,0:T(8,128)} fusion(bf16[2048,1536]{1,0:T(8,128)(2,1)} %all-gather.13.cloned.1.call-done, f32[1024,1536]{1,0:T(8,128)} %get-tuple-element.139, f32[1024,1536]{1,0:T(8,128)} %fusion.61, f32[1024,1536]{1,0:T(8,128)} %fusion.60), kind=kOutput, calls=%fused_computation.77 | convolution fusion | flops 6472335360 | bytes 33554432 | tf_op jit(solution)/shard_map/dot_general | solution.py:375
  472.6 10.8 %add_convert_fusion.1 = bf16[1024,2048]{1,0:T(8,128)(2,1)S(1)} fusion(f32[1024,2048]{1,0:T(8,128)} %fusion.21, bf16[1024,1536]{1,0:T(8,128)(2,1)S(1)} %copy-done.71, bf16[2048,1536]{1,0:T(8,128)(2,1)} %all-gather.15.cloned.1.call-done), kind=kOutput, calls=%fused_computation.1 | convolution fusion | flops 6446645248 | bytes 22020096 | tf_op jit(solution)/shard_map/dot_general | solution.py:375
  489.0 15.7 %collective-permute-done.39 = bf16[1024,512]{1,0:T(8,128)(2,1)S(1)} collective-permute-done((bf16[1024,512]{1,0:T(8,128)(2,1)S(1)}, bf16[1024,512]{1,0:T(8,128)(2,1)S(1)}, u32[]{:S(2)}, u32[]{:S(2)}) %collective-permute-start.39) | collective-permute-done | bytes 1048608 | tf_op jit(solution)/shard_map/ppermute | solution.py:64
  511.5 11.1 %convolution_convert_fusion = bf16[2048,1536]{1,0:T(8,128)(2,1)} fusion(bf16[1024,2048]{1,0:T(8,128)(2,1)} %select_dynamic-update-slice_fusion.3, bf16[1024,1536]{1,0:T(8,128)(2,1)S(1)} %copy-done.69), kind=kOutput, calls=%fused_computation.2 | convolution fusion | flops 6445596672 | bytes 13631488 | tf_op jit(solution)/shard_map/dot_general | solution.py:371
  536.1 24.6 %collective-permute-start.45 = (f32[8,128]{1,0:T(8,128)S(1)}, f32[8,128]{1,0:T(8,128)S(1)}, u32[]{:S(2)}, u32[]{:S(2)}) collective-permute-start(f32[8,128]{1,0:T(8,128)S(1)} %bitcast.210), channel_id=1, source_target_pairs={{0,1},{1,2},{2,3},{3,0},{4,5},{5,6},{6,7},{7,4},{8,9},{9,10},{10,1... | collective-permute-start | bytes 12296 | tf_op jit(solution)/shard_map/ppermute | solution.py:73
  565.4 15.1 %collective-permute-done.45 = f32[8,128]{1,0:T(8,128)S(1)} collective-permute-done((f32[8,128]{1,0:T(8,128)S(1)}, f32[8,128]{1,0:T(8,128)S(1)}, u32[]{:S(2)}, u32[]{:S(2)}) %collective-permute-start.45) | collective-permute-done | bytes 4128 | tf_op jit(solution)/shard_map/ppermute | solution.py:73
  589.0 19.7 %collective-permute-done.49 = bf16[1024,512]{1,0:T(8,128)(2,1)S(1)} collective-permute-done((bf16[1024,512]{1,0:T(8,128)(2,1)S(1)}, bf16[1024,512]{1,0:T(8,128)(2,1)S(1)}, u32[]{:S(2)}, u32[]{:S(2)}) %collective-permute-start.49) | collective-permute-done | bytes 1048608 | tf_op jit(solution)/shard_map/ppermute | solution.py:40
  624.4 12.2 %collective-permute-done.52 = bf16[1024,512]{1,0:T(8,128)(2,1)S(1)} collective-permute-done((bf16[1024,512]{1,0:T(8,128)(2,1)S(1)}, bf16[1024,512]{1,0:T(8,128)(2,1)S(1)}, u32[]{:S(2)}, u32[]{:S(2)}) %collective-permute-start.52) | collective-permute-done | bytes 1048608 | tf_op jit(solution)/shard_map/ppermute | solution.py:41
  688.1 10.1 %shard_map.349 = (f32[1024,704]{1,0:T(8,128)S(1)}, f32[1024,704]{1,0:T(8,128)}, bf16[1024,704]{1,0:T(8,128)(2,1)S(1)}, f32[8,704]{1,0:T(8,128)S(1)}, f32[8,704]{...) custom-call(f32[1024,704]{1,0:T(8,128)} %fusion.62.gated_grad, f32[1024,704]{1,0:T(8,128)} %copy-done.23, ...), custom_call_target="tpu_custom_call" | custom-call | flops 14417920 | bytes 18743296 | tf_op jit(solution)/shard_map/pallas_call | solution.py:244
  707.8 16.6 %shard_map.350 = (bf16[1024,704]{1,0:T(8,128)(2,1)S(1)}, bf16[1024,704]{1,0:T(8,128)(2,1)}, f32[1024,704]{1,0:T(8,128)}, f32[48,704]{1,0:T(8,128)S(1)}, f32[64,704]{1,0:T(8,128)S(1)}) custom-call(f32[1024,704]{1,0:T(8,128)} %copy-done.4, f32[1024,704]{1,0:T(8,128)} %get-tuple-element.47.after, f32[8,704]{1,0:T(8,128)S(1)} %multiply_add_fusion.2.enter, ...), custom_call_target="tpu_custom_call" | custom-call | flops 2030043136 | bytes 28835840 | tf_op jit(solution)/shard_map/pallas_call | solution.py:335
  741.8 17.7 %collective-permute-start.56 = (bf16[1024,512]{1,0:T(8,128)(2,1)}, bf16[1024,512]{1,0:T(8,128)(2,1)}, u32[]{:S(2)}, u32[]{:S(2)}) collective-permute-start(bf16[1024,512]{1,0:T(8,128)(2,1)} %get-tuple-element.97), channel_id=1, source_target_pairs={{0,1},{4,5},{8,9},{12,13},{16,17},{20,21},{24,25},{28,29}} | collective-permute-start | bytes 3145736 | tf_op jit(solution)/shard_map/ppermute | solution.py:64
  765.2 13.7 %collective-permute-done.56 = bf16[1024,512]{1,0:T(8,128)(2,1)} collective-permute-done((bf16[1024,512]{1,0:T(8,128)(2,1)}, bf16[1024,512]{1,0:T(8,128)(2,1)}, u32[]{:S(2)}, u32[]{:S(2)}) %collective-permute-start.56) | collective-permute-done | bytes 1048608 | tf_op jit(solution)/shard_map/ppermute | solution.py:64
  814.2 11.3 %collective-permute-start.62 = (f32[8,128]{1,0:T(8,128)S(1)}, f32[8,128]{1,0:T(8,128)S(1)}, u32[]{:S(2)}, u32[]{:S(2)}) collective-permute-start(f32[8,128]{1,0:T(8,128)S(1)} %bitcast_add_fusion.1), channel_id=1, source_target_pairs={{0,1},{1,2},{2,3},{3,0},{4,5},{5,6},{6,7},{7,4},{8,9},{9,10},{10,1... | collective-permute-start | bytes 12296 | tf_op jit(solution)/shard_map/ppermute | solution.py:73
  829.9 23.4 %all-reduce.10 = (f32[4,704]{1,0:T(4,128)}, f32[704]{0:T(1024)}, f32[704]{0:T(1024)}, f32[704]{0:T(1024)}, f32[704]{0:T(1024)}) all-reduce(f32[4,704]{1,0:T(4,128)S(1)} %slice_add_fusion, f32[704]{0:T(1024)S(1)} %get-tuple-element.66, f32[704]{0:T(1024)S(1)} %get-tuple-element.65, ...), channel_id=1, replica_groups=mesh['seq'=2,'row'=4,'rep'=4] {'seq','row'}, use_global_device_ids=true, to_apply=%region_14.15 | all-reduce | flops 5632 | bytes 45056 | tf_op jit(solution)/shard_map/psum | solution.py:517
  865.7 38.1 %psum.63 = f32[2,2048]{1,0:T(2,128)S(1)} all-reduce(f32[2,2048]{1,0:T(2,128)S(1)} %constant_dynamic-update-slice_fusion), channel_id=1, replica_groups=mesh['seq'=2,'row'=4,'rep'=4] {'seq','row','rep'}, use_global_device_ids=true, to_apply=%region_23.24 | all-reduce | flops 4096 | bytes 32768 | tf_op jit(solution)/shard_map/psum | solution.py:520
  (430 shorter events, 371.7 us)
Async XLA Ops:
  7.2 99.8 %all-gather.7.cloned.1.call-start = ((), (), s32[]{:S(2)}) async-start(), calls=%async_computation.6 | async-start | bytes 3244032 | tf_op jit(solution)/shard_map/all_gather | solution.py:400
  7.9 129.1 %all-gather.9.cloned.1.call-start = ((), (), s32[]{:S(2)}) async-start(), calls=%async_computation.7 | async-start | bytes 3244032 | tf_op jit(solution)/shard_map/all_gather | solution.py:400
  8.7 140.9 %all-gather.11.cloned.1.call-start = ((), (), s32[]{:S(2)}) async-start(), calls=%async_computation.8 | async-start | bytes 3244032 | tf_op jit(solution)/shard_map/all_gather | solution.py:400
  9.4 376.0 %all-gather.15.cloned.1.call-start = ((), (), s32[]{:S(2)}) async-start(), calls=%async_computation.10 | async-start | bytes 7077888 | tf_op jit(solution)/shard_map/all_gather | solution.py:400
  10.0 387.2 %all-gather.13.cloned.1.call-start = ((), (), s32[]{:S(2)}) async-start(), calls=%async_computation.9 | async-start | bytes 7077888 | tf_op jit(solution)/shard_map/all_gather | solution.py:400
  49.6 359.3 %all-gather.17.cloned.1.call-start = ((), (), s32[]{:S(2)}) async-start(), calls=%async_computation.11 | async-start | bytes 7077888 | tf_op jit(solution)/shard_map/all_gather | solution.py:400
  204.7 648.6 %reduce-scatter.13.cloned.1.call-start = ((), (), s32[]{:S(2)}) async-start(), calls=%async_computation.15 | async-start | bytes 7077888 | tf_op jit(solution)/shard_map/reduce_scatter | solution.py:404
  204.8 35.6 %collective-permute-start.14 = (bf16[1024,512]{1,0:T(8,128)(2,1)}, bf16[1024,512]{1,0:T(8,128)(2,1)}, u32[]{:S(2)}, u32[]{:S(2)}) collective-permute-start(bf16[1024,512]{1,0:T(8,128)(2,1)} %get-tuple-element.107), channel_id=1, source_target_pairs={{0,1},{1,2},{2,3},{4,5},{5,6},{6,7},{8,9},{9,10},{10,11},{12,13},{... | collective-permute-start | bytes 3145736 | tf_op jit(solution)/shard_map/ppermute | solution.py:64
  220.2 45.3 %collective-permute-start.34 = (bf16[1024,512]{1,0:T(8,128)(2,1)S(1)}, bf16[1024,512]{1,0:T(8,128)(2,1)}, u32[]{:S(2)}, u32[]{:S(2)}) collective-permute-start(bf16[1024,512]{1,0:T(8,128)(2,1)S(1)} %get-tuple-element.81), channel_id=1, source_target_pairs={{0,1},{1,2},{2,3},{4,5},{5,6},{6,7},{8,9},{9,10},{10,11},{12,13},{... | collective-permute-start | bytes 3145736 | tf_op jit(solution)/shard_map/ppermute | solution.py:40
  266.3 39.2 %collective-permute-start.21 = (bf16[1024,512]{1,0:T(8,128)(2,1)S(1)}, bf16[1024,512]{1,0:T(8,128)(2,1)S(1)}, u32[]{:S(2)}, u32[]{:S(2)}) collective-permute-start(bf16[1024,512]{1,0:T(8,128)(2,1)S(1)} %get-tuple-element.83), channel_id=1, source_target_pairs={{1,0},{2,1},{3,2},{5,4},{6,5},{7,6},{9,8},{10,9},{11,10},{13,12},{... | collective-permute-start | bytes 3145736 | tf_op jit(solution)/shard_map/ppermute | solution.py:41
  283.0 44.9 %collective-permute-start.37 = (bf16[1024,512]{1,0:T(8,128)(2,1)S(1)}, bf16[1024,512]{1,0:T(8,128)(2,1)S(1)}, u32[]{:S(2)}, u32[]{:S(2)}) collective-permute-start(bf16[1024,512]{1,0:T(8,128)(2,1)S(1)} %collective-permute-done.33), channel_id=1, source_target_pairs={{1,0},{2,1},{5,4},{6,5},{9,8},{10,9},{13,12},{14,13},{17,16},{18,1... | collective-permute-start | bytes 3145736 | tf_op jit(solution)/shard_map/ppermute | solution.py:41
  284.3 44.9 %collective-permute-start.23 = (bf16[1024,512]{1,0:T(8,128)(2,1)S(1)}, bf16[1024,512]{1,0:T(8,128)(2,1)S(1)}, u32[]{:S(2)}, u32[]{:S(2)}) collective-permute-start(bf16[1024,512]{1,0:T(8,128)(2,1)S(1)} %collective-permute-done.22), channel_id=1, source_target_pairs={{1,2},{2,3},{5,6},{6,7},{9,10},{10,11},{13,14},{14,15},{17,18},{18... | collective-permute-start | bytes 3145736 | tf_op jit(solution)/shard_map/ppermute | solution.py:40
  285.0 44.9 %collective-permute-start.36 = (bf16[1024,512]{1,0:T(8,128)(2,1)S(1)}, bf16[1024,512]{1,0:T(8,128)(2,1)S(1)}, u32[]{:S(2)}, u32[]{:S(2)}) collective-permute-start(bf16[1024,512]{1,0:T(8,128)(2,1)S(1)} %collective-permute-done.35), channel_id=1, source_target_pairs={{2,3},{6,7},{10,11},{14,15},{18,19},{22,23},{26,27},{30,31}} | collective-permute-start | bytes 3145736 | tf_op jit(solution)/shard_map/ppermute | solution.py:40
  305.4 44.9 %collective-permute-start.25 = (bf16[1024,512]{1,0:T(8,128)(2,1)S(1)}, bf16[1024,512]{1,0:T(8,128)(2,1)S(1)}, u32[]{:S(2)}, u32[]{:S(2)}) collective-permute-start(bf16[1024,512]{1,0:T(8,128)(2,1)S(1)} %collective-permute-done.21), channel_id=1, source_target_pairs={{1,0},{2,1},{5,4},{6,5},{9,8},{10,9},{13,12},{14,13},{17,16},{18,1... | collective-permute-start | bytes 3145736 | tf_op jit(solution)/shard_map/ppermute | solution.py:41
  327.9 44.9 %collective-permute-start.38 = (bf16[1024,512]{1,0:T(8,128)(2,1)S(1)}, bf16[1024,512]{1,0:T(8,128)(2,1)S(1)}, u32[]{:S(2)}, u32[]{:S(2)}) collective-permute-start(bf16[1024,512]{1,0:T(8,128)(2,1)S(1)} %collective-permute-done.37), channel_id=1, source_target_pairs={{1,0},{5,4},{9,8},{13,12},{17,16},{21,20},{25,24},{29,28}} | collective-permute-start | bytes 3145736 | tf_op jit(solution)/shard_map/ppermute | solution.py:41
  329.2 45.0 %collective-permute-start.24 = (bf16[1024,512]{1,0:T(8,128)(2,1)S(1)}, bf16[1024,512]{1,0:T(8,128)(2,1)S(1)}, u32[]{:S(2)}, u32[]{:S(2)}) collective-permute-start(bf16[1024,512]{1,0:T(8,128)(2,1)S(1)} %collective-permute-done.23), channel_id=1, source_target_pairs={{2,3},{6,7},{10,11},{14,15},{18,19},{22,23},{26,27},{30,31}} | collective-permute-start | bytes 3145736 | tf_op jit(solution)/shard_map/ppermute | solution.py:40
  441.5 414.5 %reduce-scatter.15.cloned.1.call-start = ((), (), s32[]{:S(2)}) async-start(), calls=%async_computation.16 | async-start | bytes 7077888 | tf_op jit(solution)/shard_map/reduce_scatter | solution.py:404
  453.0 405.4 %reduce-scatter.17.cloned.1.call-start = ((), (), s32[]{:S(2)}) async-start(), calls=%async_computation.17 | async-start | bytes 7077888 | tf_op jit(solution)/shard_map/reduce_scatter | solution.py:404
  487.4 35.3 %collective-permute-start.42 = (bf16[1024,512]{1,0:T(8,128)(2,1)}, bf16[1024,512]{1,0:T(8,128)(2,1)}, u32[]{:S(2)}, u32[]{:S(2)}) collective-permute-start(bf16[1024,512]{1,0:T(8,128)(2,1)} %get-tuple-element.102), channel_id=1, source_target_pairs={{3,2},{7,6},{11,10},{15,14},{19,18},{23,22},{27,26},{31,30}} | collective-permute-start | bytes 3145736 | tf_op jit(solution)/shard_map/ppermute | solution.py:65
  522.6 381.9 %reduce-scatter.11.cloned.1.call-start = ((), (), s32[]{:S(2)}) async-start(), calls=%async_computation.14 | async-start | bytes 3244032 | tf_op jit(solution)/shard_map/reduce_scatter | solution.py:404
  529.3 52.6 %collective-permute-start.41 = (bf16[1024,512]{1,0:T(8,128)(2,1)S(1)}, bf16[1024,512]{1,0:T(8,128)(2,1)S(1)}, u32[]{:S(2)}, u32[]{:S(2)}) collective-permute-start(bf16[1024,512]{1,0:T(8,128)(2,1)S(1)} %get-tuple-element.99), channel_id=1, source_target_pairs={{0,1},{1,2},{2,3},{4,5},{5,6},{6,7},{8,9},{9,10},{10,11},{12,13},{... | collective-permute-start | bytes 3145736 | tf_op jit(solution)/shard_map/ppermute | solution.py:64
  534.8 47.1 %collective-permute-start.44 = (bf16[1024,512]{1,0:T(8,128)(2,1)S(1)}, bf16[1024,512]{1,0:T(8,128)(2,1)S(1)}, u32[]{:S(2)}, u32[]{:S(2)}) collective-permute-start(bf16[1024,512]{1,0:T(8,128)(2,1)S(1)} %add_convert_fusion.7), channel_id=1, source_target_pairs={{1,0},{2,1},{3,2},{5,4},{6,5},{7,6},{9,8},{10,9},{11,10},{13,12},{... | collective-permute-start | bytes 3145736 | tf_op jit(solution)/shard_map/ppermute | solution.py:65
  536.1 44.4 %collective-permute-start.45 = (f32[8,128]{1,0:T(8,128)S(1)}, f32[8,128]{1,0:T(8,128)S(1)}, u32[]{:S(2)}, u32[]{:S(2)}) collective-permute-start(f32[8,128]{1,0:T(8,128)S(1)} %bitcast.210), channel_id=1, source_target_pairs={{0,1},{1,2},{2,3},{3,0},{4,5},{5,6},{6,7},{7,4},{8,9},{9,10},{10,1... | collective-permute-start | bytes 12296 | tf_op jit(solution)/shard_map/ppermute | solution.py:73
  660.3 246.0 %reduce-scatter.9.cloned.1.call-start = ((), (), s32[]{:S(2)}) async-start(), calls=%async_computation.13 | async-start | bytes 3244032 | tf_op jit(solution)/shard_map/reduce_scatter | solution.py:404
  672.9 112.7 %collective-permute-start.29 = (bf16[1024,512]{1,0:T(8,128)(2,1)}, bf16[1024,512]{1,0:T(8,128)(2,1)}, u32[]{:S(2)}, u32[]{:S(2)}) collective-permute-start(bf16[1024,512]{1,0:T(8,128)(2,1)} %get-tuple-element.103), channel_id=1, source_target_pairs={{0,1},{1,2},{2,3},{4,5},{5,6},{6,7},{8,9},{9,10},{10,11},{12,13},{... | collective-permute-start | bytes 3145736 | tf_op jit(solution)/shard_map/ppermute | solution.py:64
  681.5 104.1 %collective-permute-start.32 = (bf16[1024,512]{1,0:T(8,128)(2,1)}, bf16[1024,512]{1,0:T(8,128)(2,1)}, u32[]{:S(2)}, u32[]{:S(2)}) collective-permute-start(bf16[1024,512]{1,0:T(8,128)(2,1)} %add_convert_fusion.12), channel_id=1, source_target_pairs={{1,0},{2,1},{3,2},{5,4},{6,5},{7,6},{9,8},{10,9},{11,10},{13,12},{... | collective-permute-start | bytes 3145736 | tf_op jit(solution)/shard_map/ppermute | solution.py:65
  706.6 201.6 %reduce-scatter.7.cloned.1.call-start = ((), (), s32[]{:S(2)}) async-start(), calls=%async_computation.12 | async-start | bytes 3244032 | tf_op jit(solution)/shard_map/reduce_scatter | solution.py:404
  741.8 37.1 %collective-permute-start.56 = (bf16[1024,512]{1,0:T(8,128)(2,1)}, bf16[1024,512]{1,0:T(8,128)(2,1)}, u32[]{:S(2)}, u32[]{:S(2)}) collective-permute-start(bf16[1024,512]{1,0:T(8,128)(2,1)} %get-tuple-element.97), channel_id=1, source_target_pairs={{0,1},{4,5},{8,9},{12,13},{16,17},{20,21},{24,25},{28,29}} | collective-permute-start | bytes 3145736 | tf_op jit(solution)/shard_map/ppermute | solution.py:64
  764.3 145.9 %all-reduce.14.cloned.1.call-start = ((), (), s32[]{:S(2)}) async-start(), calls=%async_computation.18 | async-start | bytes 2883584 | tf_op jit(solution)/shard_map/psum | solution.py:517
  803.1 58.0 %collective-permute-start.58 = (bf16[1024,512]{1,0:T(8,128)(2,1)}, bf16[1024,512]{1,0:T(8,128)(2,1)S(1)}, u32[]{:S(2)}, u32[]{:S(2)}) collective-permute-start(bf16[1024,512]{1,0:T(8,128)(2,1)} %get-tuple-element.95), channel_id=1, source_target_pairs={{0,1},{1,2},{2,3},{4,5},{5,6},{6,7},{8,9},{9,10},{10,11},{12,13},{... | collective-permute-start | bytes 3145736 | tf_op jit(solution)/shard_map/ppermute | solution.py:64
  809.6 51.5 %collective-permute-start.61 = (bf16[1024,512]{1,0:T(8,128)(2,1)}, bf16[1024,512]{1,0:T(8,128)(2,1)}, u32[]{:S(2)}, u32[]{:S(2)}) collective-permute-start(bf16[1024,512]{1,0:T(8,128)(2,1)} %add_convert_fusion.3), channel_id=1, source_target_pairs={{1,0},{2,1},{3,2},{5,4},{6,5},{7,6},{9,8},{10,9},{11,10},{13,12},{... | collective-permute-start | bytes 3145736 | tf_op jit(solution)/shard_map/ppermute | solution.py:65
  814.2 39.1 %collective-permute-start.62 = (f32[8,128]{1,0:T(8,128)S(1)}, f32[8,128]{1,0:T(8,128)S(1)}, u32[]{:S(2)}, u32[]{:S(2)}) collective-permute-start(f32[8,128]{1,0:T(8,128)S(1)} %bitcast_add_fusion.1), channel_id=1, source_target_pairs={{0,1},{1,2},{2,3},{3,0},{4,5},{5,6},{6,7},{7,4},{8,9},{9,10},{10,1... | collective-permute-start | bytes 12296 | tf_op jit(solution)/shard_map/ppermute | solution.py:73
  (120 other events, 1920.0 us)
Sparse Core Ops, SparseCore 0:
  9.9 34.3 all-gather.6
  46.2 31.6 all-gather.8
  79.8 31.6 all-gather.10
  113.2 45.5 all-gather.14
  160.5 45.5 all-gather.12
  207.8 45.5 all-gather.16
  441.6 60.5 reduce-scatter.12
  506.0 61.7 reduce-scatter.14
  571.1 61.7 reduce-scatter.16
  660.4 40.7 reduce-scatter.10
  706.7 60.2 reduce-scatter.8
  770.7 44.8 reduce-scatter.6
  819.4 60.0 all-reduce.13

commit v2 on v1

--- a/solution.py
+++ b/solution.py
@@ -1,3 +1,5 @@
+from functools import partial as partial_call
+
 import jax
 import jax.numpy as jnp
 from jax import lax
@@ -29,41 +31,48 @@
     return jnp.where(y < 0.4, series, 1.0 - jnp.exp(-y))
 
 
-def gather_line(own, axis):
+after = lax.optimization_barrier
+
+
+def pass_on(held, k, axis):
+    count = lax.axis_size(axis)
+    right = lax.ppermute(held[0], axis, [(i, i + 1) for i in range(k - 1, count - 1)])
+    left = lax.ppermute(held[1], axis, [(i, i - 1) for i in range(1, count - k + 1)])
+    return right, left
+
+
+def put_together(passed, axis):
     count, me = lax.axis_size(axis), lax.axis_index(axis)
+    own = passed[0][0]
     width = own.shape[1]
     total = jnp.zeros((own.shape[0], count * width), own.dtype)
     total = lax.dynamic_update_slice(total, own, (0, me * width))
-    right, left = own, own
-    held = {}
-    for k in range(1, count):
-        right = lax.ppermute(right, axis, [(i, i + 1) for i in range(k - 1, count - 1)])
-        left = lax.ppermute(left, axis, [(i, i - 1) for i in range(1, count - k + 1)])
-        held[-k], held[k] = right, left
     for k in range(1, count):
         there = me + k
-        piece = jnp.where(there < count, held[k], held[k - count])
+        piece = jnp.where(there < count, passed[k][1], passed[count - k][0])
         total = lax.dynamic_update_slice(total, piece, (0, lax.rem(there, count) * width))
     return total
 
 
-def reduce_line(whole, axis):
+def line_part(whole, target, axis):
+    count = lax.axis_size(axis)
+    width = whole.shape[1] // count
+    return lax.dynamic_slice_in_dim(whole, jnp.clip(target, 0, count - 1) * width, width, 1).astype(F32)
+
+
+def reduce_step(whole, held, k, axis):
     count, me = lax.axis_size(axis), lax.axis_index(axis)
-    width = whole.shape[1] // count
-
-    def part(target):
-        target = jnp.clip(target, 0, count - 1)
-        return lax.dynamic_slice_in_dim(whole, target * width, width, 1).astype(F32)
-
-    right = left = None
-    for k in range(1, count):
-        far = count - k
-        to_right, to_left = part(me + far), part(me - far)
-        if k > 1:
-            to_right, to_left = to_right + right, to_left + left
-        right = lax.ppermute(to_right.astype(BF), axis, [(i, i + 1) for i in range(k)]).astype(F32)
-        left = lax.ppermute(to_left.astype(BF), axis, [(i, i - 1) for i in range(far, count)]).astype(F32)
-    return part(me) + right + left
+    far = count - k
+    right, left = line_part(whole, me + far, axis), line_part(whole, me - far, axis)
+    if held is not None:
+        right, left = right + held[0].astype(F32), left + held[1].astype(F32)
+    right = lax.ppermute(right.astype(BF), axis, [(i, i + 1) for i in range(k)])
+    left = lax.ppermute(left.astype(BF), axis, [(i, i - 1) for i in range(far, count)])
+    return right, left
+
+
+def reduce_end(whole, held, axis):
+    return line_part(whole, lax.axis_index(axis), axis) + held[0].astype(F32) + held[1].astype(F32)
 
 
 def small_sum(own, axis):
@@ -74,9 +83,30 @@
     return total
 
 
-def row_sum(values, axis):
-    sums = jnp.sum(values, axis=1)
-    return small_sum(sums.reshape(8, -1), axis).reshape(-1, 1)
+def small_gather(own, axis):
+    count, me = lax.axis_size(axis), lax.axis_index(axis)
+    width = own.shape[1]
+    total = lax.dynamic_update_slice(jnp.zeros((own.shape[0], count * width), own.dtype), own, (0, me * width))
+    for k in range(1, count):
+        piece = lax.ppermute(own, axis, [(i, (i + k) % count) for i in range(count)])
+        total = lax.dynamic_update_slice(total, piece, (0, lax.rem(me - k + count, count) * width))
+    return total
+
+
+def sum_small(parts, axes):
+    width = 256
+    padded = []
+    for part in parts:
+        columns = -part.shape[1] % width
+        padded.append(jnp.pad(part, ((0, 0), (0, columns))).reshape(-1, width))
+    counts = [p.shape[0] for p in padded]
+    joined = jnp.concatenate(padded + [jnp.zeros((-sum(counts) % 16, width), F32)], axis=0).astype(BF)
+    joined = jnp.sum(lax.all_gather(joined, axes).astype(F32), axis=0)
+    out, start = [], 0
+    for part, rows in zip(parts, counts):
+        out.append(joined[start : start + rows].reshape(part.shape[0], -1)[:, : part.shape[1]])
+        start += rows
+    return out
 
 
 def by_step(values):
@@ -89,15 +119,16 @@
     return values.reshape(length // SEGS, SEGS, width).transpose(1, 0, 2).reshape(length, width)
 
 
-def block_diagonal(blocks):
+def block_diagonal(blocks, width):
     heads, wide = blocks.shape[0], blocks.shape[1]
-    rows = [jnp.pad(blocks[h], ((0, 0), (h * wide, (heads - 1 - h) * wide))) for h in range(heads)]
+    rows = [jnp.pad(blocks[h], ((0, 0), (h * wide, width - (h + 1) * wide))) for h in range(heads)]
+    rows.append(jnp.zeros((width - heads * wide, width), blocks.dtype))
     return jnp.concatenate(rows, axis=0)
 
 
-def diagonal_blocks(dense, heads):
-    wide = dense.shape[0] // heads
-    return jnp.stack([dense[h * wide : (h + 1) * wide, h * wide : (h + 1) * wide] for h in range(heads)])
+def diagonal_rows(dense, heads, wide):
+    blocks = [dense[h * wide : (h + 1) * wide, h * wide : (h + 1) * wide] for h in range(heads)]
+    return jnp.concatenate(blocks, axis=0)
 
 
 def forward_kernel(
@@ -114,7 +145,7 @@
         prod_now[...] = jnp.ones_like(prod_now)
         state_now[...] = jnp.zeros_like(state_now)
 
-    now = conv_in[...].astype(F32)
+    now = conv_in[...].astype(BF).astype(F32)
     ext = jnp.concatenate([last_rows[...], now], axis=0)
     same_all = same[...]
     total = params[4:5, :] + params[0:1, :] * now
@@ -157,7 +188,7 @@
 
 
 def recur_forward(conv_in, same, prefix, params, decay_w, input_w, rows=128):
-    length, width = conv_in.shape
+    length, width = conv_in.shape[0], params.shape[1]
     block = pl.BlockSpec((rows, width), lambda i: (i, 0))
     fixed = lambda shape: pl.BlockSpec(shape, lambda i: (0, 0))
     big = jax.ShapeDtypeStruct((length, width), F32)
@@ -182,9 +213,7 @@
             pltpu.VMEM((rows, width), F32),
         ],
         compiler_params=pltpu.CompilerParams(vmem_limit_bytes=LIMIT),
-        cost_estimate=pl.CostEstimate(
-            flops=4 * length * width * width, bytes_accessed=26 * length * width, transcendentals=5 * length * width
-        ),
+        cost_estimate=pl.CostEstimate(flops=length * width, bytes_accessed=4 * length * width, transcendentals=0),
     )(conv_in, same, prefix, params, decay_w, input_w)
 
 
@@ -238,22 +267,21 @@
     length, width = gated_grad.shape
     last = length // rows - 1
     block = pl.BlockSpec((rows, width), lambda i: (last - i, 0))
+    second = pl.BlockSpec((rows, width), lambda i: (last - i, 1))
     fixed = lambda shape: pl.BlockSpec(shape, lambda i: (0, 0))
     big = jax.ShapeDtypeStruct((length, width), F32)
     small = jax.ShapeDtypeStruct((SEGS, width), F32)
     return pl.pallas_call(
         adjoint_kernel,
         grid=(length // rows,),
-        in_specs=[block] * 4,
+        in_specs=[block, second, block, block],
         out_specs=[block] * 3 + [fixed((SEGS, width))] * 3 + [pl.BlockSpec((rows, 128), lambda i: (last - i, 0))],
         out_shape=[big, big, jax.ShapeDtypeStruct((length, width), BF)]
         + [small] * 3
         + [jax.ShapeDtypeStruct((length, 128), F32)],
         scratch_shapes=[pltpu.VMEM((SEGS, width), F32)] * 3 + [pltpu.VMEM((rows, width), F32)],
         compiler_params=pltpu.CompilerParams(vmem_limit_bytes=LIMIT),
-        cost_estimate=pl.CostEstimate(
-            flops=20 * length * width, bytes_accessed=26 * length * width, transcendentals=length * width
-        ),
+        cost_estimate=pl.CostEstimate(flops=length * width, bytes_accessed=4 * length * width, transcendentals=0),
     )(gated_grad, gate_branch, hidden, retain)
 
 
@@ -300,7 +328,7 @@
         + lax.dot_general(input_grad, input_w[...], dims, preferred_element_type=F32)
     )
     same_all = same[...]
-    now = conv_in[...].astype(F32)
+    now = conv_in[...].astype(BF).astype(F32)
     low = params[0:1, :] * conv_grad
     out_sums[0:8, :] += sums(conv_grad * now)
     for k, held in ((1, next_one), (2, next_two), (3, next_three)):
@@ -354,13 +382,296 @@
             pltpu.VMEM((24, width), F32),
         ],
         compiler_params=pltpu.CompilerParams(vmem_limit_bytes=LIMIT),
-        cost_estimate=pl.CostEstimate(
-            flops=4 * length * width * width, bytes_accessed=40 * length * width, transcendentals=5 * length * width
-        ),
+        cost_estimate=pl.CostEstimate(flops=length * width, bytes_accessed=4 * length * width, transcendentals=0),
     )(
         local, after, enter, hidden, hidden, carry, conv_out, decay_sig, gate_sig, retain, same, params, conv_in,
         decay_w, input_w,
     )
+
+
+def exchange_kernel(count, chunks, mode, *refs):
+    backward, summing = mode == "back", mode != "first"
+    if backward:
+        (partial, residual, middle, scale, mean, gain, out, out_own, out_gain) = refs[:9]
+        gathered = out
+        rest = refs[9:]
+    elif summing:
+        (partial, residual, gain, out, out_scale, out_own, gathered) = refs[:7]
+        rest = refs[7:]
+    else:
+        (residual, gain, out, out_scale, gathered) = refs[:5]
+        rest = refs[5:]
+    if summing:
+        right, left, total, sum_send, sum_recv, all_send, all_recv = rest
+    else:
+        all_send, all_recv = rest
+    me = lax.axis_index("rep")
+    length, width = residual.shape
+    rows = length // chunks
+    last = count - 1
+
+    barrier = pltpu.get_barrier_semaphore()
+
+    @pl.when(me > 0)
+    def _():
+        pl.semaphore_signal(barrier, inc=1, device_id={"rep": me - 1}, device_id_type=pl.DeviceIdType.MESH)
+
+    @pl.when(me < last)
+    def _():
+        pl.semaphore_signal(barrier, inc=1, device_id={"rep": me + 1}, device_id_type=pl.DeviceIdType.MESH)
+
+    inner = jnp.logical_and(me > 0, me < last)
+
+    @pl.when(inner)
+    def _():
+        pl.semaphore_wait(barrier, 2)
+
+    @pl.when(jnp.logical_not(inner))
+    def _():
+        pl.semaphore_wait(barrier, 1)
+
+    if backward:
+        out_gain[...] = jnp.zeros_like(out_gain)
+
+    def at(c):
+        return pl.ds(pl.multiple_of(c * rows, rows), rows)
+
+    def columns(device):
+        return pl.ds(pl.multiple_of(device * width, width), width)
+
+    def sum_copy(side, slot, c):
+        buffer, to = ((right, me + 1), (left, me - 1))[side]
+        return pltpu.make_async_remote_copy(
+            src_ref=buffer.at[slot, at(c)],
+            dst_ref=buffer.at[slot - 1, at(c)],
+            send_sem=sum_send.at[side, slot, c],
+            recv_sem=sum_recv.at[side, slot - 1, c],
+            device_id={"rep": to},
+            device_id_type=pl.DeviceIdType.MESH,
+        )
+
+    def sum_arrived(side, slot, c):
+        buffer, sender = ((right, me - 1), (left, me + 1))[side]
+        pltpu.make_async_remote_copy(
+            src_ref=buffer.at[slot, at(c)],
+            dst_ref=buffer.at[slot, at(c)],
+            send_sem=sum_send.at[side, slot, c],
+            recv_sem=sum_recv.at[side, slot, c],
+            device_id={"rep": sender},
+            device_id_type=pl.DeviceIdType.MESH,
+        ).wait_recv()
+
+    def all_copy(side, far, c):
+        source, to = ((me - far, me + 1), (me + far, me - 1))[side]
+        piece = gathered.at[at(c), columns(source)]
+        return pltpu.make_async_remote_copy(
+            src_ref=piece,
+            dst_ref=piece,
+            send_sem=all_send.at[side, far, c],
+            recv_sem=all_recv.at[side, far + 1, c],
+            device_id={"rep": to},
+            device_id_type=pl.DeviceIdType.MESH,
+        )
+
+    def all_arrived(side, far, c):
+        source, sender = ((me - far, me - 1), (me + far, me + 1))[side]
+        piece = gathered.at[at(c), columns(source)]
+        pltpu.make_async_remote_copy(
+            src_ref=piece,
+            dst_ref=piece,
+            send_sem=all_send.at[side, far, c],
+            recv_sem=all_recv.at[side, far, c],
+            device_id={"rep": sender},
+            device_id_type=pl.DeviceIdType.MESH,
+        ).wait_recv()
+
+    def inside(c):
+        return jnp.logical_and(c >= 0, c < chunks)
+
+    def tick(now, _):
+        for side in (0, 1) if summing else ():
+            place = (me, last - me)[side]
+            c = now - place
+            for slot in range(last, 0, -1):
+
+                @pl.when(jnp.logical_and(inside(c), place + slot <= last))
+                def _(side=side, place=place, c=c, slot=slot):
+                    buffer = (right, left)[side]
+                    target = (me + slot, me - slot)[side]
+
+                    @pl.when(place > 0)
+                    def _():
+                        sum_arrived(side, slot, c)
+                        added = buffer[slot, at(c), :].astype(F32) + partial[at(c), columns(target)].astype(F32)
+                        buffer[slot, at(c), :] = added.astype(BF)
+
+                    @pl.when(place == 0)
+                    def _():
+                        buffer[slot, at(c), :] = partial[at(c), columns(target)]
+
+                    sum_copy(side, slot, c).start()
+
+        def finish(done):
+            total[...] = partial[at(done), columns(me)].astype(F32)
+
+            @pl.when(me > 0)
+            def _():
+                sum_arrived(0, 0, done)
+                total[...] += right[0, at(done), :].astype(F32)
+
+            @pl.when(me < last)
+            def _():
+                sum_arrived(1, 0, done)
+                total[...] += left[0, at(done), :].astype(F32)
+
+            if backward:
+                size = scale[at(done), 0:1]
+                normal = middle[at(done), :] * size
+                summed = total[...]
+                own = residual[at(done), :].astype(F32) + size * (
+                    summed * gain[...] - normal * mean[at(done), 0:1]
+                )
+                out_gain[...] += jnp.sum((summed * normal).reshape(rows // 8, 8, width), axis=0)
+            else:
+                own = residual[at(done), :].astype(F32) + total[...]
+            out_own[at(done), :] = own
+            gathered[at(done), columns(me)] = own.astype(BF)
+
+        done = now - last if summing else now
+
+        @pl.when(inside(done))
+        def _():
+            if summing:
+                finish(done)
+            else:
+                gathered[at(done), columns(me)] = residual[at(done), :]
+
+            @pl.when(me < last)
+            def _():
+                all_copy(0, 0, done).start()
+
+            @pl.when(me > 0)
+            def _():
+                all_copy(1, 0, done).start()
+
+        for far in range(1, count):
+            c = done - far
+            for side in (0, 1):
+                place = (me, last - me)[side]
+
+                @pl.when(jnp.logical_and(inside(c), place >= far))
+                def _(side=side, place=place, c=c, far=far):
+                    all_arrived(side, far, c)
+
+                    @pl.when(place < last)
+                    def _():
+                        all_copy(side, far, c).start()
+
+        if not backward:
+            full = done - last
+
+            @pl.when(inside(full))
+            def _():
+                values = gathered[at(full), :].astype(F32)
+                size = lax.rsqrt(jnp.mean(values * values, axis=1, keepdims=True) + eps)
+                out[at(full), :] = (values * size * gain[...]).astype(BF)
+                out_scale[at(full), :] = jnp.broadcast_to(size, (rows, 128))
+
+        return 0
+
+    lax.fori_loop(0, chunks + (2 * last if summing else last), tick, 0)
+
+    def settle(c, _):
+        for side in (0, 1):
+            place = (me, last - me)[side]
+            for slot in range(1, count) if summing else ():
+
+                @pl.when(place + slot <= last)
+                def _(side=side, slot=slot):
+                    sum_copy(side, slot, c).wait_send()
+
+            for far in range(0, last):
+
+                @pl.when(jnp.logical_and(place < last, place >= far))
+                def _(side=side, far=far):
+                    all_copy(side, far, c).wait_send()
+
+        return 0
+
+    lax.fori_loop(0, chunks, settle, 0)
+
+
+def exchange(mode, operands, width, chunks=16):
+    count = lax.axis_size("rep")
+    length = operands[0].shape[0]
+    features = count * width
+    backward, summing = mode == "back", mode != "first"
+    vmem = pl.BlockSpec(memory_space=pltpu.VMEM)
+    scratch = [pltpu.SemaphoreType.DMA((2, count, chunks)), pltpu.SemaphoreType.DMA((2, count, chunks))]
+    out_shape = [jax.ShapeDtypeStruct((length, features), BF)]
+    if summing:
+        scratch = [
+            pltpu.VMEM((count, length, width), BF),
+            pltpu.VMEM((count, length, width), BF),
+            pltpu.VMEM((length // chunks, width), F32),
+        ] + scratch * 2
+    if not backward:
+        out_shape.append(jax.ShapeDtypeStruct((length, 128), F32))
+        scratch = [pltpu.VMEM((length, features), BF)] + scratch
+    if summing:
+        out_shape.append(jax.ShapeDtypeStruct((length, width), F32))
+    if backward:
+        out_shape.append(jax.ShapeDtypeStruct((8, width), F32))
+    return pl.pallas_call(
+        partial_call(exchange_kernel, count, chunks, mode),
+        in_specs=[vmem] * len(operands),
+        out_specs=[vmem] * len(out_shape),
+        out_shape=out_shape,
+        scratch_shapes=scratch,
+        compiler_params=pltpu.CompilerParams(
+            collective_id=("first", "norm", "back").index(mode), has_side_effects=True, vmem_limit_bytes=LIMIT
+        ),
+        cost_estimate=pl.CostEstimate(
+            flops=10 * length * features, bytes_accessed=160 * length * features, transcendentals=0
+        ),
+    )(*operands)
+
+
+def feed_kernel(cot, pre_gate, pre_up, down, out_low, out_grads, out_dot):
+    half = out_low.shape[1]
+    upstream = jnp.dot(cot[...], down[...], preferred_element_type=F32)
+    gate_pre, up_pre = pre_gate[...], pre_up[...]
+    value, slope = gelu_both(gate_pre)
+    out_low[...] = (value * up_pre).astype(BF)
+    gate_grad, up_grad = upstream * up_pre * slope, upstream * value
+    out_grads[:, :half] = gate_grad.astype(BF)
+    out_grads[:, half:] = up_grad.astype(BF)
+    dots = jnp.sum(gate_grad * gate_pre + up_grad * up_pre, axis=1, keepdims=True)
+    out_dot[...] = jnp.broadcast_to(dots, out_dot.shape)
+
+
+def feed_backward(cot, pre, down, rows=256):
+    length, features = cot.shape
+    half = down.shape[1]
+    block = lambda width, column=0: pl.BlockSpec((rows, width), lambda i: (i, column))
+    return pl.pallas_call(
+        feed_kernel,
+        grid=(length // rows,),
+        in_specs=[
+            block(features), block(half), block(half, 1),
+            pl.BlockSpec((features, half), lambda i: (0, 0), pipeline_mode=pl.Buffered(1)),
+        ],
+        out_specs=[block(half), block(2 * half), block(128)],
+        out_shape=[
+            jax.ShapeDtypeStruct((length, half), BF),
+            jax.ShapeDtypeStruct((length, 2 * half), BF),
+            jax.ShapeDtypeStruct((length, 128), F32),
+        ],
+        compiler_params=pltpu.CompilerParams(vmem_limit_bytes=LIMIT),
+        cost_estimate=pl.CostEstimate(
+            flops=2 * length * features * half, bytes_accessed=40 * length * half, transcendentals=length * half
+        ),
+    )(cot, pre, pre, down)
 
 
 def per_segment(small, length):
@@ -389,7 +700,7 @@
     length = segment_ids.shape[1]
     taps = conv_kernel.shape[0]
     edge = taps - 1
-    heads = decay_gate.shape[0]
+    heads, head_width = decay_gate.shape[0], decay_gate.shape[2]
     rep = lax.axis_index("rep")
     seq, seqs = lax.axis_index("seq"), lax.axis_size("seq")
     at_start = seq == 0
@@ -400,19 +711,29 @@
         return lax.all_gather(shard, ("seq", "row"), axis=0, tiled=True)
 
     def spread(partial_grad):
-        low = partial_grad.astype(BF)
-        return lax.psum_scatter(low, ("seq", "row"), scatter_dimension=0, tiled=True).astype(F32)
+        return lax.psum_scatter(partial_grad, ("seq", "row"), scatter_dimension=0, tiled=True)
 
     def own_part(vector):
         return lax.dynamic_slice_in_dim(vector, rep * own_width, own_width, 0)[None]
 
-    x_own = by_step(block_input[0]).astype(F32)
+    channels = conv_bias.shape[0]
+    spare = -channels % 128
+
+    def wide(values, fill=0):
+        return jnp.pad(values, ((0, 0),) * (values.ndim - 1) + ((0, spare),), constant_values=fill)
+
+    width = channels + spare
+
+    x_low = by_step(block_input[0])
+    x_own = x_low.astype(F32)
     cot_own = by_step(cotangent[0] * pad_mask[0][:, None].astype(BF))
     mixer_own, feed_own = own_part(mixer_gain), own_part(feed_gain)
-    s1 = lax.rsqrt(row_sum(x_own * x_own, "rep") / features + eps)
-    normed = gather_line((x_own * s1 * mixer_own).astype(BF), "rep")
-    w_input, w_gate, w_output = weights(recur_input), weights(recur_gate), weights(recur_output)
-    w_feed_gate, w_feed_up, w_down = weights(feed_gate), weights(feed_up), weights(feed_down)
+    normed, s1 = exchange("first", (x_low, mixer_gain[None]), own_width)
+    s1 = s1[:, :1]
+    w_recur = weights(jnp.concatenate([wide(recur_input), wide(recur_gate), wide(recur_output)], axis=1))
+    w_feed = weights(jnp.concatenate([feed_gate, feed_up], axis=1))
+    w_down = weights(feed_down)
+    w_input, w_output = w_recur[:, : 2 * width], w_recur[:, 2 * width :]
 
     left_ids = lax.ppermute(segment_ids[:, -edge:].astype(F32), "seq", to_next).astype(jnp.int32)
     left_ids = jnp.where(at_start, jnp.broadcast_to(segment_ids[:, :1], left_ids.shape), left_ids)
@@ -421,19 +742,21 @@
     same = by_step(jnp.stack(same + [same[0]] * (8 - taps), axis=1))
 
     rate = 8.0 * jax.nn.softplus(decay_logit)
-    params = jnp.concatenate([conv_kernel, jnp.stack([conv_bias, decay_bias, input_bias, rate])], axis=0)
-    decay_w, input_w = block_diagonal(decay_gate), block_diagonal(input_gate)
-
-    conv_in = dot(normed, w_input).astype(BF)
-    gate_branch = dot(normed, w_gate)
-    ends = conv_in.reshape(length // SEGS, SEGS, -1)[-edge:]
+    params = wide(jnp.concatenate([conv_kernel, jnp.stack([conv_bias, decay_bias, input_bias])], axis=0))
+    params = jnp.concatenate([params, wide(rate[None], 1)], axis=0)
+    decay_w, input_w = block_diagonal(decay_gate, width), block_diagonal(input_gate, width)
+    state_init = wide(state_init)
+
+    projected = dot(normed, w_input)
+    gate_branch = projected[:, width:]
+    ends = projected[-edge * SEGS :, :width].astype(BF).reshape(edge, SEGS, width)
     left = lax.ppermute(ends[:, -1], "seq", to_next)
-    left = jnp.where(at_start, window_init[0], left)
+    left = jnp.where(at_start, wide(window_init[0]), left)
     prefix = jnp.concatenate([left[:, None], ends[:, :-1]], axis=1).reshape(edge * SEGS, -1)
-    block_windows = ends[:, -1]
+    block_windows = ends[:, -1, :channels]
 
     conv_out, decay_sig, gate_sig, retain, products, states, pre_a, pre_b, total = recur_forward(
-        conv_in, same, prefix, params, decay_w, input_w
+        projected, same, prefix, params, decay_w, input_w
     )
     state_in = state_init
     for k in range(1, seqs):
@@ -441,87 +764,124 @@
         state_in = jnp.where(seq == k, arriving, state_in)
     block_states = total[0:1] * state_in + total[1:2]
     carry = pre_a * state_in + pre_b
+
+    cot_own, normed = after((cot_own, normed))
+    cot_pass = [(cot_own, cot_own)]
+    cot_pass.append(pass_on(cot_pass[-1], 1, "rep"))
+    states, cot_pass[-1] = after((states, cot_pass[-1]))
+    cot_pass.append(pass_on(cot_pass[-1], 2, "rep"))
+
     hidden = states + products * per_segment(carry, length)
     gated = (hidden * gelu(gate_branch)).astype(BF)
-
-    middle = x_own + reduce_line(back_dot(gated, w_output).astype(BF), "rep")
-    s2 = lax.rsqrt(row_sum(middle * middle, "rep") / features + eps)
-    normed_mid = gather_line((middle * s2 * feed_own).astype(BF), "rep")
-    cot = gather_line(cot_own, "rep")
-    gate_pre, up_pre = dot(normed_mid, w_feed_gate), dot(normed_mid, w_feed_up)
-    grad_feed = dot(cot, w_down)
-    value, slope = gelu_both(gate_pre)
-    feed_low = (value * up_pre).astype(BF)
-    gate_grad_f, up_grad_f = grad_feed * up_pre * slope, grad_feed * value
-    gate_grad, up_grad = gate_grad_f.astype(BF), up_grad_f.astype(BF)
-    mid_mean = row_sum(gate_grad_f * gate_pre + up_grad_f * up_pre, "rep") / features
-
-    mid_grad = reduce_line((back_dot(gate_grad, w_feed_gate) + back_dot(up_grad, w_feed_up)).astype(BF), "rep")
-    xh2 = middle * s2
-    feed_gain_own = jnp.sum(mid_grad * xh2, axis=0)
-    middle_grad = cot_own.astype(F32) + s2 * (mid_grad * feed_own - xh2 * mid_mean)
-    middle_low = gather_line(middle_grad.astype(BF), "rep")
-    feed_down_grad = spread(rows_dot(cot, feed_low))
-    feed_gate_grad = spread(rows_dot(normed_mid, gate_grad))
-    feed_up_grad = spread(rows_dot(normed_mid, up_grad))
-    feed_out = reduce_line(back_dot(feed_low, w_down).astype(BF), "rep")
-    block_output = by_segment((middle + feed_out).astype(BF))[None]
-
+    branch = back_dot(gated, w_output).astype(BF)
+    branch, cot_pass[-1] = after((branch, cot_pass[-1]))
+    normed_mid, s2, middle = exchange("norm", (branch, x_low, feed_gain[None]), own_width)
+    normed_mid, cot_pass[-1] = after((normed_mid, cot_pass[-1]))
+    cot_pass.append(pass_on(cot_pass[-1], 3, "rep"))
+    pre = dot(normed_mid, w_feed)
+    pre, cot_pass[-1] = after((pre, cot_pass[-1]))
+    cot = put_together(cot_pass, "rep")
+    feed_low, feed_grads, mid_mean = feed_backward(cot, pre, w_down)
+    mid_mean = small_sum(mid_mean[:, 0].reshape(8, -1), "rep").reshape(-1, 1) / features
+
+    half = w_down.shape[1]
+    down_grad = rows_dot(cot, feed_low).astype(BF)
+    feed_grads, down_grad = after((feed_grads, down_grad))
+    feed_all = rows_dot(normed_mid, feed_grads).astype(BF)
+    feed_part = back_dot(feed_low, w_down).astype(BF)
+    feed_grads, feed_all, feed_part = after((feed_grads, feed_all, feed_part))
+    mid_grad = back_dot(feed_grads, w_feed).astype(BF)
+    down_grad, feed_all = spread(down_grad), spread(feed_all)
+    middle_low, middle_grad, feed_gain_own = exchange(
+        "back",
+        (mid_grad, cot_own, middle, s2, jnp.broadcast_to(mid_mean, (length, 128)), feed_own),
+        own_width,
+    )
+    middle_low, down_grad, feed_all = after((middle_low, down_grad, feed_all))
+    feed_down_grad = down_grad.astype(F32)
+    feed_gate_grad, feed_up_grad = feed_all[:, :half].astype(F32), feed_all[:, half:].astype(F32)
+    feed_gain_own = jnp.sum(feed_gain_own, axis=0)
+
+    feed_part, middle_low = after((feed_part, middle_low))
+    feed_pass = reduce_step(feed_part, None, 1, "rep")
     gated_grad = dot(middle_low, w_output)
-    recur_output_grad = spread(rows_dot(middle_low, gated))
-    local, after, branch_grad, enter_a, enter_b, back_total, branch_dot = recur_adjoint(
-        gated_grad, gate_branch, hidden, retain
+    local, after_prod, branch_grad, enter_a, enter_b, back_total, branch_dot = recur_adjoint(
+        gated_grad, projected, hidden, retain
     )
+    output_all = rows_dot(middle_low, gated).astype(BF)
+    local, feed_pass, output_all = after((local, feed_pass, output_all))
+    feed_pass = reduce_step(feed_part, feed_pass, 2, "rep")
+    output_all = spread(output_all)
     entering = jnp.zeros_like(state_init)
     for k in range(1, seqs):
         arriving = lax.ppermute(back_total[0:1] * entering + back_total[1:2], "seq", to_last)
         entering = jnp.where(seq == seqs - 1 - k, arriving, entering)
     enter = enter_a * entering + enter_b
     decay_grad, input_grad_low, low_grad, first, sums = recur_backward(
-        local, after, enter, hidden, carry, conv_out, decay_sig, gate_sig, retain, same, params, conv_in, decay_w, input_w
+        local, after_prod, enter, hidden, carry, conv_out, decay_sig, gate_sig, retain, same, params, projected,
+        decay_w, input_w,
     )
+    low_grad, feed_pass = after((low_grad, feed_pass))
+    for k in range(3, lax.axis_size("rep")):
+        feed_pass = reduce_step(feed_part, feed_pass, k, "rep")
     owed = [first[0:8], first[8:24], first[24:48]]
     owed = [o.reshape(k + 1, SEGS, -1) for k, o in enumerate(owed)]
     ahead = prefix.reshape(edge, SEGS, -1).astype(F32)
     back_share = jnp.zeros_like(ahead)
-    tap_extra = [jnp.zeros_like(conv_bias)]
+    tap_extra = [jnp.zeros((width,), F32)]
     for k in range(1, taps):
         term = jnp.pad(owed[k - 1], ((edge - k, 0), (0, 0), (0, 0)))
         tap_extra.append(jnp.sum(term * ahead, axis=(0, 1)))
-        back_share = back_share + conv_kernel[k] * term
+        back_share = back_share + params[k] * term
     from_right = lax.ppermute(back_share[:, 0], "seq", to_last)
     share = jnp.concatenate([back_share[:, 1:], from_right[:, None]], axis=1)
     low_grad = low_grad.reshape(length // SEGS, SEGS, -1)
     low_grad = jnp.concatenate([low_grad[:-edge], low_grad[-edge:] + share], axis=0).reshape(length, -1)
-    input_low = low_grad.astype(BF)
-    in_mean = jnp.sum(low_grad * conv_in.astype(F32), axis=1) + branch_dot[:, 0]
+    in_mean = jnp.sum(low_grad * projected[:, :width].astype(BF).astype(F32), axis=1) + branch_dot[:, 0]
     in_mean = small_sum(in_mean.reshape(8, -1), "rep").reshape(-1, 1) / features
 
-    normed_grad = reduce_line((back_dot(input_low, w_input) + back_dot(branch_grad, w_gate)).astype(BF), "rep")
-    recur_gate_grad = spread(rows_dot(normed, branch_grad))
-    recur_input_grad = spread(rows_dot(normed, input_low))
+    both_grads = jnp.concatenate([low_grad.astype(BF), branch_grad], axis=1)
+    normed_part = back_dot(both_grads, w_input).astype(BF)
+    normed_part, output_all, feed_pass = after((normed_part, output_all, feed_pass))
+    feed_out = reduce_end(feed_part, feed_pass, "rep")
+    block_output = by_segment((middle + feed_out).astype(BF))[None]
+    normed_part, both_grads, conv_out, decay_grad, input_grad_low = after(
+        (normed_part, both_grads, conv_out, decay_grad, input_grad_low)
+    )
+    conv_low = conv_out.astype(BF)
+    decay_gate_grad = diagonal_rows(rows_dot(conv_low, decay_grad), heads, head_width)
+    input_gate_grad = diagonal_rows(rows_dot(conv_low, input_grad_low), heads, head_width)
+    sums = jnp.sum(sums.reshape(8, 8, -1), axis=1)
+    conv_kernel_grad = sums[:taps] + jnp.stack(tap_extra)
+    logit_grad = sums[7:, :channels] * 8.0 * jax.nn.sigmoid(decay_logit)
+    vectors = jnp.concatenate([conv_kernel_grad, sums[4:7]], axis=0)[:, :channels]
+    vectors = jnp.concatenate([vectors, logit_grad], axis=0)
+    parts = (decay_gate_grad, input_gate_grad, vectors)
+    both_grads, parts = after((both_grads, parts))
+    summed = sum_small(parts, ("seq", "row"))
+    recur_all = spread(rows_dot(normed, both_grads).astype(BF))
+    recur_output_grad = output_all[:, :channels].astype(F32)
+    recur_input_grad = recur_all[:, :channels].astype(F32)
+    recur_gate_grad = recur_all[:, width : width + channels].astype(F32)
+    decay_gate_grad, input_gate_grad = (g[:, :head_width].reshape(decay_gate.shape) for g in summed[:2])
+    vectors = summed[2]
+
+    normed_pass = None
+    for k in range(1, lax.axis_size("rep")):
+        normed_pass = reduce_step(normed_part, normed_pass, k, "rep")
+    normed_grad = reduce_end(normed_part, normed_pass, "rep")
     xh1 = x_own * s1
     mixer_gain_own = jnp.sum(normed_grad * xh1, axis=0)
     input_grad = middle_grad + s1 * (normed_grad * mixer_own - xh1 * in_mean)
     input_grad = by_segment(input_grad.astype(BF))[None]
-
-    conv_low = conv_out.astype(BF)
-    decay_gate_grad = diagonal_blocks(rows_dot(conv_low, decay_grad), heads)
-    input_gate_grad = diagonal_blocks(rows_dot(conv_low, input_grad_low), heads)
-    sums = jnp.sum(sums.reshape(8, 8, -1), axis=1)
-    conv_kernel_grad = sums[:taps] + jnp.stack(tap_extra)
-    small = (
-        conv_kernel_grad, sums[4], decay_gate_grad, input_gate_grad, sums[5], sums[6],
-        sums[7] * 8.0 * jax.nn.sigmoid(decay_logit),
-    )
-    small = lax.psum(small, ("seq", "row"))
-    gains = jnp.stack([mixer_gain_own, feed_gain_own])
-    gains = lax.dynamic_update_slice(jnp.zeros((2, features), F32), gains, (0, rep * own_width))
-    gains = lax.psum(gains, ("seq", "row", "rep"))
+    gains = jnp.stack([mixer_gain_own, feed_gain_own]).reshape(8, -1)
+    gains = small_sum(small_sum(gains, "row"), "seq").reshape(2, own_width)
+    gains = small_gather(gains, "rep")
     return (
-        block_output, block_states[:, None], block_windows[None, None], input_grad,
+        block_output, block_states[:, None, :channels], block_windows[None, None], input_grad,
         recur_input_grad, recur_gate_grad, recur_output_grad, feed_gate_grad, feed_up_grad, feed_down_grad,
-        *small, gains[0], gains[1],
+        vectors[:taps], vectors[4], decay_gate_grad, input_gate_grad, vectors[5], vectors[6], vectors[7],
+        gains[0], gains[1],
     )
 
 

time: 932 us -> 785 us (0.84)
  Pallas kernels: 38.7 us -> 357 us
  waiting for transfers between devices: 295 us -> 73.1 us
  starting transfers between devices: 210 us -> 90.7 us
  blocking collectives: 61.5 us -> 0 us
  other arithmetic: 92.3 us -> 50.1 us
  matrix products: 165 us -> 137 us
    pallas_call x1 -> x5, Pallas kernels: 10.1 us -> 327 us  [the longest x3 300 us: exchange(): pl.pallas_call(partial_call(exchange_kernel, count, chunks, mode), in_spe...]
    ppermute x48 -> x21, waiting for transfers between devices: 272 us -> 62.1 us  [the longest x6 49.5 us: reduce_step(): right = lax.ppermute(right.astype(BF), axis, [(i, i + 1) for i in range(k)])]
    ppermute x48 -> x21, starting transfers between devices: 138 us -> 45.5 us  [the longest x6 24 us: reduce_step(): right = lax.ppermute(right.astype(BF), axis, [(i, i + 1) for i in range(k)])]
    psum x2 -> x0, blocking collectives: 61.5 us -> none  [the longest x1 38.1 us: shards(): gains = lax.psum(gains, ('seq', 'row', 'rep'))]
    convert_element_type x19 -> x10, other arithmetic: 40 us -> 12.4 us  [the longest x3 5.28 us: reduce_step(): left.astype(BF)]
    ppermute x12 -> x10, starting transfers between devices: 57.9 us -> 32.4 us  [small_sum(): lax.ppermute(own, axis, [(i, (i + k) % count) for i in range(count)])]
    dot_general x6 -> x3, matrix products: 61.2 us -> 38.7 us  [dot(): return jnp.dot(left, right, preferred_element_type=F32)]
    dynamic_update_slice x17 -> x3, other arithmetic: 23.5 us -> 6.45 us  [put_together(): lax.dynamic_update_slice(total, piece, (0, lax.rem(there, count) * width))]
  transfers between devices with their start and end apart: 78 -> 44, of which waited for: 28 -> 10; matrix products, arithmetic and copies ran while one was open for 27% -> 23% of each run, Pallas kernels for 4% -> 44%
where the time goes in v2:
time: 785 us; the launch traced here: 775 us
  Pallas kernels  357 us (45%)
  matrix products  137 us (17%)
  starting transfers between devices  90.7 us (12%)
  waiting for transfers between devices  73.1 us (9%)
  local copies, waits for them, and re-layouts  50.6 us (6%)
  other arithmetic  50.1 us (6%)
  between operations  16 us (2%)
    pallas_call x3, Pallas kernels, exchange(): pl.pallas_call(partial_call(exchange_kernel, count, chunks, mode), in_spe...  300 us
    ppermute x6, waiting for transfers between devices, reduce_step(): right = lax.ppermute(right.astype(BF), axis, [(i, i + 1) for i in range(k)])  49.5 us
    dot_general x4, matrix products, back_dot(): lax.dot_general(left, right, (((1,), (1,)), ((), ())), preferred_element_...  49.2 us
    dot_general x6, matrix products, rows_dot(): lax.dot_general(left, right, (((0,), (0,)), ((), ())), preferred_element_...  49.2 us
    dot_general x3, matrix products, dot(): return jnp.dot(left, right, preferred_element_type=F32)  38.7 us
    ppermute x10, starting transfers between devices, small_sum(): lax.ppermute(own, axis, [(i, (i + k) % count) for i in range(count)])  32.4 us
    unnamed x138, local copies, waits for them, and re-layouts  26.7 us
    ppermute x6, starting transfers between devices, reduce_step(): right = lax.ppermute(right.astype(BF), axis, [(i, i + 1) for i in range(k)])  24 us
  transfers between devices with their start and end apart: 44, of which 10 were waited for; matrix products, arithmetic and copies ran while one was open for 23% of the time, Pallas kernels for 44%

profile of v2, /device:TPU:0, one launch (start us, length us, event | category | flops | bytes accessed | tf_op | source)
XLA Modules:
  0.0 774.6 jit_solution(3345251664573882023)
XLA Ops:
  12.0 75.7 %shard_map.348 = (bf16[1024,2048]{1,0:T(8,128)(2,1)S(1)}, f32[1024,128]{1,0:T(8,128)S(1)}) custom-call(bf16[1024,512]{1,0:T(8,128)(2,1)S(1)} %bitcast.144, f32[1,2048]{1,0:T(1,128)S(1)} %bitcast.149), custom_call_target="tpu_custom_call" | custom-call | flops 20971520 | bytes 335544320 | tf_op jit(solution)/shard_map/pallas_call | solution.py:625
  91.7 5.5 collective-permute-start.2
  111.3 12.5 %fusion.53 = (bf16[1024,1536]{1,0:T(8,128)(2,1)S(1)}, f32[1024,1536]{1,0:T(8,128)}) fusion(bf16[1024,2048]{1,0:T(8,128)(2,1)} %copy-done.24, bf16[2048,2304]{0,1:T(8,128)(2,1)} %all-gather.5.cloned.1.call-done), kind=kOutput, calls=%fused_computation.182 | convolution fusion | flops 6444023808 | bytes 19922944 | tf_op jit(solution)/shard_map/dot_general | solution.py:690
  131.6 12.3 %shard_map.349 = (f32[1024,768]{1,0:T(8,128)S(1)}, f32[1024,768]{1,0:T(8,128)}, f32[1024,768]{1,0:T(8,128)}, f32[1024,768]{1,0:T(8,128)}, f32[1024,768]{1,0:T(8,...) custom-call(f32[1024,1536]{1,0:T(8,128)} %get-tuple-element.325.conv_in.gate_bra, ...), custom_call_target="tpu_custom_call" | custom-call | flops 786432 | bytes 3145728 | tf_op jit(solution)/shard_map/pallas_call | solution.py:196
  157.7 7.0 fusion.12
  164.7 7.4 convolution_convert_fusion.5.refs_0_
  172.1 7.1 collective-permute-done.6
  179.3 113.6 %shard_map.350 = (bf16[1024,2048]{1,0:T(8,128)(2,1)}, f32[1024,128]{1,0:T(8,128)S(1)}, f32[1024,512]{1,0:T(8,128)S(1)}) custom-call(bf16[1024,2048]{1,0:T(8,128)(2,1)} %convolution_convert_fusion.5.refs_0_, bf16[1024,512]{1,0:T(8,128)(2,1)S(1)} %bitcast.145, f32[1,2048]{1,0:T(1,128)S(1)} %bitcast.148), custom_call_target="tpu_custom_call" | custom-call | flops 20971520 | bytes 335544320 | tf_op jit(solution)/shard_map/pallas_call | solution.py:625
  297.9 19.2 %fusion.54.pre_gate.pre_up = f32[1024,3072]{1,0:T(8,128)} fusion(bf16[1024,2048]{1,0:T(8,128)(2,1)} %get-tuple-element.110, bf16[2048,3072]{1,0:T(8,128)(2,1)} %all-gather.7.cloned.1.call-done), kind=kOutput, calls=%fused_computation.183 | convolution fusion | flops 12884901888 | bytes 29360128 | tf_op jit(solution)/shard_map/dot_general | solution.py:690
  323.6 17.4 %shard_map.351 = (bf16[1024,1536]{1,0:T(8,128)(2,1)}, bf16[1024,3072]{1,0:T(8,128)(2,1)}, f32[1024,128]{1,0:T(8,128)S(1)}) custom-call(bf16[1024,2048]{1,0:T(8,128)(2,1)} %select_dynamic-update-slice_fusion.cot, f32[1024,3072]{1,0:T(8,128)} %fusion.54.pre_gate.pre_up, f32[1024,3072]{1,0:T(8,128)} %fusion.54.pre_gate.pre_up, ...), custom_call_target="tpu_custom_call" | custom-call | flops 6442450944 | bytes 62914560 | tf_op jit(solution)/shard_map/pallas_call | solution.py:657
  340.9 11.5 %convolution_convert_fusion.2 = bf16[2048,1536]{1,0:T(8,128)(2,1)} fusion(bf16[1024,2048]{1,0:T(8,128)(2,1)} %select_dynamic-update-slice_fusion.cot, bf16[1024,1536]{1,0:T(8,128)(2,1)} %get-tuple-element.117), kind=kOutput, calls=%fused_computation.3 | convolution fusion | flops 6445596672 | bytes 13631488 | tf_op jit(solution)/shard_map/dot_general | solution.py:682
  352.9 11.3 %convolution_convert_fusion.4 = bf16[1024,2048]{1,0:T(8,128)(2,1)} fusion(bf16[1024,1536]{1,0:T(8,128)(2,1)} %get-tuple-element.117, bf16[2048,1536]{1,0:T(8,128)(2,1)} %all-gather.9.cloned.1.call-done.down), kind=kOutput, calls=%fused_computation.10 | convolution fusion | flops 6444548096 | bytes 13631488 | tf_op jit(solution)/shard_map/dot_general | solution.py:686
  364.2 19.3 %convolution_convert_fusion = bf16[2048,3072]{1,0:T(8,128)(2,1)} fusion(bf16[1024,2048]{1,0:T(8,128)(2,1)S(1)} %copy-done.59, bf16[1024,3072]{1,0:T(8,128)(2,1)} %get-tuple-element.120), kind=kOutput, calls=%fused_computation.1 | convolution fusion | flops 12891193344 | bytes 23068672 | tf_op jit(solution)/shard_map/dot_general | solution.py:682
  384.0 5.8 collective-permute-start.10
  391.8 19.5 %convolution_convert_fusion.3.refs_0_ = bf16[1024,2048]{1,0:T(8,128)(2,1)} fusion(bf16[1024,3072]{1,0:T(8,128)(2,1)} %get-tuple-element.120, bf16[2048,3072]{1,0:T(8,128)(2,1)} %all-gather.7.cloned.1.call-done), kind=kOutput, calls=%fused_computation.9 | convolution fusion | flops 12886999040 | bytes 23068672 | tf_op jit(solution)/shard_map/dot_general | solution.py:686
  411.6 110.9 %shard_map.352 = (bf16[1024,2048]{1,0:T(8,128)(2,1)}, f32[1024,512]{1,0:T(8,128)S(1)}, f32[8,512]{1,0:T(8,128)S(1)}) custom-call(bf16[1024,2048]{1,0:T(8,128)(2,1)} %convolution_convert_fusion.3.refs_0_, bf16[1024,512]{1,0:T(8,128)(2,1)S(1)} %fusion.26.refs_1_, f32[1024,512]{1,0:T(8,128)} %copy-done, f32[1024,128]{1,0:T(8,128)S(1)} %copy-done.15, ...), custom_call_target="tpu_custom_call" | custom-call | flops 20971520 | bytes 335544320 | tf_op jit(solution)/shard_map/pallas_call | solution.py:625
  530.6 7.0 fusion.14.gated_grad
  537.6 9.5 %shard_map.353 = (f32[1024,768]{1,0:T(8,128)S(1)}, f32[1024,768]{1,0:T(8,128)}, bf16[1024,768]{1,0:T(8,128)(2,1)S(1)}, f32[8,768]{1,0:T(8,128)S(1)}, f32[8,768]{...) custom-call(f32[1024,768]{1,0:T(8,128)} %fusion.14.gated_grad, ...), custom_call_target="tpu_custom_call" | custom-call | flops 786432 | bytes 3145728 | tf_op jit(solution)/shard_map/pallas_call | solution.py:274
  552.1 5.1 convolution_convert_fusion.6
  560.3 17.6 %shard_map.354 = (bf16[1024,768]{1,0:T(8,128)(2,1)S(1)}, bf16[1024,768]{1,0:T(8,128)(2,1)}, f32[1024,768]{1,0:T(8,128)}, f32[48,768]{1,0:T(8,128)S(1)}, f32[64,768]{1,0:T(8,128)S(1)}) custom-call(f32[1024,768]{1,0:T(8,128)} %copy-done.9, f32[1024,768]{1,0:T(8,128)} %get-tuple-element.132.after, f32[8,768]{1,0:T(8,128)S(1)} %multiply_add_fusion.1.enter, ...), custom_call_target="tpu_custom_call" | custom-call | flops 786432 | bytes 3145728 | tf_op jit(solution)/shard_map/pallas_call | solution.py:363
  581.7 4.4 collective-permute-done.17
  586.1 9.7 %collective-permute-done.15 = bf16[1024,512]{1,0:T(8,128)(2,1)S(1)} collective-permute-done((bf16[1024,512]{1,0:T(8,128)(2,1)S(1)}, bf16[1024,512]{1,0:T(8,128)(2,1)S(1)}, u32[]{:S(2)}, u32[]{:S(2)}) %collective-permute-start.15) | collective-permute-done | bytes 1048608 | tf_op jit(solution)/shard_map/ppermute | solution.py:69
  598.1 6.2 collective-permute-start.18
  607.7 11.1 %fusion.4 = bf16[1024,2048]{1,0:T(8,128)(2,1)} fusion(bf16[2048,2304]{0,1:T(8,128)(2,1)} %all-gather.5.cloned.1.call-done, bf16[1024,768]{1,0:T(8,128)(2,1)S(1)} %copy-done.13, bf16[1024,768]{1,0:T(8,128)(2,1)S(1)} %fusion.17), kind=kOutput, calls=%fused_computation.11 | convolution fusion | flops 6450839552 | bytes 13631488 | tf_op jit(solution)/shard_map/dot_general | solution.py:686
  628.0 8.9 %convolution_convert_fusion.1 = bf16[2048,1536]{1,0:T(8,128)(2,1)} fusion(bf16[1024,2048]{1,0:T(8,128)(2,1)S(1)} %copy-done.25, bf16[1024,1536]{1,0:T(8,128)(2,1)S(1)} %copy-done.33), kind=kOutput, calls=%fused_computation.2 | convolution fusion | flops 6445596672 | bytes 13631488 | tf_op jit(solution)/shard_map/dot_general | solution.py:682
  645.6 21.8 %collective-permute-done.20 = bf16[1024,512]{1,0:T(8,128)(2,1)S(1)} collective-permute-done((bf16[1024,512]{1,0:T(8,128)(2,1)S(1)}, bf16[1024,512]{1,0:T(8,128)(2,1)S(1)}, u32[]{:S(2)}, u32[]{:S(2)}) %collective-permute-start.20) | collective-permute-done | bytes 1048608 | tf_op jit(solution)/shard_map/ppermute | solution.py:69
  667.9 4.8 collective-permute-start.21
  672.8 17.9 %collective-permute-done.21 = bf16[1024,512]{1,0:T(8,128)(2,1)S(1)} collective-permute-done((bf16[1024,512]{1,0:T(8,128)(2,1)S(1)}, bf16[1024,512]{1,0:T(8,128)(2,1)S(1)}, u32[]{:S(2)}, u32[]{:S(2)}) %collective-permute-start.21) | collective-permute-done | bytes 1048608 | tf_op jit(solution)/shard_map/ppermute | solution.py:69
  695.7 5.1 collective-permute-start.22
  705.7 19.1 %collective-permute-start.27 = (f32[8,128]{1,0:T(8,128)S(1)}, f32[8,128]{1,0:T(8,128)S(1)}, u32[]{:S(2)}, u32[]{:S(2)}) collective-permute-start(f32[8,128]{1,0:T(8,128)S(1)} %bitcast_add_fusion), channel_id=1, source_target_pairs={{0,2},{1,3},{2,0},{3,1},{4,6},{5,7},{6,4},{7,5},{8,10},{9,11},{10,... | collective-permute-start | bytes 12296 | tf_op jit(solution)/shard_map/ppermute | solution.py:82
  730.2 5.5 collective-permute-done.27
  751.7 5.4 collective-permute-done.33
  (340 shorter events, 143.4 us)
Async XLA Ops:
  7.2 104.1 %all-gather.5.cloned.1.call-start = ((), (), s32[]{:S(2)}) async-start(), calls=%async_computation.4 | async-start | bytes 10616832 | tf_op jit(solution)/shard_map/all_gather | solution.py:711
  9.7 288.2 %all-gather.7.cloned.1.call-start = ((), (), s32[]{:S(2)}) async-start(), calls=%async_computation.5 | async-start | bytes 14155776 | tf_op jit(solution)/shard_map/all_gather | solution.py:711
  11.2 312.4 %all-gather.9.cloned.1.call-start = ((), (), s32[]{:S(2)}) async-start(), calls=%async_computation.6 | async-start | bytes 7077888 | tf_op jit(solution)/shard_map/all_gather | solution.py:711
  90.4 63.7 %collective-permute-start.3 = (bf16[1024,512]{1,0:T(8,128)(2,1)S(1)}, bf16[1024,512]{1,0:T(8,128)(2,1)}, u32[]{:S(2)}, u32[]{:S(2)}) collective-permute-start(bf16[1024,512]{1,0:T(8,128)(2,1)S(1)} %fusion.26.refs_1_), channel_id=1, source_target_pairs={{1,0},{2,1},{3,2},{5,4},{6,5},{7,6},{9,8},{10,9},{11,10},{13,12},{... | collective-permute-start | bytes 3145736 | tf_op jit(solution)/shard_map/ppermute | solution.py:40
  91.7 62.4 %collective-permute-start.2 = (bf16[1024,512]{1,0:T(8,128)(2,1)S(1)}, bf16[1024,512]{1,0:T(8,128)(2,1)}, u32[]{:S(2)}, u32[]{:S(2)}) collective-permute-start(bf16[1024,512]{1,0:T(8,128)(2,1)S(1)} %fusion.26.refs_1_), channel_id=1, source_target_pairs={{0,1},{1,2},{2,3},{4,5},{5,6},{6,7},{8,9},{9,10},{10,11},{12,13},{... | collective-permute-start | bytes 3145736 | tf_op jit(solution)/shard_map/ppermute | solution.py:39
  98.0 12.6 %collective-permute-start = (f32[1,3]{1,0:T(1,128)S(1)}, f32[1,3]{1,0:T(1,128)S(1)}, u32[]{:S(2)}, u32[]{:S(2)}) collective-permute-start(f32[1,3]{1,0:T(1,128)S(1)} %slice_convert_fusion.5), channel_id=1, source_target_pairs={{0,16},{1,17},{2,18},{3,19},{4,20},{5,21},{6,22},{7,23},{8,24},{9,... | collective-permute-start | bytes 44 | tf_op jit(solution)/shard_map/ppermute | solution.py:738
  101.4 422.4 %reduce-scatter.5.cloned.1.call-start = ((), (), s32[]{:S(2)}) async-start(), calls=%async_computation.7 | async-start | bytes 7077888 | tf_op jit(solution)/shard_map/reduce_scatter | solution.py:714
  146.2 10.8 %collective-permute-start.4 = (f32[1,768]{1,0:T(1,128)S(1)}, f32[1,768]{1,0:T(1,128)S(1)}, u32[]{:S(2)}, u32[]{:S(2)}) collective-permute-start(f32[1,768]{1,0:T(1,128)S(1)} %get-tuple-element.315), channel_id=1, source_target_pairs={{0,16},{1,17},{2,18},{3,19},{4,20},{5,21},{6,22},{7,23},{8,24},{9,... | collective-permute-start | bytes 9224 | tf_op jit(solution)/shard_map/ppermute | solution.py:763
  154.2 18.0 %collective-permute-start.5 = (bf16[1024,512]{1,0:T(8,128)(2,1)}, bf16[1024,512]{1,0:T(8,128)(2,1)}, u32[]{:S(2)}, u32[]{:S(2)}) collective-permute-start(bf16[1024,512]{1,0:T(8,128)(2,1)} %collective-permute-done.2), channel_id=1, source_target_pairs={{1,2},{2,3},{5,6},{6,7},{9,10},{10,11},{13,14},{14,15},{17,18},{18... | collective-permute-start | bytes 3145736 | tf_op jit(solution)/shard_map/ppermute | solution.py:39
  155.8 23.5 %collective-permute-start.6 = (bf16[1024,512]{1,0:T(8,128)(2,1)}, bf16[1024,512]{1,0:T(8,128)(2,1)}, u32[]{:S(2)}, u32[]{:S(2)}) collective-permute-start(bf16[1024,512]{1,0:T(8,128)(2,1)} %collective-permute-done.3), channel_id=1, source_target_pairs={{1,0},{2,1},{5,4},{6,5},{9,8},{10,9},{13,12},{14,13},{17,16},{18,1... | collective-permute-start | bytes 3145736 | tf_op jit(solution)/shard_map/ppermute | solution.py:40
  294.9 22.1 %collective-permute-start.7 = (bf16[1024,512]{1,0:T(8,128)(2,1)}, bf16[1024,512]{1,0:T(8,128)(2,1)}, u32[]{:S(2)}, u32[]{:S(2)}) collective-permute-start(bf16[1024,512]{1,0:T(8,128)(2,1)} %collective-permute-done.5), channel_id=1, source_target_pairs={{2,3},{6,7},{10,11},{14,15},{18,19},{22,23},{26,27},{30,31}} | collective-permute-start | bytes 3145736 | tf_op jit(solution)/shard_map/ppermute | solution.py:39
  296.6 20.6 %collective-permute-start.8 = (bf16[1024,512]{1,0:T(8,128)(2,1)}, bf16[1024,512]{1,0:T(8,128)(2,1)S(1)}, u32[]{:S(2)}, u32[]{:S(2)}) collective-permute-start(bf16[1024,512]{1,0:T(8,128)(2,1)} %collective-permute-done.6), channel_id=1, source_target_pairs={{1,0},{5,4},{9,8},{13,12},{17,16},{21,20},{25,24},{29,28}} | collective-permute-start | bytes 3145736 | tf_op jit(solution)/shard_map/ppermute | solution.py:40
  352.5 171.3 %reduce-scatter.7.cloned.1.call-start = ((), (), s32[]{:S(2)}) async-start(), calls=%async_computation.8 | async-start | bytes 14155776 | tf_op jit(solution)/shard_map/reduce_scatter | solution.py:714
  383.5 237.2 %reduce-scatter.9.cloned.1.call-start = ((), (), s32[]{:S(2)}) async-start(), calls=%async_computation.9 | async-start | bytes 3538944 | tf_op jit(solution)/shard_map/reduce_scatter | solution.py:714
  384.0 27.4 %collective-permute-start.10 = (f32[8,128]{1,0:T(8,128)S(1)}, f32[8,128]{1,0:T(8,128)S(1)}, u32[]{:S(2)}, u32[]{:S(2)}) collective-permute-start(f32[8,128]{1,0:T(8,128)S(1)} %bitcast.162), channel_id=1, source_target_pairs={{0,2},{1,3},{2,0},{3,1},{4,6},{5,7},{6,4},{7,5},{8,10},{9,11},{10,... | collective-permute-start | bytes 12296 | tf_op jit(solution)/shard_map/ppermute | solution.py:82
  389.8 21.5 %collective-permute-start.11 = (f32[8,128]{1,0:T(8,128)S(1)}, f32[8,128]{1,0:T(8,128)S(1)}, u32[]{:S(2)}, u32[]{:S(2)}) collective-permute-start(f32[8,128]{1,0:T(8,128)S(1)} %bitcast.163), channel_id=1, source_target_pairs={{0,3},{1,0},{2,1},{3,2},{4,7},{5,4},{6,5},{7,6},{8,11},{9,8},{10,9... | collective-permute-start | bytes 12296 | tf_op jit(solution)/shard_map/ppermute | solution.py:82
  390.2 21.2 %collective-permute-start.9 = (f32[8,128]{1,0:T(8,128)S(1)}, f32[8,128]{1,0:T(8,128)S(1)}, u32[]{:S(2)}, u32[]{:S(2)}) collective-permute-start(f32[8,128]{1,0:T(8,128)S(1)} %bitcast.164), channel_id=1, source_target_pairs={{0,1},{1,2},{2,3},{3,0},{4,5},{5,6},{6,7},{7,4},{8,9},{9,10},{10,1... | collective-permute-start | bytes 12296 | tf_op jit(solution)/shard_map/ppermute | solution.py:82
  526.6 30.6 %collective-permute-start.13 = (bf16[1024,512]{1,0:T(8,128)(2,1)}, bf16[1024,512]{1,0:T(8,128)(2,1)}, u32[]{:S(2)}, u32[]{:S(2)}) collective-permute-start(bf16[1024,512]{1,0:T(8,128)(2,1)} %get-tuple-element.289), channel_id=1, source_target_pairs={{3,2},{7,6},{11,10},{15,14},{19,18},{23,22},{27,26},{31,30}} | collective-permute-start | bytes 3145736 | tf_op jit(solution)/shard_map/ppermute | solution.py:70
  528.3 28.9 %collective-permute-start.12 = (bf16[1024,512]{1,0:T(8,128)(2,1)S(1)}, bf16[1024,512]{1,0:T(8,128)(2,1)}, u32[]{:S(2)}, u32[]{:S(2)}) collective-permute-start(bf16[1024,512]{1,0:T(8,128)(2,1)S(1)} %get-tuple-element.290), channel_id=1, source_target_pairs={{0,1},{4,5},{8,9},{12,13},{16,17},{20,21},{24,25},{28,29}} | collective-permute-start | bytes 3145736 | tf_op jit(solution)/shard_map/ppermute | solution.py:69
  557.3 200.5 %reduce-scatter.11.cloned.1.call-start = ((), (), s32[]{:S(2)}) async-start(), calls=%async_computation.10 | async-start | bytes 7077888 | tf_op jit(solution)/shard_map/reduce_scatter | solution.py:714
  578.7 17.2 %collective-permute-start.15 = (bf16[1024,512]{1,0:T(8,128)(2,1)S(1)}, bf16[1024,512]{1,0:T(8,128)(2,1)S(1)}, u32[]{:S(2)}, u32[]{:S(2)}) collective-permute-start(bf16[1024,512]{1,0:T(8,128)(2,1)S(1)} %get-tuple-element.288), channel_id=1, source_target_pairs={{0,1},{1,2},{4,5},{5,6},{8,9},{9,10},{12,13},{13,14},{16,17},{17,1... | collective-permute-start | bytes 3145736 | tf_op jit(solution)/shard_map/ppermute | solution.py:69
  596.7 24.0 %collective-permute-start.19 = (bf16[1024,512]{1,0:T(8,128)(2,1)S(1)}, bf16[1024,512]{1,0:T(8,128)(2,1)}, u32[]{:S(2)}, u32[]{:S(2)}) collective-permute-start(bf16[1024,512]{1,0:T(8,128)(2,1)S(1)} %get-tuple-element.285), channel_id=1, source_target_pairs={{1,0},{2,1},{3,2},{5,4},{6,5},{7,6},{9,8},{10,9},{11,10},{13,12},{... | collective-permute-start | bytes 3145736 | tf_op jit(solution)/shard_map/ppermute | solution.py:70
  598.1 22.6 %collective-permute-start.18 = (bf16[1024,512]{1,0:T(8,128)(2,1)S(1)}, bf16[1024,512]{1,0:T(8,128)(2,1)}, u32[]{:S(2)}, u32[]{:S(2)}) collective-permute-start(bf16[1024,512]{1,0:T(8,128)(2,1)S(1)} %get-tuple-element.286), channel_id=1, source_target_pairs={{0,1},{1,2},{2,3},{4,5},{5,6},{6,7},{8,9},{9,10},{10,11},{12,13},{... | collective-permute-start | bytes 3145736 | tf_op jit(solution)/shard_map/ppermute | solution.py:69
  636.8 124.4 %all-gather.11.cloned.1.call-start = ((), (), s32[]{:S(2)}) async-start(), calls=%async_computation.11 | async-start | bytes 6635520 | tf_op jit(solution)/shard_map/all_gather | solution.py:104
  640.7 26.7 %collective-permute-start.20 = (bf16[1024,512]{1,0:T(8,128)(2,1)S(1)}, bf16[1024,512]{1,0:T(8,128)(2,1)S(1)}, u32[]{:S(2)}, u32[]{:S(2)}) collective-permute-start(bf16[1024,512]{1,0:T(8,128)(2,1)S(1)} %get-tuple-element.283), channel_id=1, source_target_pairs={{0,1},{4,5},{8,9},{12,13},{16,17},{20,21},{24,25},{28,29}} | collective-permute-start | bytes 3145736 | tf_op jit(solution)/shard_map/ppermute | solution.py:69
  644.9 27.9 %collective-permute-start.23 = (bf16[1024,512]{1,0:T(8,128)(2,1)S(1)}, bf16[1024,512]{1,0:T(8,128)(2,1)S(1)}, u32[]{:S(2)}, u32[]{:S(2)}) collective-permute-start(bf16[1024,512]{1,0:T(8,128)(2,1)S(1)} %get-tuple-element.284), channel_id=1, source_target_pairs={{3,2},{7,6},{11,10},{15,14},{19,18},{23,22},{27,26},{31,30}} | collective-permute-start | bytes 3145736 | tf_op jit(solution)/shard_map/ppermute | solution.py:70
  667.9 22.8 %collective-permute-start.21 = (bf16[1024,512]{1,0:T(8,128)(2,1)S(1)}, bf16[1024,512]{1,0:T(8,128)(2,1)S(1)}, u32[]{:S(2)}, u32[]{:S(2)}) collective-permute-start(bf16[1024,512]{1,0:T(8,128)(2,1)S(1)} %add_convert_fusion.4), channel_id=1, source_target_pairs={{0,1},{1,2},{4,5},{5,6},{8,9},{9,10},{12,13},{13,14},{16,17},{17,1... | collective-permute-start | bytes 3145736 | tf_op jit(solution)/shard_map/ppermute | solution.py:69
  695.7 40.1 %collective-permute-start.22 = (bf16[1024,512]{1,0:T(8,128)(2,1)S(1)}, bf16[1024,512]{1,0:T(8,128)(2,1)S(1)}, u32[]{:S(2)}, u32[]{:S(2)}) collective-permute-start(bf16[1024,512]{1,0:T(8,128)(2,1)S(1)} %get-tuple-element.281), channel_id=1, source_target_pairs={{0,1},{1,2},{2,3},{4,5},{5,6},{6,7},{8,9},{9,10},{10,11},{12,13},{... | collective-permute-start | bytes 3145736 | tf_op jit(solution)/shard_map/ppermute | solution.py:69
  702.4 33.4 %collective-permute-start.25 = (bf16[1024,512]{1,0:T(8,128)(2,1)S(1)}, bf16[1024,512]{1,0:T(8,128)(2,1)S(1)}, u32[]{:S(2)}, u32[]{:S(2)}) collective-permute-start(bf16[1024,512]{1,0:T(8,128)(2,1)S(1)} %add_convert_fusion.1), channel_id=1, source_target_pairs={{1,0},{2,1},{3,2},{5,4},{6,5},{7,6},{9,8},{10,9},{11,10},{13,12},{... | collective-permute-start | bytes 3145736 | tf_op jit(solution)/shard_map/ppermute | solution.py:70
  705.7 30.0 %collective-permute-start.27 = (f32[8,128]{1,0:T(8,128)S(1)}, f32[8,128]{1,0:T(8,128)S(1)}, u32[]{:S(2)}, u32[]{:S(2)}) collective-permute-start(f32[8,128]{1,0:T(8,128)S(1)} %bitcast_add_fusion), channel_id=1, source_target_pairs={{0,2},{1,3},{2,0},{3,1},{4,6},{5,7},{6,4},{7,5},{8,10},{9,11},{10,... | collective-permute-start | bytes 12296 | tf_op jit(solution)/shard_map/ppermute | solution.py:82
  724.8 10.9 %collective-permute-start.28 = (f32[8,128]{1,0:T(8,128)S(1)}, f32[8,128]{1,0:T(8,128)S(1)}, u32[]{:S(2)}, u32[]{:S(2)}) collective-permute-start(f32[8,128]{1,0:T(8,128)S(1)} %bitcast_add_fusion), channel_id=1, source_target_pairs={{0,3},{1,0},{2,1},{3,2},{4,7},{5,4},{6,5},{7,6},{8,11},{9,8},{10,9... | collective-permute-start | bytes 12296 | tf_op jit(solution)/shard_map/ppermute | solution.py:82
  725.7 10.0 %collective-permute-start.26 = (f32[8,128]{1,0:T(8,128)S(1)}, f32[8,128]{1,0:T(8,128)S(1)}, u32[]{:S(2)}, u32[]{:S(2)}) collective-permute-start(f32[8,128]{1,0:T(8,128)S(1)} %bitcast_add_fusion), channel_id=1, source_target_pairs={{0,1},{1,2},{2,3},{3,0},{4,5},{5,6},{6,7},{7,4},{8,9},{9,10},{10,1... | collective-permute-start | bytes 12296 | tf_op jit(solution)/shard_map/ppermute | solution.py:82
  (74 other events, 1077.2 us)
Sparse Core Ops, SparseCore 0:
  10.5 63.2 all-gather.4
  76.3 72.1 all-gather.6
  150.3 45.6 all-gather.8
  352.6 64.1 reduce-scatter.4
  420.5 92.4 reduce-scatter.6
  557.4 47.7 reduce-scatter.8
  637.0 64.2 reduce-scatter.10
  703.3 43.8 all-gather.10

commit v3 on v2

--- a/solution.py
+++ b/solution.py
@@ -32,47 +32,6 @@
 
 
 after = lax.optimization_barrier
-
-
-def pass_on(held, k, axis):
-    count = lax.axis_size(axis)
-    right = lax.ppermute(held[0], axis, [(i, i + 1) for i in range(k - 1, count - 1)])
-    left = lax.ppermute(held[1], axis, [(i, i - 1) for i in range(1, count - k + 1)])
-    return right, left
-
-
-def put_together(passed, axis):
-    count, me = lax.axis_size(axis), lax.axis_index(axis)
-    own = passed[0][0]
-    width = own.shape[1]
-    total = jnp.zeros((own.shape[0], count * width), own.dtype)
-    total = lax.dynamic_update_slice(total, own, (0, me * width))
-    for k in range(1, count):
-        there = me + k
-        piece = jnp.where(there < count, passed[k][1], passed[count - k][0])
-        total = lax.dynamic_update_slice(total, piece, (0, lax.rem(there, count) * width))
-    return total
-
-
-def line_part(whole, target, axis):
-    count = lax.axis_size(axis)
-    width = whole.shape[1] // count
-    return lax.dynamic_slice_in_dim(whole, jnp.clip(target, 0, count - 1) * width, width, 1).astype(F32)
-
-
-def reduce_step(whole, held, k, axis):
-    count, me = lax.axis_size(axis), lax.axis_index(axis)
-    far = count - k
-    right, left = line_part(whole, me + far, axis), line_part(whole, me - far, axis)
-    if held is not None:
-        right, left = right + held[0].astype(F32), left + held[1].astype(F32)
-    right = lax.ppermute(right.astype(BF), axis, [(i, i + 1) for i in range(k)])
-    left = lax.ppermute(left.astype(BF), axis, [(i, i - 1) for i in range(far, count)])
-    return right, left
-
-
-def reduce_end(whole, held, axis):
-    return line_part(whole, lax.axis_index(axis), axis) + held[0].astype(F32) + held[1].astype(F32)
 
 
 def small_sum(own, axis):
@@ -93,15 +52,18 @@
     return total
 
 
-def sum_small(parts, axes):
+def join_small(parts):
     width = 256
     padded = []
     for part in parts:
         columns = -part.shape[1] % width
         padded.append(jnp.pad(part, ((0, 0), (0, columns))).reshape(-1, width))
     counts = [p.shape[0] for p in padded]
-    joined = jnp.concatenate(padded + [jnp.zeros((-sum(counts) % 16, width), F32)], axis=0).astype(BF)
-    joined = jnp.sum(lax.all_gather(joined, axes).astype(F32), axis=0)
+    spare = jnp.zeros((-sum(counts) % 16, width), F32)
+    return jnp.concatenate(padded + [spare], axis=0).astype(BF), counts
+
+
+def split_small(joined, counts, parts):
     out, start = [], 0
     for part, rows in zip(parts, counts):
         out.append(joined[start : start + rows].reshape(part.shape[0], -1)[:, : part.shape[1]])
@@ -132,8 +94,8 @@
 
 
 def forward_kernel(
-    conv_in, same, prefix, params, decay_w, input_w,
-    out_conv, out_decay, out_gate, out_retain, out_prod, out_state, out_pre_a, out_pre_b, out_total,
+    conv_in, gate_branch, same, prefix, params, decay_w, input_w,
+    out_gelu, out_conv, out_decay, out_gate, out_retain, out_prod, out_state, out_pre_a, out_pre_b, out_total,
     last_rows, prod_now, state_now, inflow_s,
 ):
     step = pl.program_id(0)
@@ -145,6 +107,7 @@
         prod_now[...] = jnp.ones_like(prod_now)
         state_now[...] = jnp.zeros_like(state_now)
 
+    out_gelu[...] = gelu(gate_branch[...])
     now = conv_in[...].astype(BF).astype(F32)
     ext = jnp.concatenate([last_rows[...], now], axis=0)
     same_all = same[...]
@@ -198,14 +161,15 @@
         grid=(length // rows,),
         in_specs=[
             block,
+            pl.BlockSpec((rows, width), lambda i: (i, 1)),
             pl.BlockSpec((rows, 8), lambda i: (i, 0)),
             fixed((24, width)),
             fixed((8, width)),
             fixed((width, width)),
             fixed((width, width)),
         ],
-        out_specs=[block] * 6 + [fixed((SEGS, width))] * 3,
-        out_shape=[big] * 6 + [small] * 3,
+        out_specs=[block] * 7 + [fixed((SEGS, width))] * 3,
+        out_shape=[big] * 7 + [small] * 3,
         scratch_shapes=[
             pltpu.VMEM((24, width), F32),
             pltpu.VMEM((SEGS, width), F32),
@@ -214,7 +178,7 @@
         ],
         compiler_params=pltpu.CompilerParams(vmem_limit_bytes=LIMIT),
         cost_estimate=pl.CostEstimate(flops=length * width, bytes_accessed=4 * length * width, transcendentals=0),
-    )(conv_in, same, prefix, params, decay_w, input_w)
+    )(conv_in, conv_in, same, prefix, params, decay_w, input_w)
 
 
 def adjoint_kernel(
@@ -390,48 +354,93 @@
 
 
 def exchange_kernel(count, chunks, mode, *refs):
-    backward, summing = mode == "back", mode != "first"
-    if backward:
-        (partial, residual, middle, scale, mean, gain, out, out_own, out_gain) = refs[:9]
+    backward, summing, gathering = mode in ("back", "last"), mode != "first", mode != "last"
+    refs = list(refs)
+    take = lambda number: [refs.pop(0) for _ in range(number)]
+    if mode == "first":
+        residual, gain, out, out_scale, gathered = take(5)
+    elif mode == "norm":
+        states, products, gates, carry, weight, residual, gain, out, out_scale, out_own, out_hidden, out_gated = take(12)
+        (gathered,) = take(1)
+    elif mode == "back":
+        grads, weight, residual, middle, scale, mean, gain, out, out_own, out_gain = take(10)
         gathered = out
-        rest = refs[9:]
-    elif summing:
-        (partial, residual, gain, out, out_scale, out_own, gathered) = refs[:7]
-        rest = refs[7:]
     else:
-        (residual, gain, out, out_scale, gathered) = refs[:5]
-        rest = refs[5:]
+        grads, weight, residual, middle, scale, mean, gain, small, feed_sums, out_own, out_small, out_gains = take(12)
+        out_gain, gain_own, gain_row, gain_seq, small_own, small_row, small_seq = take(7)
+        gain_sems, small_sems = take(2)
     if summing:
-        right, left, total, sum_send, sum_recv, all_send, all_recv = rest
-    else:
-        all_send, all_recv = rest
+        partial, held_weight, right, left, total, weight_sem, sum_send, sum_recv = take(8)
+    if gathering:
+        all_send, all_recv = take(2)
     me = lax.axis_index("rep")
     length, width = residual.shape
     rows = length // chunks
     last = count - 1
 
+    if summing:
+        start = weight.shape[1] - held_weight.shape[1] if mode == "norm" else 0
+        load = pltpu.make_async_copy(weight.at[:, pl.ds(start, held_weight.shape[1])], held_weight, weight_sem)
+        load.start()
     barrier = pltpu.get_barrier_semaphore()
-
-    @pl.when(me > 0)
-    def _():
-        pl.semaphore_signal(barrier, inc=1, device_id={"rep": me - 1}, device_id_type=pl.DeviceIdType.MESH)
-
-    @pl.when(me < last)
-    def _():
-        pl.semaphore_signal(barrier, inc=1, device_id={"rep": me + 1}, device_id_type=pl.DeviceIdType.MESH)
-
-    inner = jnp.logical_and(me > 0, me < last)
-
-    @pl.when(inner)
-    def _():
-        pl.semaphore_wait(barrier, 2)
-
-    @pl.when(jnp.logical_not(inner))
-    def _():
-        pl.semaphore_wait(barrier, 1)
+    if gathering:
+
+        @pl.when(me > 0)
+        def _():
+            pl.semaphore_signal(barrier, inc=1, device_id={"rep": me - 1}, device_id_type=pl.DeviceIdType.MESH)
+
+        @pl.when(me < last)
+        def _():
+            pl.semaphore_signal(barrier, inc=1, device_id={"rep": me + 1}, device_id_type=pl.DeviceIdType.MESH)
+
+        inner = jnp.logical_and(me > 0, me < last)
+
+        @pl.when(inner)
+        def _():
+            pl.semaphore_wait(barrier, 2)
+
+        @pl.when(jnp.logical_not(inner))
+        def _():
+            pl.semaphore_wait(barrier, 1)
+
+    else:
+        for axis in ("row", "seq", "rep"):
+            for d in range(1, lax.axis_size(axis)):
+                peer = lax.rem(lax.axis_index(axis) + d, lax.axis_size(axis))
+                pl.semaphore_signal(barrier, inc=1, device_id={axis: peer}, device_id_type=pl.DeviceIdType.MESH)
+        pl.semaphore_wait(barrier, sum(lax.axis_size(axis) - 1 for axis in ("row", "seq", "rep")))
+
+    def to_peers(axis, source, target, sems):
+        copies = []
+        for d in range(1, lax.axis_size(axis)):
+            peer = lax.rem(lax.axis_index(axis) + d, lax.axis_size(axis))
+            copies.append(
+                pltpu.make_async_remote_copy(
+                    src_ref=source,
+                    dst_ref=target(d),
+                    send_sem=sems.at[0, d],
+                    recv_sem=sems.at[1, d],
+                    device_id={axis: peer},
+                    device_id_type=pl.DeviceIdType.MESH,
+                )
+            )
+        return copies
+
+    if mode == "last":
+        small_rows = to_peers("row", small_own, lambda d: small_row.at[d], small_sems.at[0])
+        small_seqs = to_peers("seq", small_row.at[0], lambda d: small_seq.at[d], small_sems.at[1])
+        gain_rows = to_peers("row", gain_own, lambda d: gain_row.at[d], gain_sems.at[0])
+        gain_seqs = to_peers("seq", gain_row.at[0], lambda d: gain_seq.at[d], gain_sems.at[1])
+        own_gains = out_gains.at[:, pl.ds(pl.multiple_of(me * width, width), width)]
+        gain_reps = to_peers("rep", gain_seq.at[0], lambda d: own_gains, gain_sems.at[2])
+        small_own[...] = small[...]
+        for copy in small_rows:
+            copy.start()
 
     if backward:
         out_gain[...] = jnp.zeros_like(out_gain)
+    if summing:
+        load.wait()
 
     def at(c):
         return pl.ds(pl.multiple_of(c * rows, rows), rows)
@@ -488,7 +497,41 @@
     def inside(c):
         return jnp.logical_and(c >= 0, c < chunks)
 
+    stride = 1
+
+    def produce(c):
+        some = pl.ds(pl.multiple_of(c * rows, stride * rows), stride * rows)
+        if mode == "norm":
+            wide = (stride * rows // SEGS, SEGS, carry.shape[1])
+            enter = jnp.broadcast_to(carry[...][None], wide).reshape(stride * rows, carry.shape[1])
+            hidden = states[some, :] + products[some, :] * enter
+            low = (hidden * gates[some, :]).astype(BF)
+            out_hidden[some, :] = hidden
+            out_gated[some, :] = low
+        else:
+            low = grads[some, :]
+        partial[some, :] = back_dot(low, held_weight[...]).astype(BF)
+
     def tick(now, _):
+        if mode == "last":
+
+            @pl.when(now == chunks - 2)
+            def _():
+                for copy in small_rows:
+                    copy.wait_recv()
+                added = small_own[...].astype(F32)
+                for d in range(1, lax.axis_size("row")):
+                    added = added + small_row[d].astype(F32)
+                small_row[0] = added.astype(BF)
+                for copy in small_seqs:
+                    copy.start()
+
+        if summing:
+
+            @pl.when(jnp.logical_and(now < chunks, lax.rem(now, stride) == 0))
+            def _():
+                produce(now)
+
         for side in (0, 1) if summing else ():
             place = (me, last - me)[side]
             c = now - place
@@ -526,7 +569,7 @@
 
             if backward:
                 size = scale[at(done), 0:1]
-                normal = middle[at(done), :] * size
+                normal = middle[at(done), :].astype(F32) * size
                 summed = total[...]
                 own = residual[at(done), :].astype(F32) + size * (
                     summed * gain[...] - normal * mean[at(done), 0:1]
@@ -534,8 +577,9 @@
                 out_gain[...] += jnp.sum((summed * normal).reshape(rows // 8, 8, width), axis=0)
             else:
                 own = residual[at(done), :].astype(F32) + total[...]
-            out_own[at(done), :] = own
-            gathered[at(done), columns(me)] = own.astype(BF)
+            out_own[at(done), :] = own.astype(out_own.dtype)
+            if gathering:
+                gathered[at(done), columns(me)] = own.astype(BF)
 
         done = now - last if summing else now
 
@@ -545,16 +589,17 @@
                 finish(done)
             else:
                 gathered[at(done), columns(me)] = residual[at(done), :]
-
-            @pl.when(me < last)
-            def _():
-                all_copy(0, 0, done).start()
-
-            @pl.when(me > 0)
-            def _():
-                all_copy(1, 0, done).start()
-
-        for far in range(1, count):
+            if gathering:
+
+                @pl.when(me < last)
+                def _():
+                    all_copy(0, 0, done).start()
+
+                @pl.when(me > 0)
+                def _():
+                    all_copy(1, 0, done).start()
+
+        for far in range(1, count) if gathering else ():
             c = done - far
             for side in (0, 1):
                 place = (me, last - me)[side]
@@ -579,7 +624,7 @@
 
         return 0
 
-    lax.fori_loop(0, chunks + (2 * last if summing else last), tick, 0)
+    lax.fori_loop(0, chunks + last * (summing + gathering), tick, 0)
 
     def settle(c, _):
         for side in (0, 1):
@@ -590,13 +635,47 @@
                 def _(side=side, slot=slot):
                     sum_copy(side, slot, c).wait_send()
 
-            for far in range(0, last):
+            for far in range(0, last) if gathering else ():
 
                 @pl.when(jnp.logical_and(place < last, place >= far))
                 def _(side=side, far=far):
                     all_copy(side, far, c).wait_send()
 
         return 0
+
+    if mode == "last":
+        mixer_sum = jnp.sum(out_gain[...], axis=0, keepdims=True)
+        feed_sum = jnp.sum(feed_sums[...], axis=0, keepdims=True)
+        gain_own[...] = jnp.concatenate([mixer_sum, feed_sum, jnp.zeros((6, width), F32)], axis=0)
+        for copy in gain_rows:
+            copy.start()
+        for copy in small_seqs:
+            copy.wait_recv()
+        added = small_row[0].astype(F32)
+        for d in range(1, lax.axis_size("seq")):
+            added = added + small_seq[d].astype(F32)
+        out_small[...] = added
+        for copy in gain_rows:
+            copy.wait_recv()
+        added = gain_own[...]
+        for d in range(1, lax.axis_size("row")):
+            added = added + gain_row[d]
+        gain_row[0] = added
+        for copy in gain_seqs:
+            copy.start()
+        for copy in gain_seqs:
+            copy.wait_recv()
+        added = gain_row[0]
+        for d in range(1, lax.axis_size("seq")):
+            added = added + gain_seq[d]
+        gain_seq[0] = added
+        for copy in gain_reps:
+            copy.start()
+        own_gains[...] = added
+        for copy in gain_reps:
+            copy.wait_recv()
+        for copy in small_rows + small_seqs + gain_rows + gain_seqs + gain_reps:
+            copy.wait_send()
 
     lax.fori_loop(0, chunks, settle, 0)
 
@@ -605,31 +684,61 @@
     count = lax.axis_size("rep")
     length = operands[0].shape[0]
     features = count * width
-    backward, summing = mode == "back", mode != "first"
+    backward, summing, gathering = mode in ("back", "last"), mode != "first", mode != "last"
     vmem = pl.BlockSpec(memory_space=pltpu.VMEM)
-    scratch = [pltpu.SemaphoreType.DMA((2, count, chunks)), pltpu.SemaphoreType.DMA((2, count, chunks))]
-    out_shape = [jax.ShapeDtypeStruct((length, features), BF)]
+    in_specs = [vmem] * len(operands)
+    sems = [pltpu.SemaphoreType.DMA((2, count, chunks)), pltpu.SemaphoreType.DMA((2, count, chunks))]
+    full, own = jax.ShapeDtypeStruct((length, features), BF), jax.ShapeDtypeStruct((length, width), F32)
+    scale, gain = jax.ShapeDtypeStruct((length, 128), F32), jax.ShapeDtypeStruct((8, width), F32)
+    if mode == "first":
+        out_shape = [full, scale]
+    elif mode == "norm":
+        hidden = operands[0].shape
+        out_shape = [full, scale, own, jax.ShapeDtypeStruct(hidden, F32), jax.ShapeDtypeStruct(hidden, BF)]
+    elif mode == "back":
+        out_shape = [full, own, gain]
+    else:
+        small = operands[7].shape
+        out_shape = [
+            jax.ShapeDtypeStruct((length, width), BF),
+            jax.ShapeDtypeStruct(small, F32),
+            jax.ShapeDtypeStruct((8, features), F32),
+        ]
+    scratch = [] if backward else [pltpu.VMEM((length, features), BF)]
+    if mode == "last":
+        row, seq = lax.axis_size("row"), lax.axis_size("seq")
+        most = max(row, seq, count)
+        scratch += [
+            pltpu.VMEM((8, width), F32),
+            pltpu.VMEM((8, width), F32),
+            pltpu.VMEM((row, 8, width), F32),
+            pltpu.VMEM((seq, 8, width), F32),
+            pltpu.VMEM(small, BF),
+            pltpu.VMEM((row,) + small, BF),
+            pltpu.VMEM((seq,) + small, BF),
+            pltpu.SemaphoreType.DMA((3, 2, most)),
+            pltpu.SemaphoreType.DMA((2, 2, most)),
+        ]
     if summing:
-        scratch = [
+        in_specs[4 if mode == "norm" else 1] = pl.BlockSpec(memory_space=pl.ANY)
+        scratch += [
+            pltpu.VMEM((length, features), BF),
+            pltpu.VMEM((features, operands[0].shape[1]), BF),
             pltpu.VMEM((count, length, width), BF),
             pltpu.VMEM((count, length, width), BF),
             pltpu.VMEM((length // chunks, width), F32),
-        ] + scratch * 2
-    if not backward:
-        out_shape.append(jax.ShapeDtypeStruct((length, 128), F32))
-        scratch = [pltpu.VMEM((length, features), BF)] + scratch
-    if summing:
-        out_shape.append(jax.ShapeDtypeStruct((length, width), F32))
-    if backward:
-        out_shape.append(jax.ShapeDtypeStruct((8, width), F32))
+            pltpu.SemaphoreType.DMA,
+        ] + sems
+    if gathering:
+        scratch += sems
     return pl.pallas_call(
         partial_call(exchange_kernel, count, chunks, mode),
-        in_specs=[vmem] * len(operands),
+        in_specs=in_specs,
         out_specs=[vmem] * len(out_shape),
         out_shape=out_shape,
         scratch_shapes=scratch,
         compiler_params=pltpu.CompilerParams(
-            collective_id=("first", "norm", "back").index(mode), has_side_effects=True, vmem_limit_bytes=LIMIT
+            collective_id=("first", "norm", "back", "last").index(mode), has_side_effects=True, vmem_limit_bytes=LIMIT
         ),
         cost_estimate=pl.CostEstimate(
             flops=10 * length * features, bytes_accessed=160 * length * features, transcendentals=0
@@ -725,14 +834,12 @@
     width = channels + spare
 
     x_low = by_step(block_input[0])
-    x_own = x_low.astype(F32)
     cot_own = by_step(cotangent[0] * pad_mask[0][:, None].astype(BF))
     mixer_own, feed_own = own_part(mixer_gain), own_part(feed_gain)
     normed, s1 = exchange("first", (x_low, mixer_gain[None]), own_width)
-    s1 = s1[:, :1]
     w_recur = weights(jnp.concatenate([wide(recur_input), wide(recur_gate), wide(recur_output)], axis=1))
-    w_feed = weights(jnp.concatenate([feed_gate, feed_up], axis=1))
-    w_down = weights(feed_down)
+    cot_own, normed, w_recur = after((cot_own, normed, w_recur))
+    cot = lax.all_gather(cot_own, "rep", axis=1, tiled=True)
     w_input, w_output = w_recur[:, : 2 * width], w_recur[:, 2 * width :]
 
     left_ids = lax.ppermute(segment_ids[:, -edge:].astype(F32), "seq", to_next).astype(jnp.int32)
@@ -748,14 +855,18 @@
     state_init = wide(state_init)
 
     projected = dot(normed, w_input)
-    gate_branch = projected[:, width:]
+    feed_shard, feed_down, projected = after(
+        (jnp.concatenate([feed_gate, feed_up], axis=1), feed_down, projected)
+    )
+    w_feed = weights(feed_shard)
+    w_down = weights(feed_down)
     ends = projected[-edge * SEGS :, :width].astype(BF).reshape(edge, SEGS, width)
     left = lax.ppermute(ends[:, -1], "seq", to_next)
     left = jnp.where(at_start, wide(window_init[0]), left)
     prefix = jnp.concatenate([left[:, None], ends[:, :-1]], axis=1).reshape(edge * SEGS, -1)
     block_windows = ends[:, -1, :channels]
 
-    conv_out, decay_sig, gate_sig, retain, products, states, pre_a, pre_b, total = recur_forward(
+    gates, conv_out, decay_sig, gate_sig, retain, products, states, pre_a, pre_b, total = recur_forward(
         projected, same, prefix, params, decay_w, input_w
     )
     state_in = state_init
@@ -765,53 +876,35 @@
     block_states = total[0:1] * state_in + total[1:2]
     carry = pre_a * state_in + pre_b
 
-    cot_own, normed = after((cot_own, normed))
-    cot_pass = [(cot_own, cot_own)]
-    cot_pass.append(pass_on(cot_pass[-1], 1, "rep"))
-    states, cot_pass[-1] = after((states, cot_pass[-1]))
-    cot_pass.append(pass_on(cot_pass[-1], 2, "rep"))
-
-    hidden = states + products * per_segment(carry, length)
-    gated = (hidden * gelu(gate_branch)).astype(BF)
-    branch = back_dot(gated, w_output).astype(BF)
-    branch, cot_pass[-1] = after((branch, cot_pass[-1]))
-    normed_mid, s2, middle = exchange("norm", (branch, x_low, feed_gain[None]), own_width)
-    normed_mid, cot_pass[-1] = after((normed_mid, cot_pass[-1]))
-    cot_pass.append(pass_on(cot_pass[-1], 3, "rep"))
+    normed_mid, s2, middle, hidden, gated = exchange(
+        "norm", (states, products, gates, carry, w_recur, x_low, feed_gain[None]), own_width
+    )
+    normed_mid, cot = after((normed_mid, cot))
     pre = dot(normed_mid, w_feed)
-    pre, cot_pass[-1] = after((pre, cot_pass[-1]))
-    cot = put_together(cot_pass, "rep")
     feed_low, feed_grads, mid_mean = feed_backward(cot, pre, w_down)
     mid_mean = small_sum(mid_mean[:, 0].reshape(8, -1), "rep").reshape(-1, 1) / features
 
     half = w_down.shape[1]
+    feed_part = back_dot(feed_low, w_down).astype(BF)
+    feed_low, feed_part = after((feed_low, feed_part))
     down_grad = rows_dot(cot, feed_low).astype(BF)
-    feed_grads, down_grad = after((feed_grads, down_grad))
+    feed_grads, down_grad, mid_mean = after((feed_grads, down_grad, mid_mean))
     feed_all = rows_dot(normed_mid, feed_grads).astype(BF)
-    feed_part = back_dot(feed_low, w_down).astype(BF)
-    feed_grads, feed_all, feed_part = after((feed_grads, feed_all, feed_part))
-    mid_grad = back_dot(feed_grads, w_feed).astype(BF)
+    feed_grads, feed_all = after((feed_grads, feed_all))
     down_grad, feed_all = spread(down_grad), spread(feed_all)
     middle_low, middle_grad, feed_gain_own = exchange(
         "back",
-        (mid_grad, cot_own, middle, s2, jnp.broadcast_to(mid_mean, (length, 128)), feed_own),
+        (feed_grads, w_feed, cot_own, middle, s2, jnp.broadcast_to(mid_mean, (length, 128)), feed_own),
         own_width,
     )
-    middle_low, down_grad, feed_all = after((middle_low, down_grad, feed_all))
-    feed_down_grad = down_grad.astype(F32)
-    feed_gate_grad, feed_up_grad = feed_all[:, :half].astype(F32), feed_all[:, half:].astype(F32)
-    feed_gain_own = jnp.sum(feed_gain_own, axis=0)
 
     feed_part, middle_low = after((feed_part, middle_low))
-    feed_pass = reduce_step(feed_part, None, 1, "rep")
+    feed_out = lax.psum_scatter(feed_part, "rep", scatter_dimension=1, tiled=True)
     gated_grad = dot(middle_low, w_output)
     local, after_prod, branch_grad, enter_a, enter_b, back_total, branch_dot = recur_adjoint(
         gated_grad, projected, hidden, retain
     )
     output_all = rows_dot(middle_low, gated).astype(BF)
-    local, feed_pass, output_all = after((local, feed_pass, output_all))
-    feed_pass = reduce_step(feed_part, feed_pass, 2, "rep")
-    output_all = spread(output_all)
     entering = jnp.zeros_like(state_init)
     for k in range(1, seqs):
         arriving = lax.ppermute(back_total[0:1] * entering + back_total[1:2], "seq", to_last)
@@ -821,9 +914,6 @@
         local, after_prod, enter, hidden, carry, conv_out, decay_sig, gate_sig, retain, same, params, projected,
         decay_w, input_w,
     )
-    low_grad, feed_pass = after((low_grad, feed_pass))
-    for k in range(3, lax.axis_size("rep")):
-        feed_pass = reduce_step(feed_part, feed_pass, k, "rep")
     owed = [first[0:8], first[8:24], first[24:48]]
     owed = [o.reshape(k + 1, SEGS, -1) for k, o in enumerate(owed)]
     ahead = prefix.reshape(edge, SEGS, -1).astype(F32)
@@ -841,13 +931,9 @@
     in_mean = small_sum(in_mean.reshape(8, -1), "rep").reshape(-1, 1) / features
 
     both_grads = jnp.concatenate([low_grad.astype(BF), branch_grad], axis=1)
-    normed_part = back_dot(both_grads, w_input).astype(BF)
-    normed_part, output_all, feed_pass = after((normed_part, output_all, feed_pass))
-    feed_out = reduce_end(feed_part, feed_pass, "rep")
-    block_output = by_segment((middle + feed_out).astype(BF))[None]
-    normed_part, both_grads, conv_out, decay_grad, input_grad_low = after(
-        (normed_part, both_grads, conv_out, decay_grad, input_grad_low)
-    )
+    both_grads, in_mean, down_grad, feed_all = after((both_grads, in_mean, down_grad, feed_all))
+    feed_down_grad = down_grad.astype(F32)
+    feed_gate_grad, feed_up_grad = feed_all[:, :half].astype(F32), feed_all[:, half:].astype(F32)
     conv_low = conv_out.astype(BF)
     decay_gate_grad = diagonal_rows(rows_dot(conv_low, decay_grad), heads, head_width)
     input_gate_grad = diagonal_rows(rows_dot(conv_low, input_grad_low), heads, head_width)
@@ -857,26 +943,28 @@
     vectors = jnp.concatenate([conv_kernel_grad, sums[4:7]], axis=0)[:, :channels]
     vectors = jnp.concatenate([vectors, logit_grad], axis=0)
     parts = (decay_gate_grad, input_gate_grad, vectors)
-    both_grads, parts = after((both_grads, parts))
-    summed = sum_small(parts, ("seq", "row"))
-    recur_all = spread(rows_dot(normed, both_grads).astype(BF))
+    small, counts = join_small(parts)
+    recur_raw = rows_dot(normed, both_grads).astype(BF)
+    both_grads, recur_raw, output_all, feed_out = after((both_grads, recur_raw, output_all, feed_out))
+    output_all, recur_all = spread(output_all), spread(recur_raw)
+    input_grad, summed, gains = exchange(
+        "last",
+        (
+            both_grads, w_recur, middle_grad, x_low, s1, jnp.broadcast_to(in_mean, (length, 128)), mixer_own,
+            small, feed_gain_own,
+        ),
+        own_width,
+    )
+    input_grad, feed_out, recur_all, output_all = after((input_grad, feed_out, recur_all, output_all))
     recur_output_grad = output_all[:, :channels].astype(F32)
     recur_input_grad = recur_all[:, :channels].astype(F32)
     recur_gate_grad = recur_all[:, width : width + channels].astype(F32)
-    decay_gate_grad, input_gate_grad = (g[:, :head_width].reshape(decay_gate.shape) for g in summed[:2])
-    vectors = summed[2]
-
-    normed_pass = None
-    for k in range(1, lax.axis_size("rep")):
-        normed_pass = reduce_step(normed_part, normed_pass, k, "rep")
-    normed_grad = reduce_end(normed_part, normed_pass, "rep")
-    xh1 = x_own * s1
-    mixer_gain_own = jnp.sum(normed_grad * xh1, axis=0)
-    input_grad = middle_grad + s1 * (normed_grad * mixer_own - xh1 * in_mean)
-    input_grad = by_segment(input_grad.astype(BF))[None]
-    gains = jnp.stack([mixer_gain_own, feed_gain_own]).reshape(8, -1)
-    gains = small_sum(small_sum(gains, "row"), "seq").reshape(2, own_width)
-    gains = small_gather(gains, "rep")
+    input_grad = by_segment(input_grad)[None]
+    block_output = by_segment((middle + feed_out.astype(F32)).astype(BF))[None]
+    decay_gate_grad, input_gate_grad, vectors = split_small(summed, counts, parts)
+    decay_gate_grad, input_gate_grad = (
+        g[:, :head_width].reshape(decay_gate.shape) for g in (decay_gate_grad, input_gate_grad)
+    )
     return (
         block_output, block_states[:, None, :channels], block_windows[None, None], input_grad,
         recur_input_grad, recur_gate_grad, recur_output_grad, feed_gate_grad, feed_up_grad, feed_down_grad,

time: 785 us -> 744 us (0.948)
  Pallas kernels: 357 us -> 493 us
  starting transfers between devices: 90.7 us -> 20.3 us
  matrix products: 137 us -> 102 us
  waiting for transfers between devices: 73.1 us -> 39.8 us
  other arithmetic: 50.1 us -> 22.4 us
    pallas_call x3 -> x4, Pallas kernels: 300 us -> 433 us  [exchange(): pl.pallas_call(partial_call(exchange_kernel, count, chunks, mode), in_spe...]
    ppermute x21 -> x0, waiting for transfers between devices: 62.1 us -> none  [the longest x6 49.5 us: reduce_step(): right = lax.ppermute(right.astype(BF), axis, [(i, i + 1) for i in range(k)])]
    ppermute x21 -> x0, starting transfers between devices: 45.5 us -> none  [the longest x6 24 us: reduce_step(): right = lax.ppermute(right.astype(BF), axis, [(i, i + 1) for i in range(k)])]
    dot_general x4 -> x1, matrix products: 49.2 us -> 10.1 us  [back_dot(): lax.dot_general(left, right, (((1,), (1,)), ((), ())), preferred_element_...]
    ppermute x10 -> x6, starting transfers between devices: 32.4 us -> 6.68 us  [small_sum(): lax.ppermute(own, axis, [(i, (i + k) % count) for i in range(count)])]
    convert_element_type x6 -> x0, other arithmetic: 14.6 us -> none  [the longest x1 7.03 us: shards(): gated = (hidden * gelu(gate_branch)).astype(BF)]
    reduce_scatter x0 -> x1, waiting for transfers between devices: none -> 14.1 us  [shards(): lax.psum_scatter(feed_part, 'rep', scatter_dimension=1, tiled=True)]
    reduce_scatter x4, waiting for transfers between devices: 0.01 us -> 11.9 us  [spread(): lax.psum_scatter(partial_grad, ('seq', 'row'), scatter_dimension=0, tiled...]
  transfers between devices with their start and end apart: 44 -> 20, of which waited for: 10 -> 8; matrix products, arithmetic and copies ran while one was open for 23% -> 18% of each run, Pallas kernels for 44% -> 65%
where the time goes in v3:
time: 744 us; the launch traced here: 736 us
  Pallas kernels  493 us (66%)
  matrix products  102 us (14%)
  local copies, waits for them, and re-layouts  43.8 us (6%)
  waiting for transfers between devices  39.8 us (5%)
  other arithmetic  22.4 us (3%)
  starting transfers between devices  20.3 us (3%)
  between operations  15.1 us (2%)
    pallas_call x4, Pallas kernels, exchange(): pl.pallas_call(partial_call(exchange_kernel, count, chunks, mode), in_spe...  433 us
    dot_general x6, matrix products, rows_dot(): lax.dot_general(left, right, (((0,), (0,)), ((), ())), preferred_element_...  52.5 us
    dot_general x3, matrix products, dot(): return jnp.dot(left, right, preferred_element_type=F32)  39 us
    unnamed x127, local copies, waits for them, and re-layouts  30.1 us
    pallas_call x1, Pallas kernels, feed_backward(): pl.pallas_call(feed_kernel, grid=(length // rows,), in_specs=[block(featu...  17.4 us
    pallas_call x1, Pallas kernels, recur_backward(): pl.pallas_call(backward_kernel, grid=(length // rows,), in_specs=[block,...  17 us
  transfers between devices with their start and end apart: 20, of which 8 were waited for; matrix products, arithmetic and copies ran while one was open for 18% of the time, Pallas kernels for 65%

profile of v3, /device:TPU:0, one launch (start us, length us, event | category | flops | bytes accessed | tf_op | source)
XLA Modules:
  0.0 736.1 jit_solution(12592303758224455410)
XLA Ops:
  13.4 75.7 %shard_map.348 = (bf16[1024,2048]{1,0:T(8,128)(2,1)S(1)}, f32[1024,128]{1,0:T(8,128)S(1)}) custom-call(bf16[1024,512]{1,0:T(8,128)(2,1)S(1)} %bitcast.126, f32[1,2048]{1,0:T(1,128)S(1)} %bitcast.133), custom_call_target="tpu_custom_call" | custom-call | flops 20971520 | bytes 335544320 | tf_op jit(solution)/shard_map/pallas_call | solution.py:734
  93.5 2.5 pad_maximum_fusion.1
  96.1 11.8 %fusion.conv_in.gate_branch = f32[1024,1536]{1,0:T(8,128)} fusion(bf16[1024,2048]{1,0:T(8,128)(2,1)} %copy-done.22, bf16[2048,2304]{1,0:T(8,128)(2,1)} %all-gather.5.cloned.1.call-done.refs_4_.refs_1_), kind=kOutput, calls=%fused_computation.3 | convolution fusion | flops 6442450944 | bytes 16777216 | tf_op jit(solution)/shard_map/dot_general | solution.py:799
  108.6 3.4 collective-permute-start
  115.8 3.2 convert.51
  120.7 2.4 collective-permute-start.1
  125.7 14.6 %shard_map.349 = (f32[1024,768]{1,0:T(8,128)S(1)}, f32[1024,768]{1,0:T(8,128)}, f32[1024,768]{1,0:T(8,128)}, f32[1024,768]{1,0:T(8,128)}, f32[1024,768]{1,0:T(8,...) custom-call(f32[1024,1536]{1,0:T(8,128)} %fusion.conv_in.gate_branch, ...), custom_call_target="tpu_custom_call" | custom-call | flops 786432 | bytes 3145728 | tf_op jit(solution)/shard_map/pallas_call | solution.py:159
  142.7 4.1 collective-permute-start.2
  148.7 135.2 %shard_map.350 = (bf16[1024,2048]{1,0:T(8,128)(2,1)}, f32[1024,128]{1,0:T(8,128)S(1)}, f32[1024,512]{1,0:T(8,128)S(1)}, f32[1024,768]{1,0:T(8,128)}, bf16[1024,768]{1,0:T(8,128)(2,1)S(1)}) custom-call(f32[1024,768]{1,0:T(8,128)} %get-tuple-element.90.refs_0_, f32[1024,768]{1,0:T(8,128)} %get-tuple-element.91.refs_1_, f32[1024,768]{1,0:T(8,128)} %copy-done.9, ...), custom_call_target="tpu_custom_call" | custom-call | flops 20971520 | bytes 335544320 | tf_op jit(solution)/shard_map/pallas_call | solution.py:734
  287.2 18.9 %fusion.56.pre_gate.pre_up = f32[1024,3072]{1,0:T(8,128)} fusion(bf16[1024,2048]{1,0:T(8,128)(2,1)} %get-tuple-element.100, bf16[2048,3072]{1,0:T(8,128)(2,1)} %all-gather.9.cloned.1.call-done.refs_1_), kind=kOutput, calls=%fused_computation.157 | convolution fusion | flops 12884901888 | bytes 29360128 | tf_op jit(solution)/shard_map/dot_general | solution.py:799
  306.1 5.4 all-gather.11.cloned.1.call-done.down
  311.5 17.4 %shard_map.351 = (bf16[1024,1536]{1,0:T(8,128)(2,1)}, bf16[1024,3072]{1,0:T(8,128)(2,1)}, f32[1024,128]{1,0:T(8,128)S(1)}) custom-call(bf16[1024,2048]{1,0:T(8,128)(2,1)} %all-gather.7.cloned.1.call-done.cot, f32[1024,3072]{1,0:T(8,128)} %fusion.56.pre_gate.pre_up, f32[1024,3072]{1,0:T(8,128)} %fusion.56.pre_gate.pre_up, ...), custom_call_target="tpu_custom_call" | custom-call | flops 6442450944 | bytes 62914560 | tf_op jit(solution)/shard_map/pallas_call | solution.py:766
  329.1 2.5 collective-permute-start.4
  333.6 10.1 %convolution_convert_fusion.3 = bf16[1024,2048]{1,0:T(8,128)(2,1)} fusion(bf16[1024,1536]{1,0:T(8,128)(2,1)} %get-tuple-element.106, bf16[2048,1536]{1,0:T(8,128)(2,1)S(1)} %copy-done.29), kind=kOutput, calls=%fused_computation.5 | convolution fusion | flops 6444548096 | bytes 13631488 | tf_op jit(solution)/shard_map/dot_general | solution.py:795
  343.7 11.5 %convolution_convert_fusion.2 = bf16[2048,1536]{1,0:T(8,128)(2,1)} fusion(bf16[1024,2048]{1,0:T(8,128)(2,1)} %all-gather.7.cloned.1.call-done.cot, bf16[1024,1536]{1,0:T(8,128)(2,1)} %get-tuple-element.106), kind=kOutput, calls=%fused_computation.2 | convolution fusion | flops 6445596672 | bytes 13631488 | tf_op jit(solution)/shard_map/dot_general | solution.py:791
  355.7 19.5 %convolution_convert_fusion = bf16[2048,3072]{1,0:T(8,128)(2,1)} fusion(bf16[1024,2048]{1,0:T(8,128)(2,1)} %get-tuple-element.100, bf16[1024,3072]{1,0:T(8,128)(2,1)} %get-tuple-element.109.refs_0_), kind=kOutput, calls=%fused_computation | convolution fusion | flops 12891193344 | bytes 23068672 | tf_op jit(solution)/shard_map/dot_general | solution.py:791
  377.5 126.8 %shard_map.352 = (bf16[1024,2048]{1,0:T(8,128)(2,1)}, f32[1024,512]{1,0:T(8,128)S(1)}, f32[8,512]{1,0:T(8,128)S(1)}) custom-call(bf16[1024,3072]{1,0:T(8,128)(2,1)} %get-tuple-element.109.refs_0_, bf16[2048,3072]{1,0:T(8,128)(2,1)} %all-gather.9.cloned.1.call-done.refs_1_, bf16[1024,512]{1,0:T(8,128)(2,1)S(1)} %copy-done, f32[1024,512]{1,0:T(8,128)} %copy-done.1, ...), custom_call_target="tpu_custom_call" | custom-call | flops 20971520 | bytes 335544320 | tf_op jit(solution)/shard_map/pallas_call | solution.py:734
  505.9 8.3 %fusion.2.gated_grad = f32[1024,768]{1,0:T(8,128)} fusion(bf16[1024,2048]{1,0:T(8,128)(2,1)} %get-tuple-element.113, bf16[2048,2304]{1,0:T(8,128)(2,1)} %all-gather.5.cloned.1.call-done.refs_4_.refs_1_), kind=kOutput, calls=%fused_computation.12 | convolution fusion | flops 3221225472 | bytes 10485760 | tf_op jit(solution)/shard_map/dot_general | solution.py:799
  514.2 10.7 %shard_map.353 = (f32[1024,768]{1,0:T(8,128)S(1)}, f32[1024,768]{1,0:T(8,128)}, bf16[1024,768]{1,0:T(8,128)(2,1)S(1)}, f32[8,768]{1,0:T(8,128)S(1)}, f32[8,768]{...) custom-call(f32[1024,768]{1,0:T(8,128)} %fusion.2.gated_grad, f32[1024,1536]{1,0:T(8,128)} %fusion.conv_in.gate_branch, ...), custom_call_target="tpu_custom_call" | custom-call | flops 786432 | bytes 3145728 | tf_op jit(solution)/shard_map/pallas_call | solution.py:238
  529.0 5.0 convolution_convert_fusion.4
  535.5 17.0 %shard_map.354 = (bf16[1024,768]{1,0:T(8,128)(2,1)S(1)}, bf16[1024,768]{1,0:T(8,128)(2,1)}, f32[1024,768]{1,0:T(8,128)}, f32[48,768]{1,0:T(8,128)S(1)}, f32[64,768]{1,0:T(8,128)S(1)}) custom-call(f32[1024,768]{1,0:T(8,128)} %copy-done.8, f32[1024,768]{1,0:T(8,128)} %get-tuple-element.117.after, f32[8,768]{1,0:T(8,128)S(1)} %multiply_add_fusion.enter, ...), custom_call_target="tpu_custom_call" | custom-call | flops 786432 | bytes 3145728 | tf_op jit(solution)/shard_map/pallas_call | solution.py:327
  553.9 2.2 slice_bitcast_fusion
  556.1 2.0 collective-permute-done.7
  561.9 2.0 pad_maximum_fusion.refs_0_
  564.4 2.6 collective-permute-done.8
  567.0 11.6 %convolution_convert_fusion.1 = bf16[2048,1536]{1,0:T(8,128)(2,1)} fusion(bf16[1024,2048]{1,0:T(8,128)(2,1)} %copy-done.22, bf16[1024,1536]{1,0:T(8,128)(2,1)} %pad_maximum_fusion.refs_0_), kind=kOutput, calls=%fused_computation.1 | convolution fusion | flops 6445596672 | bytes 13631488 | tf_op jit(solution)/shard_map/dot_general | solution.py:791
  578.6 14.1 %reduce-scatter.10.cloned.1.call-done = bf16[1024,512]{1,0:T(8,128)(2,1)} async-done(((bf16[1024,2048]{1,0:T(8,128)(2,1)}), bf16[1024,512]{1,0:T(8,128)(2,1)}) %reduce-scatter.10.cloned.1.call-update) | async-done | bytes 1048592 | tf_op jit(solution)/shard_map/reduce_scatter | solution.py:902
  595.9 3.5 convolution_convert_fusion.6
  604.0 95.6 %shard_map.355 = (bf16[1024,512]{1,0:T(8,128)(2,1)S(1)}, f32[1440,256]{1,0:T(8,128)S(1)}, f32[8,2048]{1,0:T(8,128)S(1)}) custom-call(bf16[1024,1536]{1,0:T(8,128)(2,1)} %pad_maximum_fusion.refs_0_, bf16[2048,2304]{1,0:T(8,128)(2,1)} %all-gather.5.cloned.1.call-done.refs_4_.refs_1_, f32[1024,512]{1,0:T(8,128)} %copy-done.10, bf16[1024,512]{1,0:T(8,128)(2,1)S(1)} %bitcast.128, ...), custom_call_target="tpu_custom_call" | custom-call | flops 20971520 | bytes 335544320 | tf_op jit(solution)/shard_map/pallas_call | solution.py:734
  703.0 2.7 fusion.51
  706.3 3.4 slice_convert_fusion
  709.7 11.8 %reduce-scatter.12.cloned.1.call-done = bf16[256,1536]{1,0:T(8,128)(2,1)} async-done(((bf16[2048,1536]{1,0:T(8,128)(2,1)}), bf16[256,1536]{1,0:T(8,128)(2,1)}) %reduce-scatter.12.cloned.1.call-update) | async-done | bytes 786448 | tf_op jit(solution)/shard_map/reduce_scatter | solution.py:823
  (251 shorter events, 63.4 us)
Async XLA Ops:
  7.2 86.2 %all-gather.5.cloned.1.call-start = ((), (), s32[]{:S(2)}) async-start(), calls=%async_computation.5 | async-start | bytes 10616832 | tf_op jit(solution)/shard_map/all_gather | solution.py:820
  10.8 81.0 %copy-start.32 = (bf16[1,1024,512]{2,1,0:T(8,128)(2,1)S(1)}, bf16[1,1024,512]{2,1,0:T(8,128)(2,1)}, u32[]{:S(2)}) copy-start(bf16[1,1024,512]{2,1,0:T(8,128)(2,1)} %param.22) | copy-start | bytes 3145732
  12.0 275.2 %all-gather.7.cloned.1.call-start = ((), (), s32[]{:S(2)}) async-start(), calls=%async_computation.6 | async-start | bytes 5242880 | tf_op jit(solution)/shard_map/all_gather | solution.py:842
  12.8 79.1 %copy-start.39 = (bf16[8,128]{0,1:T(8,128)(2,1)S(1)}, bf16[8,128]{0,1:T(8,128)(2,1)}, u32[]{:S(2)}) copy-start(bf16[8,128]{0,1:T(8,128)(2,1)} %copy.93) | copy-start | bytes 6148
  13.4 80.2 %copy-start.33 = (bf16[256,1536]{1,0:T(8,128)(2,1)S(1)}, bf16[256,1536]{1,0:T(8,128)(2,1)}, u32[]{:S(2)}) copy-start(bf16[256,1536]{1,0:T(8,128)(2,1)} %param.31) | copy-start | bytes 2359300
  93.5 193.7 %all-gather.9.cloned.1.call-start = ((), (), s32[]{:S(2)}) async-start(), calls=%async_computation.7 | async-start | bytes 14155776 | tf_op jit(solution)/shard_map/all_gather | solution.py:820
  96.0 16.5 %copy-start.49 = (f32[704]{0:T(1024)S(1)}, f32[704]{0:T(1024)}, u32[]{:S(2)}) copy-start(f32[704]{0:T(1024)} %param.37) | copy-start | bytes 8452
  96.0 16.6 %copy-start.50 = (f32[704]{0:T(1024)S(1)}, f32[704]{0:T(1024)}, u32[]{:S(2)}) copy-start(f32[704]{0:T(1024)} %param.38) | copy-start | bytes 8452
  96.0 16.6 %copy-start.47 = (f32[704]{0:T(1024)S(1)}, f32[704]{0:T(1024)}, u32[]{:S(2)}) copy-start(f32[704]{0:T(1024)} %param.39) | copy-start | bytes 8452
  96.0 17.2 %copy-start.45 = (f32[4,704]{1,0:T(4,128)S(1)}, f32[4,704]{1,0:T(4,128)}, u32[]{:S(2)}) copy-start(f32[4,704]{1,0:T(4,128)} %param.33) | copy-start | bytes 33796
  96.1 17.2 %copy-start.37 = (bf16[4,176,176]{2,1,0:T(8,128)(2,1)S(1)}, bf16[4,176,176]{2,1,0:T(8,128)(2,1)}, u32[]{:S(2)}) copy-start(bf16[4,176,176]{2,1,0:T(8,128)(2,1)} %param.36) | copy-start | bytes 743428
  107.9 203.6 %all-gather.11.cloned.1.call-start = ((), (), s32[]{:S(2)}) async-start(), calls=%async_computation.8 | async-start | bytes 7077888 | tf_op jit(solution)/shard_map/all_gather | solution.py:820
  108.5 458.5 %reduce-scatter.6.cloned.1.call-start = ((), (), s32[]{:S(2)}) async-start(), calls=%async_computation.9 | async-start | bytes 7077888 | tf_op jit(solution)/shard_map/reduce_scatter | solution.py:823
  108.6 6.5 collective-permute-start
  120.7 3.7 collective-permute-start.1
  123.5 16.9 %copy-start.6 = (f32[128,8,8]{2,1,0:T(8,128)}, f32[128,8,8]{2,1,0:T(8,128)S(1)}, u32[]{:S(2)}) copy-start(f32[128,8,8]{2,1,0:T(8,128)S(1)} %copy.99) | copy-start | bytes 98308
  125.7 23.0 %copy-start.20 = (f32[2048]{0:T(1024)S(1)}, f32[2048]{0:T(1024)}, u32[]{:S(2)}) copy-start(f32[2048]{0:T(1024)} %param.41) | copy-start | bytes 24580
  142.7 5.5 collective-permute-start.2
  311.5 22.1 %copy-start.29 = (bf16[2048,1536]{1,0:T(8,128)(2,1)S(1)}, bf16[2048,1536]{1,0:T(8,128)(2,1)}, u32[]{:S(2)}) copy-start(bf16[2048,1536]{1,0:T(8,128)(2,1)} %all-gather.11.cloned.1.call-done.down) | copy-start | bytes 18874372
  329.1 26.1 %collective-permute-start.4 = (f32[8,128]{1,0:T(8,128)S(1)}, f32[8,128]{1,0:T(8,128)S(1)}, u32[]{:S(2)}, u32[]{:S(2)}) collective-permute-start(f32[8,128]{1,0:T(8,128)S(1)} %bitcast.147), channel_id=1, source_target_pairs={{0,2},{1,3},{2,0},{3,1},{4,6},{5,7},{6,4},{7,5},{8,10},{9,11},{10,... | collective-permute-start | bytes 12296 | tf_op jit(solution)/shard_map/ppermute | solution.py:41
  331.6 23.6 %collective-permute-start.5 = (f32[8,128]{1,0:T(8,128)S(1)}, f32[8,128]{1,0:T(8,128)S(1)}, u32[]{:S(2)}, u32[]{:S(2)}) collective-permute-start(f32[8,128]{1,0:T(8,128)S(1)} %bitcast.148), channel_id=1, source_target_pairs={{0,3},{1,0},{2,1},{3,2},{4,7},{5,4},{6,5},{7,6},{8,11},{9,8},{10,9... | collective-permute-start | bytes 12296 | tf_op jit(solution)/shard_map/ppermute | solution.py:41
  333.0 22.2 %collective-permute-start.3 = (f32[8,128]{1,0:T(8,128)S(1)}, f32[8,128]{1,0:T(8,128)S(1)}, u32[]{:S(2)}, u32[]{:S(2)}) collective-permute-start(f32[8,128]{1,0:T(8,128)S(1)} %bitcast.149), channel_id=1, source_target_pairs={{0,1},{1,2},{2,3},{3,0},{4,5},{5,6},{6,7},{7,4},{8,9},{9,10},{10,1... | collective-permute-start | bytes 12296 | tf_op jit(solution)/shard_map/ppermute | solution.py:41
  355.3 211.7 %reduce-scatter.8.cloned.1.call-start = ((), (), s32[]{:S(2)}) async-start(), calls=%async_computation.10 | async-start | bytes 14155776 | tf_op jit(solution)/shard_map/reduce_scatter | solution.py:823
  375.2 217.5 %reduce-scatter.10.cloned.1.call-start = ((), (), s32[]{:S(2)}) async-start(), calls=%async_computation.11 | async-start | bytes 5242880 | tf_op jit(solution)/shard_map/reduce_scatter | solution.py:902
  505.6 204.1 %reduce-scatter.14.cloned.1.call-start = ((), (), s32[]{:S(2)}) async-start(), calls=%async_computation.13 | async-start | bytes 3538944 | tf_op jit(solution)/shard_map/reduce_scatter | solution.py:823
  527.6 6.5 collective-permute-start.6
  552.6 5.6 collective-permute-start.7
  559.6 4.8 collective-permute-start.9
  559.6 4.8 collective-permute-start.10
  561.2 5.8 collective-permute-start.8
  592.8 128.7 %reduce-scatter.12.cloned.1.call-start = ((), (), s32[]{:S(2)}) async-start(), calls=%async_computation.12 | async-start | bytes 7077888 | tf_op jit(solution)/shard_map/reduce_scatter | solution.py:823
  703.0 18.6 %copy-start.2 = (f32[1024,512]{1,0:T(8,128)S(1)}, f32[1024,512]{1,0:T(8,128)}, u32[]{:S(2)}) copy-start(f32[1024,512]{1,0:T(8,128)} %copy-done.1) | copy-start | bytes 6291460
  (43 other events, 174.9 us)
Sparse Core Ops, SparseCore 0:
  12.1 61.5 all-gather.4
  93.6 92.6 all-gather.6
  188.8 75.3 all-gather.8
  265.9 45.5 all-gather.10
  355.4 61.6 reduce-scatter.5
  420.9 92.3 reduce-scatter.7
  515.7 76.9 reduce-scatter.9
  596.1 59.9 reduce-scatter.13
  659.8 61.6 reduce-scatter.11

commit v4 on v3

--- a/solution.py
+++ b/solution.py
@@ -150,7 +150,7 @@
         out_total[2:8, :] = jnp.zeros((6, carry_a.shape[1]), F32)
 
 
-def recur_forward(conv_in, same, prefix, params, decay_w, input_w, rows=128):
+def recur_forward(conv_in, same, prefix, params, decay_w, input_w, rows=256):
     length, width = conv_in.shape[0], params.shape[1]
     block = pl.BlockSpec((rows, width), lambda i: (i, 0))
     fixed = lambda shape: pl.BlockSpec(shape, lambda i: (0, 0))
@@ -182,12 +182,12 @@
 
 
 def adjoint_kernel(
-    gated_grad, gate_branch, hidden, retain,
+    middle_low, weight, gate_branch, hidden, retain,
     out_local, out_after, out_branch, out_pre_a, out_pre_b, out_total, out_dot,
     local_now, after_now, next_retain, grad_s,
 ):
     step = pl.program_id(0)
-    rows = gated_grad.shape[0]
+    rows = hidden.shape[0]
 
     @pl.when(step == 0)
     def _():
@@ -196,7 +196,7 @@
         next_retain[...] = jnp.ones_like(next_retain)
 
     value, slope = gelu_both(gate_branch[...])
-    upstream = gated_grad[...]
+    upstream = jnp.dot(middle_low[...], weight[...], preferred_element_type=F32)
     grad_s[...] = upstream * value
     branch = upstream * hidden[...] * slope
     out_branch[...] = branch.astype(BF)
@@ -227,8 +227,9 @@
         out_total[2:8, :] = jnp.zeros((6, carry_a.shape[1]), F32)
 
 
-def recur_adjoint(gated_grad, gate_branch, hidden, retain, rows=128):
-    length, width = gated_grad.shape
+def recur_adjoint(middle_low, w_recur, gate_branch, hidden, retain, rows=256):
+    length, width = hidden.shape
+    features = middle_low.shape[1]
     last = length // rows - 1
     block = pl.BlockSpec((rows, width), lambda i: (last - i, 0))
     second = pl.BlockSpec((rows, width), lambda i: (last - i, 1))
@@ -238,7 +239,11 @@
     return pl.pallas_call(
         adjoint_kernel,
         grid=(length // rows,),
-        in_specs=[block, second, block, block],
+        in_specs=[
+            pl.BlockSpec((rows, features), lambda i: (last - i, 0)),
+            pl.BlockSpec((features, width), lambda i: (0, 2), pipeline_mode=pl.Buffered(1)),
+            second, block, block,
+        ],
         out_specs=[block] * 3 + [fixed((SEGS, width))] * 3 + [pl.BlockSpec((rows, 128), lambda i: (last - i, 0))],
         out_shape=[big, big, jax.ShapeDtypeStruct((length, width), BF)]
         + [small] * 3
@@ -246,13 +251,13 @@
         scratch_shapes=[pltpu.VMEM((SEGS, width), F32)] * 3 + [pltpu.VMEM((rows, width), F32)],
         compiler_params=pltpu.CompilerParams(vmem_limit_bytes=LIMIT),
         cost_estimate=pl.CostEstimate(flops=length * width, bytes_accessed=4 * length * width, transcendentals=0),
-    )(gated_grad, gate_branch, hidden, retain)
+    )(middle_low, w_recur, gate_branch, hidden, retain)
 
 
 def backward_kernel(
     local, after, enter, hidden, hidden_before, carry, conv_out, decay_sig, gate_sig, retain, same, params, conv_in,
     decay_w, input_w,
-    out_decay, out_input, out_low, out_first, out_sums,
+    out_decay, out_input, out_low, out_dot, out_first, out_sums,
     next_one, next_two, next_three,
 ):
     step = pl.program_id(0)
@@ -302,6 +307,7 @@
         low = low + params[k : k + 1, :] * moved
         out_sums[8 * k : 8 * k + 8, :] += sums(moved * now)
     out_low[...] = low
+    out_dot[...] = jnp.broadcast_to(jnp.sum(low * now, axis=1, keepdims=True), out_dot.shape)
     out_sums[32:40, :] += sums(conv_grad)
     out_sums[40:48, :] += sums(decay_grad.astype(F32))
     out_sums[48:56, :] += sums(input_grad.astype(F32))
@@ -316,7 +322,7 @@
 
 def recur_backward(
     local, after, enter, hidden, carry, conv_out, decay_sig, gate_sig, retain, same, params, conv_in, decay_w, input_w,
-    rows=128,
+    rows=256,
 ):
     length, width = local.shape
     last = length // rows - 1
@@ -332,11 +338,15 @@
             pl.BlockSpec((rows, 8), lambda i: (last - i, 0)),
             fixed((8, width)), block, fixed((width, width)), fixed((width, width)),
         ],
-        out_specs=[block, block, block, fixed((48, width)), fixed((64, width))],
+        out_specs=[
+            block, block, block, pl.BlockSpec((rows, 128), lambda i: (last - i, 0)), fixed((48, width)),
+            fixed((64, width)),
+        ],
         out_shape=[
             jax.ShapeDtypeStruct((length, width), BF),
             jax.ShapeDtypeStruct((length, width), BF),
             jax.ShapeDtypeStruct((length, width), F32),
+            jax.ShapeDtypeStruct((length, 128), F32),
             jax.ShapeDtypeStruct((48, width), F32),
             jax.ShapeDtypeStruct((64, width), F32),
         ],
@@ -353,6 +363,120 @@
     )
 
 
+class Halving:
+    def __init__(self, source, keep, arrivals, sends, receives, loads):
+        self.source, self.keep, self.arrivals = source, keep, arrivals
+        self.sends, self.receives, self.loads = sends, receives, loads
+        rows, seqs = lax.axis_size("row"), lax.axis_size("seq")
+        self.total = rows * seqs
+        self.place = lax.axis_index("seq") * rows + lax.axis_index("row")
+        self.stages = halving_stages()
+        self.height = source.shape[0] // self.total
+
+    def own_bit(self, p):
+        axis, step = self.stages[p]
+        return lax.rem(lax.axis_index(axis) // step, 2)
+
+    def block(self, p, mine, j):
+        bit = self.own_bit(p) if mine else 1 - self.own_bit(p)
+        return lax.rem(self.place, 2**p) + bit * 2**p + j * 2 ** (p + 1)
+
+    def many(self, p):
+        return self.total // 2 ** (p + 1)
+
+    def held(self, p, mine, j):
+        return self.keep.at[self.block(p, mine, j) // 2]
+
+    def rows_of(self, block):
+        return self.source.at[pl.ds(pl.multiple_of(block * self.height, self.height), self.height)]
+
+    def moves(self, p):
+        axis, step = self.stages[p]
+        partner = lax.axis_index(axis) + step - 2 * step * self.own_bit(p)
+        start = self.total - self.total // 2**p
+        copies = []
+        for j in range(self.many(p)):
+            copies.append(
+                pltpu.make_async_remote_copy(
+                    src_ref=self.held(p, False, j) if p else self.rows_of(self.block(0, False, j)),
+                    dst_ref=self.arrivals.at[start + j],
+                    send_sem=self.sends.at[start + j],
+                    recv_sem=self.receives.at[start + j],
+                    device_id={axis: partner},
+                    device_id_type=pl.DeviceIdType.MESH,
+                )
+            )
+        return copies
+
+    def local(self):
+        return [
+            pltpu.make_async_copy(self.rows_of(self.block(0, True, j)), self.keep.at[j], self.loads.at[j])
+            for j in range(self.many(0))
+        ]
+
+    def begin(self):
+        for copy in self.moves(0) + self.local():
+            copy.start()
+
+    def stage(self, p, out=None):
+        if p == 0:
+            for copy in self.local():
+                copy.wait()
+        for copy in self.moves(p):
+            copy.wait_recv()
+        start = self.total - self.total // 2**p
+        piece = 32
+        for j in range(self.many(p)):
+            slot = self.block(p, True, j) // 2
+
+            def add(i, _, j=j, slot=slot):
+                at = pl.ds(pl.multiple_of(i * piece, piece), piece)
+                added = self.keep[slot, at, :].astype(F32) + self.arrivals[start + j, at, :].astype(F32)
+                if out is None:
+                    self.keep[slot, at, :] = added.astype(BF)
+                else:
+                    out[at, :] = added
+                return 0
+
+            lax.fori_loop(0, self.height // piece, add, 0)
+        if out is None:
+            for copy in self.moves(p + 1):
+                copy.start()
+
+    def settle(self):
+        for p in range(len(self.stages)):
+            for copy in self.moves(p):
+                copy.wait_send()
+
+    def partners(self):
+        found = []
+        for p, (axis, step) in enumerate(self.stages):
+            found.append({axis: lax.axis_index(axis) + step - 2 * step * self.own_bit(p)})
+        return found
+
+
+def halving_stages():
+    stages = []
+    for axis in ("row", "seq"):
+        step = 1
+        while step < lax.axis_size(axis):
+            stages.append((axis, step))
+            step *= 2
+    return stages
+
+
+def halving_scratch(shape):
+    total = lax.axis_size("row") * lax.axis_size("seq")
+    height = shape[0] // total
+    return [
+        pltpu.VMEM((total // 2, height, shape[1]), BF),
+        pltpu.VMEM((total - 1, height, shape[1]), BF),
+        pltpu.SemaphoreType.DMA((total - 1,)),
+        pltpu.SemaphoreType.DMA((total - 1,)),
+        pltpu.SemaphoreType.DMA((total // 2,)),
+    ]
+
+
 def exchange_kernel(count, chunks, mode, *refs):
     backward, summing, gathering = mode in ("back", "last"), mode != "first", mode != "last"
     refs = list(refs)
@@ -363,12 +487,14 @@
         states, products, gates, carry, weight, residual, gain, out, out_scale, out_own, out_hidden, out_gated = take(12)
         (gathered,) = take(1)
     elif mode == "back":
-        grads, weight, residual, middle, scale, mean, gain, out, out_own, out_gain = take(10)
+        grads, weight, residual, middle, scale, mean, gain, spread_in, out, out_own, out_gain, out_spread = take(12)
         gathered = out
+        halving = Halving(spread_in, *take(5))
     else:
-        grads, weight, residual, middle, scale, mean, gain, small, feed_sums, out_own, out_small, out_gains = take(12)
-        out_gain, gain_own, gain_row, gain_seq, small_own, small_row, small_seq = take(7)
-        gain_sems, small_sems = take(2)
+        grads, weight, residual, middle, scale, mean, gain, small, feed_sums, spread_in = take(10)
+        out_own, out_small, out_gains, out_spread = take(4)
+        halving = Halving(spread_in, *take(5))
+        out_gain, gain_own, gain_row, gain_seq, small_held, small_got, gain_sems, small_sems = take(8)
     if summing:
         partial, held_weight, right, left, total, weight_sem, sum_send, sum_recv = take(8)
     if gathering:
@@ -384,6 +510,9 @@
         load.start()
     barrier = pltpu.get_barrier_semaphore()
     if gathering:
+        partners = halving.partners() if mode == "back" else []
+        for partner in partners:
+            pl.semaphore_signal(barrier, inc=1, device_id=partner, device_id_type=pl.DeviceIdType.MESH)
 
         @pl.when(me > 0)
         def _():
@@ -397,11 +526,14 @@
 
         @pl.when(inner)
         def _():
-            pl.semaphore_wait(barrier, 2)
+            pl.semaphore_wait(barrier, 2 + len(partners))
 
         @pl.when(jnp.logical_not(inner))
         def _():
-            pl.semaphore_wait(barrier, 1)
+            pl.semaphore_wait(barrier, 1 + len(partners))
+
+        if mode == "back":
+            halving.begin()
 
     else:
         for axis in ("row", "seq", "rep"):
@@ -427,15 +559,33 @@
         return copies
 
     if mode == "last":
-        small_rows = to_peers("row", small_own, lambda d: small_row.at[d], small_sems.at[0])
-        small_seqs = to_peers("seq", small_row.at[0], lambda d: small_seq.at[d], small_sems.at[1])
+        small_moves = [
+            pltpu.make_async_remote_copy(
+                src_ref=small_held.at[p],
+                dst_ref=small_got.at[p],
+                send_sem=small_sems.at[0, p],
+                recv_sem=small_sems.at[1, p],
+                device_id=partner,
+                device_id_type=pl.DeviceIdType.MESH,
+            )
+            for p, partner in enumerate(halving.partners())
+        ]
         gain_rows = to_peers("row", gain_own, lambda d: gain_row.at[d], gain_sems.at[0])
         gain_seqs = to_peers("seq", gain_row.at[0], lambda d: gain_seq.at[d], gain_sems.at[1])
         own_gains = out_gains.at[:, pl.ds(pl.multiple_of(me * width, width), width)]
         gain_reps = to_peers("rep", gain_seq.at[0], lambda d: own_gains, gain_sems.at[2])
-        small_own[...] = small[...]
-        for copy in small_rows:
-            copy.start()
+        small_held[0] = small[...]
+        small_moves[0].start()
+        halving.begin()
+
+    def small_stage(p):
+        small_moves[p].wait_recv()
+        added = small_held[p].astype(F32) + small_got[p].astype(F32)
+        if p + 1 < len(small_moves):
+            small_held[p + 1] = added.astype(BF)
+            small_moves[p + 1].start()
+        else:
+            out_small[...] = added
 
     if backward:
         out_gain[...] = jnp.zeros_like(out_gain)
@@ -513,18 +663,21 @@
         partial[some, :] = back_dot(low, held_weight[...]).astype(BF)
 
     def tick(now, _):
+        if backward:
+            for p, when in ((0, 2), (1, 15 if mode == "back" else 13)):
+                if p < len(halving.stages) - 1:
+
+                    @pl.when(now == when)
+                    def _(p=p):
+                        halving.stage(p)
+
         if mode == "last":
-
-            @pl.when(now == chunks - 2)
-            def _():
-                for copy in small_rows:
-                    copy.wait_recv()
-                added = small_own[...].astype(F32)
-                for d in range(1, lax.axis_size("row")):
-                    added = added + small_row[d].astype(F32)
-                small_row[0] = added.astype(BF)
-                for copy in small_seqs:
-                    copy.start()
+            for p, when in ((0, 1), (1, 8)):
+                if p < len(small_moves) - 1:
+
+                    @pl.when(now == when)
+                    def _(p=p):
+                        small_stage(p)
 
         if summing:
 
@@ -643,18 +796,20 @@
 
         return 0
 
+    if backward:
+        for p in range(2, len(halving.stages) - 1):
+            halving.stage(p)
+        halving.stage(len(halving.stages) - 1, out_spread)
+        halving.settle()
+
     if mode == "last":
         mixer_sum = jnp.sum(out_gain[...], axis=0, keepdims=True)
         feed_sum = jnp.sum(feed_sums[...], axis=0, keepdims=True)
         gain_own[...] = jnp.concatenate([mixer_sum, feed_sum, jnp.zeros((6, width), F32)], axis=0)
         for copy in gain_rows:
             copy.start()
-        for copy in small_seqs:
-            copy.wait_recv()
-        added = small_row[0].astype(F32)
-        for d in range(1, lax.axis_size("seq")):
-            added = added + small_seq[d].astype(F32)
-        out_small[...] = added
+        for p in range(min(2, len(small_moves) - 1), len(small_moves)):
+            small_stage(p)
         for copy in gain_rows:
             copy.wait_recv()
         added = gain_own[...]
@@ -674,7 +829,7 @@
         own_gains[...] = added
         for copy in gain_reps:
             copy.wait_recv()
-        for copy in small_rows + small_seqs + gain_rows + gain_seqs + gain_reps:
+        for copy in small_moves + gain_rows + gain_seqs + gain_reps:
             copy.wait_send()
 
     lax.fori_loop(0, chunks, settle, 0)
@@ -704,20 +859,26 @@
             jax.ShapeDtypeStruct(small, F32),
             jax.ShapeDtypeStruct((8, features), F32),
         ]
+    if backward:
+        spread = operands[-1].shape
+        devices = lax.axis_size("row") * lax.axis_size("seq")
+        out_shape.append(jax.ShapeDtypeStruct((spread[0] // devices, spread[1]), F32))
     scratch = [] if backward else [pltpu.VMEM((length, features), BF)]
+    if backward:
+        in_specs[-1] = pl.BlockSpec(memory_space=pl.ANY)
+        scratch += halving_scratch(operands[-1].shape)
     if mode == "last":
-        row, seq = lax.axis_size("row"), lax.axis_size("seq")
+        row, seq, stages = lax.axis_size("row"), lax.axis_size("seq"), len(halving_stages())
         most = max(row, seq, count)
         scratch += [
             pltpu.VMEM((8, width), F32),
             pltpu.VMEM((8, width), F32),
             pltpu.VMEM((row, 8, width), F32),
             pltpu.VMEM((seq, 8, width), F32),
-            pltpu.VMEM(small, BF),
-            pltpu.VMEM((row,) + small, BF),
-            pltpu.VMEM((seq,) + small, BF),
+            pltpu.VMEM((stages,) + small, BF),
+            pltpu.VMEM((stages,) + small, BF),
             pltpu.SemaphoreType.DMA((3, 2, most)),
-            pltpu.SemaphoreType.DMA((2, 2, most)),
+            pltpu.SemaphoreType.DMA((2, stages)),
         ]
     if summing:
         in_specs[4 if mode == "norm" else 1] = pl.BlockSpec(memory_space=pl.ANY)
@@ -738,7 +899,9 @@
         out_shape=out_shape,
         scratch_shapes=scratch,
         compiler_params=pltpu.CompilerParams(
-            collective_id=("first", "norm", "back", "last").index(mode), has_side_effects=True, vmem_limit_bytes=LIMIT
+            collective_id=("first", "norm", "back", "last").index(mode),
+            has_side_effects=True,
+            vmem_limit_bytes=LIMIT + (8 * 1024 * 1024 if mode == "back" else 0),
         ),
         cost_estimate=pl.CostEstimate(
             flops=10 * length * features, bytes_accessed=160 * length * features, transcendentals=0
@@ -746,12 +909,32 @@
     )(*operands)
 
 
-def feed_kernel(cot, pre_gate, pre_up, down, out_low, out_grads, out_dot):
+def feed_kernel(normed_mid, cot, weights, out_low, out_grads, out_part, out_dot, held, sems):
     half = out_low.shape[1]
-    upstream = jnp.dot(cot[...], down[...], preferred_element_type=F32)
-    gate_pre, up_pre = pre_gate[...], pre_up[...]
+    step = pl.program_id(0)
+    loads = [
+        pltpu.make_async_copy(weights.at[:, pl.ds(k * half, half)], held.at[k], sems.at[k]) for k in range(3)
+    ]
+
+    @pl.when(step == 0)
+    def _():
+        for load in loads:
+            load.start()
+
+    def weight(k):
+        @pl.when(step == 0)
+        def _():
+            loads[k].wait()
+
+        return held[k]
+
+    gate_pre = jnp.dot(normed_mid[...], weight(0), preferred_element_type=F32)
+    up_pre = jnp.dot(normed_mid[...], weight(1), preferred_element_type=F32)
     value, slope = gelu_both(gate_pre)
-    out_low[...] = (value * up_pre).astype(BF)
+    low = (value * up_pre).astype(BF)
+    out_low[...] = low
+    upstream = jnp.dot(cot[...], weight(2), preferred_element_type=F32)
+    out_part[...] = back_dot(low, held[2]).astype(BF)
     gate_grad, up_grad = upstream * up_pre * slope, upstream * value
     out_grads[:, :half] = gate_grad.astype(BF)
     out_grads[:, half:] = up_grad.astype(BF)
@@ -759,28 +942,27 @@
     out_dot[...] = jnp.broadcast_to(dots, out_dot.shape)
 
 
-def feed_backward(cot, pre, down, rows=256):
+def feed_both(normed_mid, cot, weights, rows=256):
     length, features = cot.shape
-    half = down.shape[1]
-    block = lambda width, column=0: pl.BlockSpec((rows, width), lambda i: (i, column))
+    half = weights.shape[1] // 3
+    block = lambda width: pl.BlockSpec((rows, width), lambda i: (i, 0))
     return pl.pallas_call(
         feed_kernel,
         grid=(length // rows,),
-        in_specs=[
-            block(features), block(half), block(half, 1),
-            pl.BlockSpec((features, half), lambda i: (0, 0), pipeline_mode=pl.Buffered(1)),
-        ],
-        out_specs=[block(half), block(2 * half), block(128)],
+        in_specs=[block(features), block(features), pl.BlockSpec(memory_space=pl.ANY)],
+        out_specs=[block(half), block(2 * half), block(features), block(128)],
         out_shape=[
             jax.ShapeDtypeStruct((length, half), BF),
             jax.ShapeDtypeStruct((length, 2 * half), BF),
+            jax.ShapeDtypeStruct((length, features), BF),
             jax.ShapeDtypeStruct((length, 128), F32),
         ],
+        scratch_shapes=[pltpu.VMEM((3, features, half), BF), pltpu.SemaphoreType.DMA((3,))],
         compiler_params=pltpu.CompilerParams(vmem_limit_bytes=LIMIT),
         cost_estimate=pl.CostEstimate(
-            flops=2 * length * features * half, bytes_accessed=40 * length * half, transcendentals=length * half
+            flops=8 * length * features * half, bytes_accessed=12 * features * half, transcendentals=length * half
         ),
-    )(cot, pre, pre, down)
+    )(normed_mid, cot, weights)
 
 
 def per_segment(small, length):
@@ -836,11 +1018,12 @@
     x_low = by_step(block_input[0])
     cot_own = by_step(cotangent[0] * pad_mask[0][:, None].astype(BF))
     mixer_own, feed_own = own_part(mixer_gain), own_part(feed_gain)
+    recur_shard = jnp.concatenate([wide(recur_input), wide(recur_gate), wide(recur_output)], axis=1)
+    recur_shard, cot_own, x_low = after((recur_shard, cot_own, x_low))
+    w_recur = weights(recur_shard)
     normed, s1 = exchange("first", (x_low, mixer_gain[None]), own_width)
-    w_recur = weights(jnp.concatenate([wide(recur_input), wide(recur_gate), wide(recur_output)], axis=1))
-    cot_own, normed, w_recur = after((cot_own, normed, w_recur))
     cot = lax.all_gather(cot_own, "rep", axis=1, tiled=True)
-    w_input, w_output = w_recur[:, : 2 * width], w_recur[:, 2 * width :]
+    w_input = w_recur[:, : 2 * width]
 
     left_ids = lax.ppermute(segment_ids[:, -edge:].astype(F32), "seq", to_next).astype(jnp.int32)
     left_ids = jnp.where(at_start, jnp.broadcast_to(segment_ids[:, :1], left_ids.shape), left_ids)
@@ -855,11 +1038,8 @@
     state_init = wide(state_init)
 
     projected = dot(normed, w_input)
-    feed_shard, feed_down, projected = after(
-        (jnp.concatenate([feed_gate, feed_up], axis=1), feed_down, projected)
-    )
+    feed_shard, projected = after((jnp.concatenate([feed_gate, feed_up, feed_down], axis=1), projected))
     w_feed = weights(feed_shard)
-    w_down = weights(feed_down)
     ends = projected[-edge * SEGS :, :width].astype(BF).reshape(edge, SEGS, width)
     left = lax.ppermute(ends[:, -1], "seq", to_next)
     left = jnp.where(at_start, wide(window_init[0]), left)
@@ -880,37 +1060,33 @@
         "norm", (states, products, gates, carry, w_recur, x_low, feed_gain[None]), own_width
     )
     normed_mid, cot = after((normed_mid, cot))
-    pre = dot(normed_mid, w_feed)
-    feed_low, feed_grads, mid_mean = feed_backward(cot, pre, w_down)
+    feed_low, feed_grads, feed_part, mid_mean = feed_both(normed_mid, cot, w_feed)
     mid_mean = small_sum(mid_mean[:, 0].reshape(8, -1), "rep").reshape(-1, 1) / features
 
-    half = w_down.shape[1]
-    feed_part = back_dot(feed_low, w_down).astype(BF)
-    feed_low, feed_part = after((feed_low, feed_part))
+    half = feed_down.shape[1]
     down_grad = rows_dot(cot, feed_low).astype(BF)
     feed_grads, down_grad, mid_mean = after((feed_grads, down_grad, mid_mean))
     feed_all = rows_dot(normed_mid, feed_grads).astype(BF)
-    feed_grads, feed_all = after((feed_grads, feed_all))
-    down_grad, feed_all = spread(down_grad), spread(feed_all)
-    middle_low, middle_grad, feed_gain_own = exchange(
+    feed_grads, feed_all, feed_part = after((feed_grads, feed_all, feed_part))
+    feed_out = lax.psum_scatter(feed_part, "rep", scatter_dimension=1, tiled=True)
+    feed_all = spread(feed_all)
+    middle_low, middle_grad, feed_gain_own, feed_down_grad = exchange(
         "back",
-        (feed_grads, w_feed, cot_own, middle, s2, jnp.broadcast_to(mid_mean, (length, 128)), feed_own),
+        (feed_grads, w_feed, cot_own, middle, s2, jnp.broadcast_to(mid_mean, (length, 128)), feed_own, down_grad),
         own_width,
     )
 
-    feed_part, middle_low = after((feed_part, middle_low))
-    feed_out = lax.psum_scatter(feed_part, "rep", scatter_dimension=1, tiled=True)
-    gated_grad = dot(middle_low, w_output)
     local, after_prod, branch_grad, enter_a, enter_b, back_total, branch_dot = recur_adjoint(
-        gated_grad, projected, hidden, retain
+        middle_low, w_recur, projected, hidden, retain
     )
     output_all = rows_dot(middle_low, gated).astype(BF)
+    local, output_all = after((local, output_all))
     entering = jnp.zeros_like(state_init)
     for k in range(1, seqs):
         arriving = lax.ppermute(back_total[0:1] * entering + back_total[1:2], "seq", to_last)
         entering = jnp.where(seq == seqs - 1 - k, arriving, entering)
     enter = enter_a * entering + enter_b
-    decay_grad, input_grad_low, low_grad, first, sums = recur_backward(
+    decay_grad, input_grad_low, low_grad, low_dot, first, sums = recur_backward(
         local, after_prod, enter, hidden, carry, conv_out, decay_sig, gate_sig, retain, same, params, projected,
         decay_w, input_w,
     )
@@ -927,12 +1103,12 @@
     share = jnp.concatenate([back_share[:, 1:], from_right[:, None]], axis=1)
     low_grad = low_grad.reshape(length // SEGS, SEGS, -1)
     low_grad = jnp.concatenate([low_grad[:-edge], low_grad[-edge:] + share], axis=0).reshape(length, -1)
-    in_mean = jnp.sum(low_grad * projected[:, :width].astype(BF).astype(F32), axis=1) + branch_dot[:, 0]
+    share_dot = jnp.sum(share * ends.astype(F32), axis=2).reshape(-1)
+    in_mean = low_dot[:, 0] + branch_dot[:, 0] + jnp.pad(share_dot, (length - share_dot.shape[0], 0))
     in_mean = small_sum(in_mean.reshape(8, -1), "rep").reshape(-1, 1) / features
 
     both_grads = jnp.concatenate([low_grad.astype(BF), branch_grad], axis=1)
-    both_grads, in_mean, down_grad, feed_all = after((both_grads, in_mean, down_grad, feed_all))
-    feed_down_grad = down_grad.astype(F32)
+    both_grads, in_mean, feed_all = after((both_grads, in_mean, feed_all))
     feed_gate_grad, feed_up_grad = feed_all[:, :half].astype(F32), feed_all[:, half:].astype(F32)
     conv_low = conv_out.astype(BF)
     decay_gate_grad = diagonal_rows(rows_dot(conv_low, decay_grad), heads, head_width)
@@ -945,18 +1121,20 @@
     parts = (decay_gate_grad, input_gate_grad, vectors)
     small, counts = join_small(parts)
     recur_raw = rows_dot(normed, both_grads).astype(BF)
-    both_grads, recur_raw, output_all, feed_out = after((both_grads, recur_raw, output_all, feed_out))
-    output_all, recur_all = spread(output_all), spread(recur_raw)
-    input_grad, summed, gains = exchange(
+    recur_all = spread(recur_raw)
+    both_grads, recur_raw, small, feed_out, feed_gate_grad, feed_up_grad = after(
+        (both_grads, recur_raw, small, feed_out, feed_gate_grad, feed_up_grad)
+    )
+    input_grad, summed, gains, output_all = exchange(
         "last",
         (
             both_grads, w_recur, middle_grad, x_low, s1, jnp.broadcast_to(in_mean, (length, 128)), mixer_own,
-            small, feed_gain_own,
+            small, feed_gain_own, output_all,
         ),
         own_width,
     )
-    input_grad, feed_out, recur_all, output_all = after((input_grad, feed_out, recur_all, output_all))
-    recur_output_grad = output_all[:, :channels].astype(F32)
+    input_grad, feed_out, recur_all = after((input_grad, feed_out, recur_all))
+    recur_output_grad = output_all[:, :channels]
     recur_input_grad = recur_all[:, :channels].astype(F32)
     recur_gate_grad = recur_all[:, width : width + channels].astype(F32)
     input_grad = by_segment(input_grad)[None]

time: 744 us -> 681 us (0.915)
  matrix products: 102 us -> 62.8 us
  waiting for transfers between devices: 39.8 us -> 7.18 us
  Pallas kernels: 493 us -> 505 us
    dot_general x3 -> x1, matrix products: 39 us -> 11.7 us  [dot(): return jnp.dot(left, right, preferred_element_type=F32)]
    pallas_call x2, Pallas kernels: 28.1 us -> 48.1 us  [the longest x1 37.1 us: feed_both(): pl.pallas_call(feed_kernel, grid=(length // rows,), in_specs=[block(featu...]
    reduce_scatter x1, waiting for transfers between devices: 14.1 us -> 0.01 us  [shards(): lax.psum_scatter(feed_part, 'rep', scatter_dimension=1, tiled=True)]
    reduce_scatter x4 -> x2, waiting for transfers between devices: 11.9 us -> 0.01 us  [spread(): lax.psum_scatter(partial_grad, ('seq', 'row'), scatter_dimension=0, tiled...]
    dot_general x1 -> x0, matrix products: 10.1 us -> none  [back_dot(): lax.dot_general(left, right, (((1,), (1,)), ((), ())), preferred_element_...]
    unnamed x127 -> x132, local copies, waits for them, and re-layouts: 30.1 us -> 26.4 us
  transfers between devices with their start and end apart: 20 -> 17, of which waited for: 8 -> 3; matrix products, arithmetic and copies ran while one was open for 18% -> 11% of each run, Pallas kernels for 65% -> 70%
where the time goes in v4:
time: 681 us; the launch traced here: 673 us
  Pallas kernels  505 us (74%)
  matrix products  62.8 us (9%)
  local copies, waits for them, and re-layouts  42.2 us (6%)
  starting transfers between devices  22.2 us (3%)
  other arithmetic  17.7 us (3%)
  between operations  15.6 us (2%)
  waiting for transfers between devices  7.18 us (1%)
    pallas_call x4, Pallas kernels, exchange(): pl.pallas_call(partial_call(exchange_kernel, count, chunks, mode), in_spe...  428 us
    dot_general x6, matrix products, rows_dot(): lax.dot_general(left, right, (((0,), (0,)), ((), ())), preferred_element_...  51 us
    pallas_call x1, Pallas kernels, feed_both(): pl.pallas_call(feed_kernel, grid=(length // rows,), in_specs=[block(featu...  37.1 us
    unnamed x132, local copies, waits for them, and re-layouts  26.4 us
    pallas_call x1, Pallas kernels, recur_backward(): pl.pallas_call(backward_kernel, grid=(length // rows,), in_specs=[block,...  15.2 us
    pallas_call x1, Pallas kernels, recur_forward(): pl.pallas_call(forward_kernel, grid=(length // rows,), in_specs=[block, p...  13.9 us
  transfers between devices with their start and end apart: 17, of which 3 were waited for; matrix products, arithmetic and copies ran while one was open for 11% of the time, Pallas kernels for 70%

profile of v4, /device:TPU:0, one launch (start us, length us, event | category | flops | bytes accessed | tf_op | source)
XLA Modules:
  0.0 673.0 jit_solution(1941620786104283693)
XLA Ops:
  12.8 2.2 copy_bitcast_fusion
  15.9 75.7 %shard_map.348 = (bf16[1024,2048]{1,0:T(8,128)(2,1)S(1)}, f32[1024,128]{1,0:T(8,128)S(1)}) custom-call(bf16[1024,512]{1,0:T(8,128)(2,1)S(1)} %get-tuple-element.87.refs_0_.refs_5_.refs_3_, f32[1,2048]{1,0:T(1,128)S(1)} %bitcast.124), custom_call_target="tpu_custom_call" | custom-call | flops 20971520 | bytes 335544320 | tf_op jit(solution)/shard_map/pallas_call | solution.py:895
  92.4 2.1 copy-done.19
  96.0 11.7 %fusion.conv_in.gate_branch = f32[1024,1536]{1,0:T(8,128)} fusion(bf16[1024,2048]{1,0:T(8,128)(2,1)} %copy-done.19, bf16[2048,2304]{1,0:T(8,128)(2,1)} %all-gather.4.cloned.1.call-done.refs_4_.weight.refs_1_), kind=kOutput, calls=%fused_computation.3 | convolution fusion | flops 6442450944 | bytes 16777216 | tf_op jit(solution)/shard_map/dot_general | solution.py:981
  108.5 3.4 collective-permute-start
  116.2 3.9 collective-permute-start.1
  123.0 13.9 %shard_map.349 = (f32[1024,768]{1,0:T(8,128)S(1)}, f32[1024,768]{1,0:T(8,128)}, f32[1024,768]{1,0:T(8,128)}, f32[1024,768]{1,0:T(8,128)}, f32[1024,768]{1,0:T(8,...) custom-call(f32[1024,1536]{1,0:T(8,128)} %fusion.conv_in.gate_branch, ...), custom_call_target="tpu_custom_call" | custom-call | flops 786432 | bytes 3145728 | tf_op jit(solution)/shard_map/pallas_call | solution.py:159
  136.9 1.7 copy-done.5
  139.3 4.7 collective-permute-start.2
  145.9 123.9 %shard_map.350 = (bf16[1024,2048]{1,0:T(8,128)(2,1)}, f32[1024,128]{1,0:T(8,128)S(1)}, f32[1024,512]{1,0:T(8,128)S(1)}, f32[1024,768]{1,0:T(8,128)}, bf16[1024,768]{1,0:T(8,128)(2,1)S(1)}) custom-call(f32[1024,768]{1,0:T(8,128)} %get-tuple-element.91.refs_0_, f32[1024,768]{1,0:T(8,128)} %get-tuple-element.92.refs_1_, f32[1024,768]{1,0:T(8,128)} %copy-done.5, ...), custom_call_target="tpu_custom_call" | custom-call | flops 20971520 | bytes 335544320 | tf_op jit(solution)/shard_map/pallas_call | solution.py:895
  273.7 37.1 %shard_map.351 = (bf16[1024,1536]{1,0:T(8,128)(2,1)S(1)}, bf16[1024,3072]{1,0:T(8,128)(2,1)}, bf16[1024,2048]{1,0:T(8,128)(2,1)}, f32[1024,128]{1,0:T(8,128)S(1)}) custom-call(bf16[1024,2048]{1,0:T(8,128)(2,1)} %get-tuple-element.100.normed_mid, bf16[1024,2048]{1,0:T(8,128)(2,1)} %all-gather.6.cloned.1.call-done.cot, ...), custom_call_target="tpu_custom_call" | custom-call | flops 25769803776 | bytes 37748736 | tf_op jit(solution)/shard_map/pallas_call | solution.py:949
  311.1 2.4 collective-permute-start.5
  314.2 11.2 %convolution_convert_fusion.2.refs_7_ = bf16[2048,1536]{1,0:T(8,128)(2,1)} fusion(bf16[1024,2048]{1,0:T(8,128)(2,1)} %all-gather.6.cloned.1.call-done.cot, bf16[1024,1536]{1,0:T(8,128)(2,1)S(1)} %get-tuple-element.104), kind=kOutput, calls=%fused_computation.2 | convolution fusion | flops 6445596672 | bytes 13631488 | tf_op jit(solution)/shard_map/dot_general | solution.py:973
  325.4 18.4 %convolution_convert_fusion = bf16[2048,3072]{1,0:T(8,128)(2,1)} fusion(bf16[1024,2048]{1,0:T(8,128)(2,1)} %get-tuple-element.100.normed_mid, bf16[1024,3072]{1,0:T(8,128)(2,1)S(1)} %bitcast.127), kind=kOutput, calls=%fused_computation | convolution fusion | flops 12891193344 | bytes 23068672 | tf_op jit(solution)/shard_map/dot_general | solution.py:973
  346.1 134.5 %shard_map.352 = (bf16[1024,2048]{1,0:T(8,128)(2,1)}, f32[1024,512]{1,0:T(8,128)}, f32[8,512]{1,0:T(8,128)}, f32[256,1536]{1,0:T(8,128)}) custom-call(bf16[1024,3072]{1,0:T(8,128)(2,1)} %get-tuple-element.108.refs_0_, bf16[2048,4608]{1,0:T(8,128)(2,1)} %all-gather.8.cloned.1.call-done.weights.refs_1_, bf16[1024,512]{1,0:T(8,128)(2,1)} %get-tuple-element.99.refs_2_, ...), custom_call_target="tpu_custom_call" | custom-call | flops 20971520 | bytes 335544320 | tf_op jit(solution)/shard_map/pallas_call | solution.py:895
  480.7 10.9 %shard_map.353 = (f32[1024,768]{1,0:T(8,128)S(1)}, f32[1024,768]{1,0:T(8,128)}, bf16[1024,768]{1,0:T(8,128)(2,1)S(1)}, f32[8,768]{1,0:T(8,128)S(1)}, f32[8,768]{...) custom-call(bf16[1024,2048]{1,0:T(8,128)(2,1)} %get-tuple-element.112.middle_low, ...), custom_call_target="tpu_custom_call" | custom-call | flops 786432 | bytes 3145728 | tf_op jit(solution)/shard_map/pallas_call | solution.py:239
  491.6 1.7 copy-done.4
  494.6 5.0 convolution_convert_fusion.3.refs_9_
  499.7 15.2 %shard_map.354 = (bf16[1024,768]{1,0:T(8,128)(2,1)S(1)}, bf16[1024,768]{1,0:T(8,128)(2,1)}, f32[1024,768]{1,0:T(8,128)}, f32[1024,128]{1,0:T(8,128)S(1)}, f32[48,768]{1,0:T(8,128)S(1)}, /*index=5*/f32[64,768]{1,0:T(8,128)S(1)}) custom-call(f32[1024,768]{1,0:T(8,128)} %copy-done.4, f32[1024,768]{1,0:T(8,128)} %get-tuple-element.118.after, ...), custom_call_target="tpu_custom_call" | custom-call | flops 786432 | bytes 3145728 | tf_op jit(solution)/shard_map/pallas_call | solution.py:333
  516.4 2.0 fusion.6
  518.7 2.0 collective-permute-done.7
  521.8 1.9 collective-permute-start.9
  523.7 1.8 collective-permute-start.10
  527.0 2.0 pad_maximum_fusion.refs_0_
  529.0 2.5 collective-permute-done.8
  531.6 11.5 %convolution_convert_fusion.1 = bf16[2048,1536]{1,0:T(8,128)(2,1)} fusion(bf16[1024,2048]{1,0:T(8,128)(2,1)} %copy-done.19, bf16[1024,1536]{1,0:T(8,128)(2,1)} %pad_maximum_fusion.refs_0_), kind=kOutput, calls=%fused_computation.1 | convolution fusion | flops 6445596672 | bytes 13631488 | tf_op jit(solution)/shard_map/dot_general | solution.py:973
  545.7 3.5 convolution_convert_fusion.5
  552.3 2.1 slice_convert_fusion.1
  555.6 94.0 %shard_map.355 = (bf16[1024,512]{1,0:T(8,128)(2,1)S(1)}, f32[1440,256]{1,0:T(8,128)}, f32[8,2048]{1,0:T(8,128)S(1)}, f32[256,768]{1,0:T(8,128)S(1)}) custom-call(bf16[1024,1536]{1,0:T(8,128)(2,1)} %pad_maximum_fusion.refs_0_, bf16[2048,2304]{1,0:T(8,128)(2,1)} %all-gather.4.cloned.1.call-done.refs_4_.weight.refs_1_, f32[1024,512]{1,0:T(8,128)} %get-tuple-element.138.refs_2_, ...), custom_call_target="tpu_custom_call" | custom-call | flops 20971520 | bytes 335544320 | tf_op jit(solution)/shard_map/pallas_call | solution.py:895
  650.6 2.4 copy.108
  654.9 2.5 fusion.52
  658.1 1.6 fusion.9
  (241 shorter events, 47.8 us)
Async XLA Ops:
  7.2 88.8 %all-gather.4.cloned.1.call-start = ((), (), s32[]{:S(2)}) async-start(), calls=%async_computation.3 | async-start | bytes 10616832 | tf_op jit(solution)/shard_map/all_gather | solution.py:1002
  15.0 79.5 %copy-start.30 = (bf16[256,1536]{1,0:T(8,128)(2,1)S(1)}, bf16[256,1536]{1,0:T(8,128)(2,1)}, u32[]{:S(2)}) copy-start(bf16[256,1536]{1,0:T(8,128)(2,1)} %param.32) | copy-start | bytes 2359300
  15.0 79.5 %copy-start.31 = (bf16[256,1536]{1,0:T(8,128)(2,1)S(1)}, bf16[256,1536]{1,0:T(8,128)(2,1)}, u32[]{:S(2)}) copy-start(bf16[256,1536]{1,0:T(8,128)(2,1)} %param.31) | copy-start | bytes 2359300
  15.0 79.5 %copy-start.32 = (bf16[256,1536]{1,0:T(8,128)(2,1)S(1)}, bf16[256,1536]{1,0:T(8,128)(2,1)}, u32[]{:S(2)}) copy-start(bf16[256,1536]{1,0:T(8,128)(2,1)} %param.30) | copy-start | bytes 2359300
  15.0 258.6 %all-gather.6.cloned.1.call-start = ((), (), s32[]{:S(2)}) async-start(), calls=%async_computation.4 | async-start | bytes 5242880 | tf_op jit(solution)/shard_map/all_gather | solution.py:1025
  15.8 257.9 %all-gather.8.cloned.1.call-start = ((), (), s32[]{:S(2)}) async-start(), calls=%async_computation.5 | async-start | bytes 21233664 | tf_op jit(solution)/shard_map/all_gather | solution.py:1002
  107.8 423.7 %reduce-scatter.4.cloned.1.call-start = ((), (), s32[]{:S(2)}) async-start(), calls=%async_computation.6 | async-start | bytes 14155776 | tf_op jit(solution)/shard_map/reduce_scatter | solution.py:1005
  108.5 5.5 collective-permute-start
  113.2 8.8 %copy-start.12 = (f32[8,768]{1,0:T(8,128)}, f32[8,768]{1,0:T(8,128)S(1)}, u32[]{:S(2)}) copy-start(f32[8,768]{1,0:T(8,128)S(1)} %select_maximum_fusion.params) | copy-start | bytes 73732
  113.2 8.1 %copy-start.48 = (bf16[1,3,704]{2,1,0:T(4,128)(2,1)S(1)}, bf16[1,3,704]{2,1,0:T(4,128)(2,1)}, u32[]{:S(2)}) copy-start(bf16[1,3,704]{2,1,0:T(4,128)(2,1)} %param.26) | copy-start | bytes 12676
  115.6 5.8 copy-start.34
  116.2 5.1 collective-permute-start.1
  123.0 15.7 %copy-start.43 = (f32[1,704]{1,0:T(1,128)S(1)}, f32[1,704]{1,0:T(1,128)}, u32[]{:S(2)}) copy-start(f32[1,704]{1,0:T(1,128)} %param.25) | copy-start | bytes 8452
  123.0 22.9 %copy-start.17 = (f32[2048]{0:T(1024)S(1)}, f32[2048]{0:T(1024)}, u32[]{:S(2)}) copy-start(f32[2048]{0:T(1024)} %param.41) | copy-start | bytes 24580
  139.3 6.0 collective-permute-start.2
  310.8 14.6 %slice-start = ((s8[6291456]{0:T(1024)(128)(4,1)}), s8[2097152]{0:T(1024)(128)(4,1)S(1)}, s32[]{:S(2)}) async-start(s8[6291456]{0:T(1024)(128)(4,1)} %bitcast.126), calls=%async_computation.9 | async-start | bytes 4194304
  311.0 14.4 %collective-permute-start.4 = (f32[8,128]{1,0:T(8,128)S(1)}, f32[8,128]{1,0:T(8,128)S(1)}, u32[]{:S(2)}, u32[]{:S(2)}) collective-permute-start(f32[8,128]{1,0:T(8,128)S(1)} %bitcast.139), channel_id=1, source_target_pairs={{0,2},{1,3},{2,0},{3,1},{4,6},{5,7},{6,4},{7,5},{8,10},{9,11},{10,... | collective-permute-start | bytes 12296 | tf_op jit(solution)/shard_map/ppermute | solution.py:41
  311.1 14.3 %collective-permute-start.5 = (f32[8,128]{1,0:T(8,128)S(1)}, f32[8,128]{1,0:T(8,128)S(1)}, u32[]{:S(2)}, u32[]{:S(2)}) collective-permute-start(f32[8,128]{1,0:T(8,128)S(1)} %bitcast.140), channel_id=1, source_target_pairs={{0,3},{1,0},{2,1},{3,2},{4,7},{5,4},{6,5},{7,6},{8,11},{9,8},{10,9... | collective-permute-start | bytes 12296 | tf_op jit(solution)/shard_map/ppermute | solution.py:41
  313.5 11.9 %collective-permute-start.3 = (f32[8,128]{1,0:T(8,128)S(1)}, f32[8,128]{1,0:T(8,128)S(1)}, u32[]{:S(2)}, u32[]{:S(2)}) collective-permute-start(f32[8,128]{1,0:T(8,128)S(1)} %bitcast.141), channel_id=1, source_target_pairs={{0,1},{1,2},{2,3},{3,0},{4,5},{5,6},{6,7},{7,4},{8,9},{9,10},{10,1... | collective-permute-start | bytes 12296 | tf_op jit(solution)/shard_map/ppermute | solution.py:41
  314.2 11.2 %slice-start.1 = ((s8[6291456]{0:T(1024)(128)(4,1)}), s8[4194304]{0:T(1024)(128)(4,1)S(1)}, s32[]{:S(2)}) async-start(s8[6291456]{0:T(1024)(128)(4,1)} %bitcast.126), calls=%async_computation.10 | async-start | bytes 8388608
  343.8 210.6 %reduce-scatter.6.cloned.1.call-start = ((), (), s32[]{:S(2)}) async-start(), calls=%async_computation.7 | async-start | bytes 5242880 | tf_op jit(solution)/shard_map/reduce_scatter | solution.py:1071
  344.4 313.7 %reduce-scatter.8.cloned.1.call-start = ((), (), s32[]{:S(2)}) async-start(), calls=%async_computation.8 | async-start | bytes 7077888 | tf_op jit(solution)/shard_map/reduce_scatter | solution.py:1005
  480.6 13.9 %copy-start.23 = (bf16[1024,768]{1,0:T(8,128)(2,1)S(1)}, bf16[1024,768]{1,0:T(8,128)(2,1)}, u32[]{:S(2)}) copy-start(bf16[1024,768]{1,0:T(8,128)(2,1)} %copy-done.22) | copy-start | bytes 4718596
  480.6 13.9 %copy-start.24 = (bf16[1024,2048]{1,0:T(8,128)(2,1)S(1)}, bf16[1024,2048]{1,0:T(8,128)(2,1)}, u32[]{:S(2)}) copy-start(bf16[1024,2048]{1,0:T(8,128)(2,1)} %get-tuple-element.112.middle_low) | copy-start | bytes 12582916
  493.3 6.4 collective-permute-start.6
  499.7 15.3 %copy-start.35 = (bf16[3,8,768]{2,1,0:T(8,128)(2,1)S(1)}, bf16[3,8,768]{2,1,0:T(8,128)(2,1)}, u32[]{:S(2)}) copy-start(bf16[3,8,768]{2,1,0:T(8,128)(2,1)} %copy-done.34) | copy-start | bytes 110596
  499.7 15.3 %copy-start.40 = (bf16[3,1,768]{2,1,0:T(2,128)(2,1)S(1)}, bf16[3,1,768]{2,1,0:T(2,128)(2,1)}, u32[]{:S(2)}) copy-start(bf16[3,1,768]{2,1,0:T(2,128)(2,1)} %copy-done.39) | copy-start | bytes 13828
  515.1 5.6 collective-permute-start.7
  521.8 7.2 %collective-permute-start.9 = (f32[8,128]{1,0:T(8,128)S(1)}, f32[8,128]{1,0:T(8,128)S(1)}, u32[]{:S(2)}, u32[]{:S(2)}) collective-permute-start(f32[8,128]{1,0:T(8,128)S(1)} %add_bitcast_fusion), channel_id=1, source_target_pairs={{0,2},{1,3},{2,0},{3,1},{4,6},{5,7},{6,4},{7,5},{8,10},{9,11},{10,... | collective-permute-start | bytes 12296 | tf_op jit(solution)/shard_map/ppermute | solution.py:41
  523.7 5.3 collective-permute-start.10
  525.5 6.0 collective-permute-start.8
  650.6 7.5 %copy-start.1 = (f32[1024,512]{1,0:T(8,128)S(1)}, f32[1024,512]{1,0:T(8,128)}, u32[]{:S(2)}) copy-start(f32[1024,512]{1,0:T(8,128)} %copy-done) | copy-start | bytes 6291460
  (42 other events, 118.2 us)
Sparse Core Ops, SparseCore 0:
  15.2 61.5 all-gather.3
  78.9 82.0 all-gather.5
  162.8 101.9 all-gather.7
  343.9 128.4 reduce-scatter.3
  474.5 76.2 reduce-scatter.5
  554.5 79.3 reduce-scatter.7

commit v5 on v4

--- a/solution.py
+++ b/solution.py
@@ -32,24 +32,6 @@
 
 
 after = lax.optimization_barrier
-
-
-def small_sum(own, axis):
-    count = lax.axis_size(axis)
-    total = own
-    for k in range(1, count):
-        total = total + lax.ppermute(own, axis, [(i, (i + k) % count) for i in range(count)])
-    return total
-
-
-def small_gather(own, axis):
-    count, me = lax.axis_size(axis), lax.axis_index(axis)
-    width = own.shape[1]
-    total = lax.dynamic_update_slice(jnp.zeros((own.shape[0], count * width), own.dtype), own, (0, me * width))
-    for k in range(1, count):
-        piece = lax.ppermute(own, axis, [(i, (i + k) % count) for i in range(count)])
-        total = lax.dynamic_update_slice(total, piece, (0, lax.rem(me - k + count, count) * width))
-    return total
 
 
 def join_small(parts):
@@ -495,6 +477,8 @@
         out_own, out_small, out_gains, out_spread = take(4)
         halving = Halving(spread_in, *take(5))
         out_gain, gain_own, gain_row, gain_seq, small_held, small_got, gain_sems, small_sems = take(8)
+    if backward:
+        mean_got, mean_sum, mean_sems = take(3)
     if summing:
         partial, held_weight, right, left, total, weight_sem, sum_send, sum_recv = take(8)
     if gathering:
@@ -509,38 +493,39 @@
         load = pltpu.make_async_copy(weight.at[:, pl.ds(start, held_weight.shape[1])], held_weight, weight_sem)
         load.start()
     barrier = pltpu.get_barrier_semaphore()
-    if gathering:
-        partners = halving.partners() if mode == "back" else []
-        for partner in partners:
-            pl.semaphore_signal(barrier, inc=1, device_id=partner, device_id_type=pl.DeviceIdType.MESH)
+
+    def greet(device):
+        pl.semaphore_signal(barrier, inc=1, device_id=device, device_id_type=pl.DeviceIdType.MESH)
+
+    if backward:
+        axes = ("rep",) if mode == "back" else ("row", "seq", "rep")
+        devices = halving.partners() if mode == "back" else []
+        for axis in axes:
+            for d in range(1, lax.axis_size(axis)):
+                devices.append({axis: lax.rem(lax.axis_index(axis) + d, lax.axis_size(axis))})
+        for device in devices:
+            greet(device)
+        pl.semaphore_wait(barrier, len(devices))
+        halving.begin()
+    else:
 
         @pl.when(me > 0)
         def _():
-            pl.semaphore_signal(barrier, inc=1, device_id={"rep": me - 1}, device_id_type=pl.DeviceIdType.MESH)
+            greet({"rep": me - 1})
 
         @pl.when(me < last)
         def _():
-            pl.semaphore_signal(barrier, inc=1, device_id={"rep": me + 1}, device_id_type=pl.DeviceIdType.MESH)
+            greet({"rep": me + 1})
 
         inner = jnp.logical_and(me > 0, me < last)
 
         @pl.when(inner)
         def _():
-            pl.semaphore_wait(barrier, 2 + len(partners))
+            pl.semaphore_wait(barrier, 2)
 
         @pl.when(jnp.logical_not(inner))
         def _():
-            pl.semaphore_wait(barrier, 1 + len(partners))
-
-        if mode == "back":
-            halving.begin()
-
-    else:
-        for axis in ("row", "seq", "rep"):
-            for d in range(1, lax.axis_size(axis)):
-                peer = lax.rem(lax.axis_index(axis) + d, lax.axis_size(axis))
-                pl.semaphore_signal(barrier, inc=1, device_id={axis: peer}, device_id_type=pl.DeviceIdType.MESH)
-        pl.semaphore_wait(barrier, sum(lax.axis_size(axis) - 1 for axis in ("row", "seq", "rep")))
+            pl.semaphore_wait(barrier, 1)
 
     def to_peers(axis, source, target, sems):
         copies = []
@@ -557,6 +542,18 @@
                 )
             )
         return copies
+
+    if backward:
+        mean_moves = to_peers("rep", mean, lambda d: mean_got.at[d], mean_sems)
+        for copy in mean_moves:
+            copy.start()
+
+    def mean_column(c):
+        per = 128 // rows
+        line = jnp.broadcast_to(mean_sum[pl.ds(c // per, 1), :], (rows, 128))
+        lane = lax.broadcasted_iota(jnp.int32, (rows, 128), 1)
+        row = lax.broadcasted_iota(jnp.int32, (rows, 128), 0) + lax.rem(c, per) * rows
+        return jnp.sum(jnp.where(lane == row, line, 0.0), axis=1, keepdims=True)
 
     if mode == "last":
         small_moves = [
@@ -576,7 +573,6 @@
         gain_reps = to_peers("rep", gain_seq.at[0], lambda d: own_gains, gain_sems.at[2])
         small_held[0] = small[...]
         small_moves[0].start()
-        halving.begin()
 
     def small_stage(p):
         small_moves[p].wait_recv()
@@ -664,6 +660,16 @@
 
     def tick(now, _):
         if backward:
+
+            @pl.when(now == last)
+            def _():
+                for copy in mean_moves:
+                    copy.wait_recv()
+                added = mean[...]
+                for d in range(1, count):
+                    added = added + mean_got[d]
+                mean_sum[...] = added * (1.0 / (count * width))
+
             for p, when in ((0, 2), (1, 15 if mode == "back" else 13)):
                 if p < len(halving.stages) - 1:
 
@@ -725,7 +731,7 @@
                 normal = middle[at(done), :].astype(F32) * size
                 summed = total[...]
                 own = residual[at(done), :].astype(F32) + size * (
-                    summed * gain[...] - normal * mean[at(done), 0:1]
+                    summed * gain[...] - normal * mean_column(done)
                 )
                 out_gain[...] += jnp.sum((summed * normal).reshape(rows // 8, 8, width), axis=0)
             else:
@@ -801,6 +807,8 @@
             halving.stage(p)
         halving.stage(len(halving.stages) - 1, out_spread)
         halving.settle()
+        for copy in mean_moves:
+            copy.wait_send()
 
     if mode == "last":
         mixer_sum = jnp.sum(out_gain[...], axis=0, keepdims=True)
@@ -880,6 +888,11 @@
             pltpu.SemaphoreType.DMA((3, 2, most)),
             pltpu.SemaphoreType.DMA((2, stages)),
         ]
+    if backward:
+        packed = (length // 128, 128)
+        scratch += [
+            pltpu.VMEM((count,) + packed, F32), pltpu.VMEM(packed, F32), pltpu.SemaphoreType.DMA((2, count)),
+        ]
     if summing:
         in_specs[4 if mode == "norm" else 1] = pl.BlockSpec(memory_space=pl.ANY)
         scratch += [
@@ -1061,7 +1074,7 @@
     )
     normed_mid, cot = after((normed_mid, cot))
     feed_low, feed_grads, feed_part, mid_mean = feed_both(normed_mid, cot, w_feed)
-    mid_mean = small_sum(mid_mean[:, 0].reshape(8, -1), "rep").reshape(-1, 1) / features
+    mid_mean = mid_mean[:, 0].reshape(-1, 128)
 
     half = feed_down.shape[1]
     down_grad = rows_dot(cot, feed_low).astype(BF)
@@ -1072,7 +1085,7 @@
     feed_all = spread(feed_all)
     middle_low, middle_grad, feed_gain_own, feed_down_grad = exchange(
         "back",
-        (feed_grads, w_feed, cot_own, middle, s2, jnp.broadcast_to(mid_mean, (length, 128)), feed_own, down_grad),
+        (feed_grads, w_feed, cot_own, middle, s2, mid_mean, feed_own, down_grad),
         own_width,
     )
 
@@ -1105,7 +1118,7 @@
     low_grad = jnp.concatenate([low_grad[:-edge], low_grad[-edge:] + share], axis=0).reshape(length, -1)
     share_dot = jnp.sum(share * ends.astype(F32), axis=2).reshape(-1)
     in_mean = low_dot[:, 0] + branch_dot[:, 0] + jnp.pad(share_dot, (length - share_dot.shape[0], 0))
-    in_mean = small_sum(in_mean.reshape(8, -1), "rep").reshape(-1, 1) / features
+    in_mean = in_mean.reshape(-1, 128)
 
     both_grads = jnp.concatenate([low_grad.astype(BF), branch_grad], axis=1)
     both_grads, in_mean, feed_all = after((both_grads, in_mean, feed_all))
@@ -1128,7 +1141,7 @@
     input_grad, summed, gains, output_all = exchange(
         "last",
         (
-            both_grads, w_recur, middle_grad, x_low, s1, jnp.broadcast_to(in_mean, (length, 128)), mixer_own,
+            both_grads, w_recur, middle_grad, x_low, s1, in_mean, mixer_own,
             small, feed_gain_own, output_all,
         ),
         own_width,

time: 681 us -> 676 us (level)
  starting transfers between devices: 22.2 us -> 14.9 us
    ppermute x6 -> x0, starting transfers between devices: 7.31 us -> none  [small_sum(): lax.ppermute(own, axis, [(i, (i + k) % count) for i in range(count)])]
    unnamed x132 -> x138, local copies, waits for them, and re-layouts: 26.4 us -> 27.5 us
  transfers between devices with their start and end apart: 17 -> 11, of which waited for: 3 -> 3; matrix products, arithmetic and copies ran while one was open for 11% -> 9% of each run, Pallas kernels for 70% -> 70%
where the time goes in v5:
time: 676 us; the launch traced here: 668 us
  Pallas kernels  504 us (75%)
  matrix products  63.3 us (9%)
  local copies, waits for them, and re-layouts  43.4 us (6%)
  other arithmetic  18.5 us (3%)
  between operations  15.6 us (2%)
  starting transfers between devices  14.9 us (2%)
  waiting for transfers between devices  7.51 us (1%)
    pallas_call x4, Pallas kernels, exchange(): pl.pallas_call(partial_call(exchange_kernel, count, chunks, mode), in_spe...  427 us
    dot_general x6, matrix products, rows_dot(): lax.dot_general(left, right, (((0,), (0,)), ((), ())), preferred_element_...  51.6 us
    pallas_call x1, Pallas kernels, feed_both(): pl.pallas_call(feed_kernel, grid=(length // rows,), in_specs=[block(featu...  37.1 us
    unnamed x138, local copies, waits for them, and re-layouts  27.5 us
    pallas_call x1, Pallas kernels, recur_backward(): pl.pallas_call(backward_kernel, grid=(length // rows,), in_specs=[block,...  15.2 us
    pallas_call x1, Pallas kernels, recur_forward(): pl.pallas_call(forward_kernel, grid=(length // rows,), in_specs=[block, p...  14 us
  transfers between devices with their start and end apart: 11, of which 3 were waited for; matrix products, arithmetic and copies ran while one was open for 9% of the time, Pallas kernels for 70%

profile of v5, /device:TPU:0, one launch (start us, length us, event | category | flops | bytes accessed | tf_op | source)
XLA Modules:
  0.0 667.5 jit_solution(2658235559240728129)
XLA Ops:
  13.4 2.9 copy_bitcast_fusion
  17.2 75.7 %shard_map.348 = (bf16[1024,2048]{1,0:T(8,128)(2,1)S(1)}, f32[1024,128]{1,0:T(8,128)S(1)}) custom-call(bf16[1024,512]{1,0:T(8,128)(2,1)S(1)} %get-tuple-element.87.refs_0_.refs_5_.refs_3_, f32[1,2048]{1,0:T(1,128)S(1)} %bitcast.117), custom_call_target="tpu_custom_call" | custom-call | flops 20971520 | bytes 335544320 | tf_op jit(solution)/shard_map/pallas_call | solution.py:908
  93.7 2.1 copy-done.22
  95.8 1.5 pad_maximum_fusion.1
  97.4 11.8 %fusion.conv_in.gate_branch = f32[1024,1536]{1,0:T(8,128)} fusion(bf16[1024,2048]{1,0:T(8,128)(2,1)} %copy-done.22, bf16[2048,2304]{1,0:T(8,128)(2,1)} %all-gather.4.cloned.1.call-done.refs_4_.weight.refs_1_), kind=kOutput, calls=%fused_computation.3 | convolution fusion | flops 6442450944 | bytes 16777216 | tf_op jit(solution)/shard_map/dot_general | solution.py:994
  109.9 3.4 collective-permute-start
  117.6 3.9 collective-permute-start.1
  124.4 14.0 %shard_map.349 = (f32[1024,768]{1,0:T(8,128)S(1)}, f32[1024,768]{1,0:T(8,128)}, f32[1024,768]{1,0:T(8,128)}, f32[1024,768]{1,0:T(8,128)}, f32[1024,768]{1,0:T(8,...) custom-call(f32[1024,1536]{1,0:T(8,128)} %fusion.conv_in.gate_branch, ...), custom_call_target="tpu_custom_call" | custom-call | flops 786432 | bytes 3145728 | tf_op jit(solution)/shard_map/pallas_call | solution.py:141
  138.4 1.7 copy-done.5
  140.7 4.7 collective-permute-start.2
  147.3 123.8 %shard_map.350 = (bf16[1024,2048]{1,0:T(8,128)(2,1)}, f32[1024,128]{1,0:T(8,128)S(1)}, f32[1024,512]{1,0:T(8,128)S(1)}, f32[1024,768]{1,0:T(8,128)}, bf16[1024,768]{1,0:T(8,128)(2,1)S(1)}) custom-call(f32[1024,768]{1,0:T(8,128)} %get-tuple-element.91.refs_0_, f32[1024,768]{1,0:T(8,128)} %get-tuple-element.92.refs_1_, f32[1024,768]{1,0:T(8,128)} %copy-done.5, ...), custom_call_target="tpu_custom_call" | custom-call | flops 20971520 | bytes 335544320 | tf_op jit(solution)/shard_map/pallas_call | solution.py:908
  271.2 1.3 copy-done
  275.0 37.1 %shard_map.351 = (bf16[1024,1536]{1,0:T(8,128)(2,1)S(1)}, bf16[1024,3072]{1,0:T(8,128)(2,1)}, bf16[1024,2048]{1,0:T(8,128)(2,1)}, f32[1024,128]{1,0:T(8,128)S(1)}) custom-call(bf16[1024,2048]{1,0:T(8,128)(2,1)} %get-tuple-element.100.normed_mid, bf16[1024,2048]{1,0:T(8,128)(2,1)} %all-gather.6.cloned.1.call-done.cot, ...), custom_call_target="tpu_custom_call" | custom-call | flops 25769803776 | bytes 37748736 | tf_op jit(solution)/shard_map/pallas_call | solution.py:962
  313.0 11.3 %convolution_convert_fusion.2.refs_7_ = bf16[2048,1536]{1,0:T(8,128)(2,1)} fusion(bf16[1024,2048]{1,0:T(8,128)(2,1)} %all-gather.6.cloned.1.call-done.cot, bf16[1024,1536]{1,0:T(8,128)(2,1)S(1)} %get-tuple-element.104), kind=kOutput, calls=%fused_computation.2 | convolution fusion | flops 6445596672 | bytes 13631488 | tf_op jit(solution)/shard_map/dot_general | solution.py:986
  324.3 18.3 %convolution_convert_fusion = bf16[2048,3072]{1,0:T(8,128)(2,1)} fusion(bf16[1024,2048]{1,0:T(8,128)(2,1)} %get-tuple-element.100.normed_mid, bf16[1024,3072]{1,0:T(8,128)(2,1)S(1)} %bitcast.120), kind=kOutput, calls=%fused_computation | convolution fusion | flops 12891193344 | bytes 23068672 | tf_op jit(solution)/shard_map/dot_general | solution.py:986
  344.0 133.3 %shard_map.352 = (bf16[1024,2048]{1,0:T(8,128)(2,1)}, f32[1024,512]{1,0:T(8,128)}, f32[8,512]{1,0:T(8,128)}, f32[256,1536]{1,0:T(8,128)}) custom-call(bf16[1024,3072]{1,0:T(8,128)(2,1)} %get-tuple-element.108.refs_0_, bf16[2048,4608]{1,0:T(8,128)(2,1)} %all-gather.8.cloned.1.call-done.weights.refs_1_, bf16[1024,512]{1,0:T(8,128)(2,1)} %get-tuple-element.99.refs_2_, ...), custom_call_target="tpu_custom_call" | custom-call | flops 20971520 | bytes 335544320 | tf_op jit(solution)/shard_map/pallas_call | solution.py:908
  477.4 11.0 %shard_map.353 = (f32[1024,768]{1,0:T(8,128)S(1)}, f32[1024,768]{1,0:T(8,128)}, bf16[1024,768]{1,0:T(8,128)(2,1)S(1)}, f32[8,768]{1,0:T(8,128)S(1)}, f32[8,768]{...) custom-call(bf16[1024,2048]{1,0:T(8,128)(2,1)} %get-tuple-element.112.middle_low, ...), custom_call_target="tpu_custom_call" | custom-call | flops 786432 | bytes 3145728 | tf_op jit(solution)/shard_map/pallas_call | solution.py:221
  488.4 1.7 copy-done.4
  491.4 5.0 convolution_convert_fusion.3.refs_9_
  496.5 15.2 %shard_map.354 = (bf16[1024,768]{1,0:T(8,128)(2,1)S(1)}, bf16[1024,768]{1,0:T(8,128)(2,1)}, f32[1024,768]{1,0:T(8,128)}, f32[1024,128]{1,0:T(8,128)S(1)}, f32[48,768]{1,0:T(8,128)S(1)}, /*index=5*/f32[64,768]{1,0:T(8,128)S(1)}) custom-call(f32[1024,768]{1,0:T(8,128)} %copy-done.4, f32[1024,768]{1,0:T(8,128)} %get-tuple-element.118.after, ...), custom_call_target="tpu_custom_call" | custom-call | flops 786432 | bytes 3145728 | tf_op jit(solution)/shard_map/pallas_call | solution.py:315
  513.2 2.0 fusion.6
  515.5 2.0 collective-permute-done.4
  519.6 2.0 pad_maximum_fusion.refs_0_
  521.6 11.8 %convolution_convert_fusion.1 = bf16[2048,1536]{1,0:T(8,128)(2,1)} fusion(bf16[1024,2048]{1,0:T(8,128)(2,1)} %copy-done.22, bf16[1024,1536]{1,0:T(8,128)(2,1)} %pad_maximum_fusion.refs_0_), kind=kOutput, calls=%fused_computation.1 | convolution fusion | flops 6445596672 | bytes 13631488 | tf_op jit(solution)/shard_map/dot_general | solution.py:986
  536.0 3.6 convolution_convert_fusion.5
  539.8 1.5 convolution_convert_fusion.4
  542.8 2.1 slice_convert_fusion.1
  544.9 2.9 reduce-scatter.6.cloned.1.call-done
  547.7 94.2 %shard_map.355 = (bf16[1024,512]{1,0:T(8,128)(2,1)S(1)}, f32[1440,256]{1,0:T(8,128)S(1)}, f32[8,2048]{1,0:T(8,128)S(1)}, f32[256,768]{1,0:T(8,128)S(1)}) custom-call(bf16[1024,1536]{1,0:T(8,128)(2,1)} %pad_maximum_fusion.refs_0_, bf16[2048,2304]{1,0:T(8,128)(2,1)} %all-gather.4.cloned.1.call-done.refs_4_.weight.refs_1_, ...), custom_call_target="tpu_custom_call" | custom-call | flops 20971520 | bytes 335544320 | tf_op jit(solution)/shard_map/pallas_call | solution.py:908
  644.9 2.4 copy.108
  649.3 2.5 fusion.52
  652.4 1.7 fusion.9
  (231 shorter events, 43.4 us)
Async XLA Ops:
  7.2 6.2 copy-start.32
  7.2 6.2 copy-start.31
  7.2 90.2 %all-gather.4.cloned.1.call-start = ((), (), s32[]{:S(2)}) async-start(), calls=%async_computation.3 | async-start | bytes 10616832 | tf_op jit(solution)/shard_map/all_gather | solution.py:1015
  16.4 79.5 %copy-start.33 = (bf16[256,1536]{1,0:T(8,128)(2,1)S(1)}, bf16[256,1536]{1,0:T(8,128)(2,1)}, u32[]{:S(2)}) copy-start(bf16[256,1536]{1,0:T(8,128)(2,1)} %param.32) | copy-start | bytes 2359300
  16.4 79.5 %copy-start.34 = (bf16[256,1536]{1,0:T(8,128)(2,1)S(1)}, bf16[256,1536]{1,0:T(8,128)(2,1)}, u32[]{:S(2)}) copy-start(bf16[256,1536]{1,0:T(8,128)(2,1)} %param.31) | copy-start | bytes 2359300
  16.4 79.5 %copy-start.35 = (bf16[256,1536]{1,0:T(8,128)(2,1)S(1)}, bf16[256,1536]{1,0:T(8,128)(2,1)}, u32[]{:S(2)}) copy-start(bf16[256,1536]{1,0:T(8,128)(2,1)} %param.30) | copy-start | bytes 2359300
  16.4 258.6 %all-gather.6.cloned.1.call-start = ((), (), s32[]{:S(2)}) async-start(), calls=%async_computation.4 | async-start | bytes 5242880 | tf_op jit(solution)/shard_map/all_gather | solution.py:1038
  17.2 257.9 %all-gather.8.cloned.1.call-start = ((), (), s32[]{:S(2)}) async-start(), calls=%async_computation.5 | async-start | bytes 21233664 | tf_op jit(solution)/shard_map/all_gather | solution.py:1015
  109.2 5.3 copy-start.50
  109.2 5.4 copy-start.40
  109.2 5.4 copy-start.41
  109.2 412.4 %reduce-scatter.4.cloned.1.call-start = ((), (), s32[]{:S(2)}) async-start(), calls=%async_computation.6 | async-start | bytes 14155776 | tf_op jit(solution)/shard_map/reduce_scatter | solution.py:1018
  109.9 5.5 collective-permute-start
  114.6 8.8 %copy-start.15 = (f32[8,768]{1,0:T(8,128)}, f32[8,768]{1,0:T(8,128)S(1)}, u32[]{:S(2)}) copy-start(f32[8,768]{1,0:T(8,128)S(1)} %select_maximum_fusion.params) | copy-start | bytes 73732
  114.6 8.1 %copy-start.51 = (bf16[1,3,704]{2,1,0:T(4,128)(2,1)S(1)}, bf16[1,3,704]{2,1,0:T(4,128)(2,1)}, u32[]{:S(2)}) copy-start(bf16[1,3,704]{2,1,0:T(4,128)(2,1)} %param.26) | copy-start | bytes 12676
  117.0 5.8 copy-start.37
  117.6 5.1 collective-permute-start.1
  124.4 15.7 %copy-start.46 = (f32[1,704]{1,0:T(1,128)S(1)}, f32[1,704]{1,0:T(1,128)}, u32[]{:S(2)}) copy-start(f32[1,704]{1,0:T(1,128)} %param.25) | copy-start | bytes 8452
  124.4 23.0 %copy-start.20 = (f32[2048]{0:T(1024)S(1)}, f32[2048]{0:T(1024)}, u32[]{:S(2)}) copy-start(f32[2048]{0:T(1024)} %param.41) | copy-start | bytes 24580
  140.7 6.0 collective-permute-start.2
  312.2 12.2 %slice-start = ((s8[6291456]{0:T(1024)(128)(4,1)}), s8[2097152]{0:T(1024)(128)(4,1)S(1)}, s32[]{:S(2)}) async-start(s8[6291456]{0:T(1024)(128)(4,1)} %bitcast.119), calls=%async_computation.9 | async-start | bytes 4194304
  313.0 11.4 %slice-start.1 = ((s8[6291456]{0:T(1024)(128)(4,1)}), s8[4194304]{0:T(1024)(128)(4,1)S(1)}, s32[]{:S(2)}) async-start(s8[6291456]{0:T(1024)(128)(4,1)} %bitcast.119), calls=%async_computation.10 | async-start | bytes 8388608
  342.7 205.0 %reduce-scatter.6.cloned.1.call-start = ((), (), s32[]{:S(2)}) async-start(), calls=%async_computation.7 | async-start | bytes 5242880 | tf_op jit(solution)/shard_map/reduce_scatter | solution.py:1084
  343.3 309.1 %reduce-scatter.8.cloned.1.call-start = ((), (), s32[]{:S(2)}) async-start(), calls=%async_computation.8 | async-start | bytes 7077888 | tf_op jit(solution)/shard_map/reduce_scatter | solution.py:1018
  477.4 14.0 %copy-start.26 = (bf16[1024,768]{1,0:T(8,128)(2,1)S(1)}, bf16[1024,768]{1,0:T(8,128)(2,1)}, u32[]{:S(2)}) copy-start(bf16[1024,768]{1,0:T(8,128)(2,1)} %copy-done.25) | copy-start | bytes 4718596
  477.4 14.0 %copy-start.27 = (bf16[1024,2048]{1,0:T(8,128)(2,1)S(1)}, bf16[1024,2048]{1,0:T(8,128)(2,1)}, u32[]{:S(2)}) copy-start(bf16[1024,2048]{1,0:T(8,128)(2,1)} %get-tuple-element.112.middle_low) | copy-start | bytes 12582916
  490.1 6.4 collective-permute-start.3
  491.4 5.1 copy-start.3
  496.5 15.3 %copy-start.38 = (bf16[3,8,768]{2,1,0:T(8,128)(2,1)S(1)}, bf16[3,8,768]{2,1,0:T(8,128)(2,1)}, u32[]{:S(2)}) copy-start(bf16[3,8,768]{2,1,0:T(8,128)(2,1)} %copy-done.37) | copy-start | bytes 110596
  496.5 15.3 %copy-start.43 = (bf16[3,1,768]{2,1,0:T(2,128)(2,1)S(1)}, bf16[3,1,768]{2,1,0:T(2,128)(2,1)}, u32[]{:S(2)}) copy-start(bf16[3,1,768]{2,1,0:T(2,128)(2,1)} %copy-done.42) | copy-start | bytes 13828
  511.9 5.6 collective-permute-start.4
  644.9 7.5 %copy-start.1 = (f32[1024,512]{1,0:T(8,128)S(1)}, f32[1024,512]{1,0:T(8,128)}, u32[]{:S(2)}) copy-start(f32[1024,512]{1,0:T(8,128)} %copy-done) | copy-start | bytes 6291460
  (39 other events, 98.3 us)
Sparse Core Ops, SparseCore 0:
  16.5 61.5 all-gather.3
  80.2 81.9 all-gather.5
  164.1 101.9 all-gather.7
  342.8 126.5 reduce-scatter.3
  471.5 76.1 reduce-scatter.5
  551.4 77.2 reduce-scatter.7

commit v6 on v5

--- a/solution.py
+++ b/solution.py
@@ -132,7 +132,7 @@
         out_total[2:8, :] = jnp.zeros((6, carry_a.shape[1]), F32)
 
 
-def recur_forward(conv_in, same, prefix, params, decay_w, input_w, rows=256):
+def recur_forward(conv_in, same, prefix, params, decay_w, input_w, rows=512):
     length, width = conv_in.shape[0], params.shape[1]
     block = pl.BlockSpec((rows, width), lambda i: (i, 0))
     fixed = lambda shape: pl.BlockSpec(shape, lambda i: (0, 0))
@@ -209,7 +209,7 @@
         out_total[2:8, :] = jnp.zeros((6, carry_a.shape[1]), F32)
 
 
-def recur_adjoint(middle_low, w_recur, gate_branch, hidden, retain, rows=256):
+def recur_adjoint(middle_low, w_recur, gate_branch, hidden, retain, rows=512):
     length, width = hidden.shape
     features = middle_low.shape[1]
     last = length // rows - 1
@@ -304,7 +304,7 @@
 
 def recur_backward(
     local, after, enter, hidden, carry, conv_out, decay_sig, gate_sig, retain, same, params, conv_in, decay_w, input_w,
-    rows=256,
+    rows=512,
 ):
     length, width = local.shape
     last = length // rows - 1

time: 676 us -> 674 us (level)
  no operation moved by 1% of the time
where the time goes in v6:
time: 674 us; the launch traced here: 668 us
  Pallas kernels  506 us (75%)
  matrix products  63.5 us (9%)
  local copies, waits for them, and re-layouts  43.3 us (6%)
  other arithmetic  18.5 us (3%)
  between operations  15.6 us (2%)
  starting transfers between devices  14.9 us (2%)
    pallas_call x4, Pallas kernels, exchange(): pl.pallas_call(partial_call(exchange_kernel, count, chunks, mode), in_spe...  425 us
    dot_general x6, matrix products, rows_dot(): lax.dot_general(left, right, (((0,), (0,)), ((), ())), preferred_element_...  51.7 us
    pallas_call x1, Pallas kernels, feed_both(): pl.pallas_call(feed_kernel, grid=(length // rows,), in_specs=[block(featu...  37.1 us
    unnamed x138, local copies, waits for them, and re-layouts  27.5 us
    pallas_call x1, Pallas kernels, recur_backward(): pl.pallas_call(backward_kernel, grid=(length // rows,), in_specs=[block,...  16.2 us
    pallas_call x1, Pallas kernels, recur_forward(): pl.pallas_call(forward_kernel, grid=(length // rows,), in_specs=[block, p...  15.7 us
  transfers between devices with their start and end apart: 11, of which 3 were waited for; matrix products, arithmetic and copies ran while one was open for 9% of the time, Pallas kernels for 70%

profile of v6, /device:TPU:0, one launch (start us, length us, event | category | flops | bytes accessed | tf_op | source)
XLA Modules:
  0.0 667.6 jit_solution(12814784376637161396)
XLA Ops:
  13.4 2.9 copy_bitcast_fusion
  17.2 75.7 %shard_map.348 = (bf16[1024,2048]{1,0:T(8,128)(2,1)S(1)}, f32[1024,128]{1,0:T(8,128)S(1)}) custom-call(bf16[1024,512]{1,0:T(8,128)(2,1)S(1)} %get-tuple-element.87.refs_0_.refs_5_.refs_3_, f32[1,2048]{1,0:T(1,128)S(1)} %bitcast.117), custom_call_target="tpu_custom_call" | custom-call | flops 20971520 | bytes 335544320 | tf_op jit(solution)/shard_map/pallas_call | solution.py:908
  93.7 2.1 copy-done.22
  95.8 1.5 pad_maximum_fusion.1
  97.4 11.8 %fusion.conv_in.gate_branch = f32[1024,1536]{1,0:T(8,128)} fusion(bf16[1024,2048]{1,0:T(8,128)(2,1)} %copy-done.22, bf16[2048,2304]{1,0:T(8,128)(2,1)} %all-gather.4.cloned.1.call-done.refs_4_.weight.refs_1_), kind=kOutput, calls=%fused_computation.3 | convolution fusion | flops 6442450944 | bytes 16777216 | tf_op jit(solution)/shard_map/dot_general | solution.py:994
  109.9 3.4 collective-permute-start
  117.6 4.2 collective-permute-start.1
  124.7 15.7 %shard_map.349 = (f32[1024,768]{1,0:T(8,128)S(1)}, f32[1024,768]{1,0:T(8,128)}, f32[1024,768]{1,0:T(8,128)}, f32[1024,768]{1,0:T(8,128)}, f32[1024,768]{1,0:T(8,...) custom-call(f32[1024,1536]{1,0:T(8,128)} %fusion.conv_in.gate_branch, ...), custom_call_target="tpu_custom_call" | custom-call | flops 786432 | bytes 3145728 | tf_op jit(solution)/shard_map/pallas_call | solution.py:141
  140.4 1.7 copy-done.5
  142.8 4.4 collective-permute-start.2
  149.1 122.1 %shard_map.350 = (bf16[1024,2048]{1,0:T(8,128)(2,1)}, f32[1024,128]{1,0:T(8,128)S(1)}, f32[1024,512]{1,0:T(8,128)S(1)}, f32[1024,768]{1,0:T(8,128)}, bf16[1024,768]{1,0:T(8,128)(2,1)S(1)}) custom-call(f32[1024,768]{1,0:T(8,128)} %get-tuple-element.91.refs_0_, f32[1024,768]{1,0:T(8,128)} %get-tuple-element.92.refs_1_, f32[1024,768]{1,0:T(8,128)} %copy-done.5, ...), custom_call_target="tpu_custom_call" | custom-call | flops 20971520 | bytes 335544320 | tf_op jit(solution)/shard_map/pallas_call | solution.py:908
  271.2 1.3 copy-done
  275.0 37.1 %shard_map.351 = (bf16[1024,1536]{1,0:T(8,128)(2,1)S(1)}, bf16[1024,3072]{1,0:T(8,128)(2,1)}, bf16[1024,2048]{1,0:T(8,128)(2,1)}, f32[1024,128]{1,0:T(8,128)S(1)}) custom-call(bf16[1024,2048]{1,0:T(8,128)(2,1)} %get-tuple-element.100.normed_mid, bf16[1024,2048]{1,0:T(8,128)(2,1)} %all-gather.6.cloned.1.call-done.cot, ...), custom_call_target="tpu_custom_call" | custom-call | flops 25769803776 | bytes 37748736 | tf_op jit(solution)/shard_map/pallas_call | solution.py:962
  313.0 11.3 %convolution_convert_fusion.2.refs_7_ = bf16[2048,1536]{1,0:T(8,128)(2,1)} fusion(bf16[1024,2048]{1,0:T(8,128)(2,1)} %all-gather.6.cloned.1.call-done.cot, bf16[1024,1536]{1,0:T(8,128)(2,1)S(1)} %get-tuple-element.104), kind=kOutput, calls=%fused_computation.2 | convolution fusion | flops 6445596672 | bytes 13631488 | tf_op jit(solution)/shard_map/dot_general | solution.py:986
  324.4 18.3 %convolution_convert_fusion = bf16[2048,3072]{1,0:T(8,128)(2,1)} fusion(bf16[1024,2048]{1,0:T(8,128)(2,1)} %get-tuple-element.100.normed_mid, bf16[1024,3072]{1,0:T(8,128)(2,1)S(1)} %bitcast.120), kind=kOutput, calls=%fused_computation | convolution fusion | flops 12891193344 | bytes 23068672 | tf_op jit(solution)/shard_map/dot_general | solution.py:986
  344.0 133.4 %shard_map.352 = (bf16[1024,2048]{1,0:T(8,128)(2,1)}, f32[1024,512]{1,0:T(8,128)}, f32[8,512]{1,0:T(8,128)}, f32[256,1536]{1,0:T(8,128)}) custom-call(bf16[1024,3072]{1,0:T(8,128)(2,1)} %get-tuple-element.108.refs_0_, bf16[2048,4608]{1,0:T(8,128)(2,1)} %all-gather.8.cloned.1.call-done.weights.refs_1_, bf16[1024,512]{1,0:T(8,128)(2,1)} %get-tuple-element.99.refs_2_, ...), custom_call_target="tpu_custom_call" | custom-call | flops 20971520 | bytes 335544320 | tf_op jit(solution)/shard_map/pallas_call | solution.py:908
  477.5 11.4 %shard_map.353 = (f32[1024,768]{1,0:T(8,128)S(1)}, f32[1024,768]{1,0:T(8,128)}, bf16[1024,768]{1,0:T(8,128)(2,1)S(1)}, f32[8,768]{1,0:T(8,128)S(1)}, f32[8,768]{...) custom-call(bf16[1024,2048]{1,0:T(8,128)(2,1)} %get-tuple-element.112.middle_low, ...), custom_call_target="tpu_custom_call" | custom-call | flops 786432 | bytes 3145728 | tf_op jit(solution)/shard_map/pallas_call | solution.py:221
  488.9 1.7 copy-done.4
  491.9 5.3 convolution_convert_fusion.3.refs_9_
  497.3 16.2 %shard_map.354 = (bf16[1024,768]{1,0:T(8,128)(2,1)S(1)}, bf16[1024,768]{1,0:T(8,128)(2,1)}, f32[1024,768]{1,0:T(8,128)}, f32[1024,128]{1,0:T(8,128)S(1)}, f32[48,768]{1,0:T(8,128)S(1)}, /*index=5*/f32[64,768]{1,0:T(8,128)S(1)}) custom-call(f32[1024,768]{1,0:T(8,128)} %copy-done.4, f32[1024,768]{1,0:T(8,128)} %get-tuple-element.118.after, ...), custom_call_target="tpu_custom_call" | custom-call | flops 786432 | bytes 3145728 | tf_op jit(solution)/shard_map/pallas_call | solution.py:315
  514.9 2.0 fusion.6
  517.2 2.0 collective-permute-done.4
  521.4 2.0 pad_maximum_fusion.refs_0_
  523.3 11.7 %convolution_convert_fusion.1 = bf16[2048,1536]{1,0:T(8,128)(2,1)} fusion(bf16[1024,2048]{1,0:T(8,128)(2,1)} %copy-done.22, bf16[1024,1536]{1,0:T(8,128)(2,1)} %pad_maximum_fusion.refs_0_), kind=kOutput, calls=%fused_computation.1 | convolution fusion | flops 6445596672 | bytes 13631488 | tf_op jit(solution)/shard_map/dot_general | solution.py:986
  537.7 3.5 convolution_convert_fusion.5
  541.5 1.5 convolution_convert_fusion.4
  544.4 2.1 slice_convert_fusion.1
  546.4 1.3 reduce-scatter.6.cloned.1.call-done
  547.8 94.3 %shard_map.355 = (bf16[1024,512]{1,0:T(8,128)(2,1)S(1)}, f32[1440,256]{1,0:T(8,128)S(1)}, f32[8,2048]{1,0:T(8,128)S(1)}, f32[256,768]{1,0:T(8,128)S(1)}) custom-call(bf16[1024,1536]{1,0:T(8,128)(2,1)} %pad_maximum_fusion.refs_0_, bf16[2048,2304]{1,0:T(8,128)(2,1)} %all-gather.4.cloned.1.call-done.refs_4_.weight.refs_1_, ...), custom_call_target="tpu_custom_call" | custom-call | flops 20971520 | bytes 335544320 | tf_op jit(solution)/shard_map/pallas_call | solution.py:908
  645.0 2.4 copy.108
  649.4 2.5 fusion.52
  652.5 1.7 fusion.9
  (231 shorter events, 43.3 us)
Async XLA Ops:
  7.2 6.2 copy-start.32
  7.2 6.2 copy-start.31
  7.2 90.2 %all-gather.4.cloned.1.call-start = ((), (), s32[]{:S(2)}) async-start(), calls=%async_computation.3 | async-start | bytes 10616832 | tf_op jit(solution)/shard_map/all_gather | solution.py:1015
  16.4 79.5 %copy-start.33 = (bf16[256,1536]{1,0:T(8,128)(2,1)S(1)}, bf16[256,1536]{1,0:T(8,128)(2,1)}, u32[]{:S(2)}) copy-start(bf16[256,1536]{1,0:T(8,128)(2,1)} %param.32) | copy-start | bytes 2359300
  16.4 79.5 %copy-start.34 = (bf16[256,1536]{1,0:T(8,128)(2,1)S(1)}, bf16[256,1536]{1,0:T(8,128)(2,1)}, u32[]{:S(2)}) copy-start(bf16[256,1536]{1,0:T(8,128)(2,1)} %param.31) | copy-start | bytes 2359300
  16.4 79.5 %copy-start.35 = (bf16[256,1536]{1,0:T(8,128)(2,1)S(1)}, bf16[256,1536]{1,0:T(8,128)(2,1)}, u32[]{:S(2)}) copy-start(bf16[256,1536]{1,0:T(8,128)(2,1)} %param.30) | copy-start | bytes 2359300
  16.4 258.6 %all-gather.6.cloned.1.call-start = ((), (), s32[]{:S(2)}) async-start(), calls=%async_computation.4 | async-start | bytes 5242880 | tf_op jit(solution)/shard_map/all_gather | solution.py:1038
  17.2 257.9 %all-gather.8.cloned.1.call-start = ((), (), s32[]{:S(2)}) async-start(), calls=%async_computation.5 | async-start | bytes 21233664 | tf_op jit(solution)/shard_map/all_gather | solution.py:1015
  109.2 5.4 copy-start.40
  109.2 5.4 copy-start.41
  109.2 414.1 %reduce-scatter.4.cloned.1.call-start = ((), (), s32[]{:S(2)}) async-start(), calls=%async_computation.6 | async-start | bytes 14155776 | tf_op jit(solution)/shard_map/reduce_scatter | solution.py:1018
  109.9 5.5 collective-permute-start
  114.6 9.1 %copy-start.15 = (f32[8,768]{1,0:T(8,128)}, f32[8,768]{1,0:T(8,128)S(1)}, u32[]{:S(2)}) copy-start(f32[8,768]{1,0:T(8,128)S(1)} %select_maximum_fusion.params) | copy-start | bytes 73732
  114.6 8.4 %copy-start.51 = (bf16[1,3,704]{2,1,0:T(4,128)(2,1)S(1)}, bf16[1,3,704]{2,1,0:T(4,128)(2,1)}, u32[]{:S(2)}) copy-start(bf16[1,3,704]{2,1,0:T(4,128)(2,1)} %param.26) | copy-start | bytes 12676
  117.0 6.1 copy-start.37
  117.6 5.4 collective-permute-start.1
  124.7 17.5 %copy-start.46 = (f32[1,704]{1,0:T(1,128)S(1)}, f32[1,704]{1,0:T(1,128)}, u32[]{:S(2)}) copy-start(f32[1,704]{1,0:T(1,128)} %param.25) | copy-start | bytes 8452
  124.7 24.4 %copy-start.20 = (f32[2048]{0:T(1024)S(1)}, f32[2048]{0:T(1024)}, u32[]{:S(2)}) copy-start(f32[2048]{0:T(1024)} %param.41) | copy-start | bytes 24580
  142.8 5.7 collective-permute-start.2
  312.2 12.2 %slice-start = ((s8[6291456]{0:T(1024)(128)(4,1)}), s8[2097152]{0:T(1024)(128)(4,1)S(1)}, s32[]{:S(2)}) async-start(s8[6291456]{0:T(1024)(128)(4,1)} %bitcast.119), calls=%async_computation.9 | async-start | bytes 4194304
  313.0 11.4 %slice-start.1 = ((s8[6291456]{0:T(1024)(128)(4,1)}), s8[4194304]{0:T(1024)(128)(4,1)S(1)}, s32[]{:S(2)}) async-start(s8[6291456]{0:T(1024)(128)(4,1)} %bitcast.119), calls=%async_computation.10 | async-start | bytes 8388608
  342.7 205.0 %reduce-scatter.6.cloned.1.call-start = ((), (), s32[]{:S(2)}) async-start(), calls=%async_computation.7 | async-start | bytes 5242880 | tf_op jit(solution)/shard_map/reduce_scatter | solution.py:1084
  343.3 309.2 %reduce-scatter.8.cloned.1.call-start = ((), (), s32[]{:S(2)}) async-start(), calls=%async_computation.8 | async-start | bytes 7077888 | tf_op jit(solution)/shard_map/reduce_scatter | solution.py:1018
  477.4 14.4 %copy-start.26 = (bf16[1024,768]{1,0:T(8,128)(2,1)S(1)}, bf16[1024,768]{1,0:T(8,128)(2,1)}, u32[]{:S(2)}) copy-start(bf16[1024,768]{1,0:T(8,128)(2,1)} %copy-done.25) | copy-start | bytes 4718596
  477.4 14.4 %copy-start.27 = (bf16[1024,2048]{1,0:T(8,128)(2,1)S(1)}, bf16[1024,2048]{1,0:T(8,128)(2,1)}, u32[]{:S(2)}) copy-start(bf16[1024,2048]{1,0:T(8,128)(2,1)} %get-tuple-element.112.middle_low) | copy-start | bytes 12582916
  490.6 6.6 collective-permute-start.3
  491.9 5.3 copy-start.3
  491.9 5.3 copy-start.14
  497.2 16.3 %copy-start.38 = (bf16[3,8,768]{2,1,0:T(8,128)(2,1)S(1)}, bf16[3,8,768]{2,1,0:T(8,128)(2,1)}, u32[]{:S(2)}) copy-start(bf16[3,8,768]{2,1,0:T(8,128)(2,1)} %copy-done.37) | copy-start | bytes 110596
  497.2 16.3 %copy-start.43 = (bf16[3,1,768]{2,1,0:T(2,128)(2,1)S(1)}, bf16[3,1,768]{2,1,0:T(2,128)(2,1)}, u32[]{:S(2)}) copy-start(bf16[3,1,768]{2,1,0:T(2,128)(2,1)} %copy-done.42) | copy-start | bytes 13828
  513.6 5.6 collective-permute-start.4
  645.0 7.5 %copy-start.1 = (f32[1024,512]{1,0:T(8,128)S(1)}, f32[1024,512]{1,0:T(8,128)}, u32[]{:S(2)}) copy-start(f32[1024,512]{1,0:T(8,128)} %copy-done) | copy-start | bytes 6291460
  (39 other events, 95.5 us)
Sparse Core Ops, SparseCore 0:
  16.5 61.5 all-gather.3
  80.2 81.5 all-gather.5
  163.7 100.6 all-gather.7
  342.8 126.5 reduce-scatter.3
  471.6 76.1 reduce-scatter.5
  551.4 77.2 reduce-scatter.7
